TPU v7x, 128 devices: a whole 4x4x4 slice. The times are simulated.
128 devices in a mesh: row: 16 (over y, z_hi, core), col: 8 (over x, z_lo).
Axes of the slice: x: 4, y: 4, z: 4 (z_hi: 2, z_lo: 2; z = z_hi * 2 + z_lo), core: 2. Of those that a mesh axis runs over, the one named last changes fastest.
Arguments:
- aligned_family_embedding: bfloat16 [512, 768, 256], P('row', 'col'), may hold values from -24 to 24
- aligned_slot_available: int32 [512, 768], P('row', 'col'), may hold values from 0 to 1, as said below
- chain_site_available: int32 [768], replicated, may hold values 0 or 1
- duo_embedding: float32 [768, 768, 128], P('row', 'col'), may hold values from -1.2 to 1.2
- averaging_layernorm_stretch: float32 [256], replicated, may hold values from 0.1 to 1.9
- lineup_layernorm_stretch: float32 [256], replicated, may hold values from 0.1 to 1.9
- duo_layernorm_stretch: float32 [128], replicated, may hold values from 0.1 to 1.9
- lefthand_linear_kernel: bfloat16 [256, 32], replicated, may hold values from -0.375 to 0.375
- righthand_linear_kernel: bfloat16 [256, 32], replicated, may hold values from -0.375 to 0.375
- kronecker_linear_kernel: bfloat16 [1024, 128], replicated, may hold values from -0.1875 to 0.1875
- duo_logit_kernel: bfloat16 [128, 8], replicated, may hold values from -0.75 to 0.75
- asker_lookup_sigmoid_kernel: bfloat16 [256, 1024], replicated, may hold values from -8 to 8
- closing_linear_kernel: bfloat16 [256, 256], replicated, may hold values from -0.375 to 0.375
Outputs:
- refreshed_family_embedding: bfloat16 [512, 768, 256], P('row', 'col')
- duo_after_averaging: float32 [768, 768, 128], P('row', 'col')
Inputs may be any that keep to these rules, and one draw needn't show every extreme that they name: `aligned_slot_available`: 0 or 1; sequence 0 is present at every residue.
All inputs are finite; a program needn't handle non-finite values.
Results may differ from a plain program's by a relative error of at most 0.0052.
Values may be sent and summed in bfloat16 or wider, within the bound.
A program may use at most 192 MiB of HBM per device.

v0:
```python
import jax
import jax.numpy as jnp
from jax import lax
from jax.sharding import PartitionSpec as P

EPSILON = 1e-05
CONTRACT_FIRST = (((0,), (0,)), ((), ()))


def laid_out(pieces, dim):
    lengths = list(pieces.shape[1:])
    lengths[dim] *= pieces.shape[0]
    return jnp.moveaxis(pieces, 0, dim).reshape(lengths)


def one_gather(arrays, axis, dims):
    line = jnp.concatenate([a.reshape(-1) for a in arrays])
    lines, at, outs = (lax.all_gather(line, axis), 0, [])
    for a, dim in zip(arrays, dims):
        pieces = lines[:, at : at + a.size].reshape(-1, *a.shape)
        outs.append(laid_out(pieces, dim))
        at += a.size
    return tuple(outs)


def in_one_piece(arrays, axis, dim, along):
    ends, at = ([], 0)
    for a in arrays[:-1]:
        at += a.shape[along]
        ends.append(at)
    both = jnp.concatenate(arrays, axis=along)
    return tuple(jnp.split(lax.all_gather(both, axis, axis=dim, tiled=True), ends, axis=along))


def sent_to_all(x, axis):
    copies = jnp.broadcast_to(x, (lax.axis_size(axis), *x.shape))
    return lax.all_to_all(copies, axis, split_axis=0, concat_axis=0, tiled=True)


def gather_directly(x, axis, dim):
    return laid_out(sent_to_all(x, axis), dim)


def sent_together(arrays, axis, split_dim, concat_dim, along):
    columns = [a.reshape(*a.shape[:along], -1) for a in arrays]
    both = jnp.concatenate(columns, axis=along)
    whole, at, outs = (
        lax.all_to_all(both, axis, split_axis=split_dim, concat_axis=concat_dim, tiled=True),
        0,
        [],
    )
    for a, column in zip(arrays, columns):
        section = whole[..., at : at + column.shape[along]]
        outs.append(section.reshape(*section.shape[:along], *a.shape[along:]))
        at += column.shape[along]
    return tuple(outs)


def standardize_features(values):
    average = jnp.mean(values, axis=-1, keepdims=True)
    centred = values - average
    variance = jnp.mean(centred * centred, axis=-1, keepdims=True)
    return centred * lax.rsqrt(variance + EPSILON)


def project_rows(inputs, weight, availability_real):
    projected = jnp.einsum("src,ca->sra", inputs, weight, preferred_element_type=jnp.float32)
    return (projected * availability_real[:, :, None]).astype(jnp.bfloat16)


def attend(queries, gate_pre, keys_all, values_all, key_mask, bias_rows, head_count):
    homolog_number, query_count, inner_width = queries.shape
    key_count = keys_all.shape[1]
    head_dim = inner_width // head_count
    block_rows = 1
    while (
        block_rows < homolog_number
        and block_rows * query_count < 512
        and (homolog_number % (2 * block_rows) == 0)
    ):
        block_rows = 2 * block_rows
    groups = homolog_number // block_rows
    score_scale = head_dim ** (-0.5)
    bias_float = bias_rows.astype(jnp.float32)

    def one_block(group_members):
        block_query, block_gate, block_key, block_value, block_mask = group_members
        query_heads = block_query.reshape(block_rows, query_count, head_count, head_dim)
        key_heads = block_key.reshape(block_rows, key_count, head_count, head_dim)
        value_heads = block_value.reshape(block_rows, key_count, head_count, head_dim)
        scores = jnp.einsum(
            "bqhd,bkhd->bhqk", query_heads, key_heads, preferred_element_type=jnp.float32
        )
        scores = (
            scores * score_scale
            + bias_float[None]
            + 1000000000.0 * (block_mask.astype(jnp.float32)[:, None, None, :] - 1.0)
        )
        highest = jnp.max(scores, axis=-1, keepdims=True)
        exponent = jnp.exp(scores - highest)
        weights = (exponent / jnp.sum(exponent, axis=-1, keepdims=True)).astype(jnp.bfloat16)
        mixed_rows = jnp.einsum(
            "bhqk,bkhd->bqhd", weights, value_heads, preferred_element_type=jnp.float32
        )
        mixed_rows = mixed_rows.reshape(block_rows, query_count, inner_width)
        return (mixed_rows * jax.nn.sigmoid(block_gate.astype(jnp.float32))).astype(jnp.bfloat16)

    def grouped(array):
        return array.reshape((groups, block_rows) + array.shape[1:])

    gated_row_output = lax.map(
        one_block,
        (
            grouped(queries),
            grouped(gate_pre),
            grouped(keys_all),
            grouped(values_all),
            grouped(key_mask),
        ),
    )
    return gated_row_output.reshape(homolog_number, query_count, inner_width)


def shards(
    aligned_family_embedding,
    aligned_slot_available,
    chain_site_available,
    duo_embedding,
    averaging_layernorm_stretch,
    lineup_layernorm_stretch,
    duo_layernorm_stretch,
    lefthand_linear_kernel,
    righthand_linear_kernel,
    kronecker_linear_kernel,
    duo_logit_kernel,
    asker_lookup_sigmoid_kernel,
    closing_linear_kernel,
):
    homolog_number, amino_position_number, discarded_carry = aligned_family_embedding.shape
    res_rows = duo_embedding.shape[0]
    opm_width = lefthand_linear_kernel.shape[1]
    head_count = duo_logit_kernel.shape[1]
    inner_width = closing_linear_kernel.shape[0]
    row_index = lax.axis_index("row")
    col_index = lax.axis_index("col")
    standardized_features = standardize_features(aligned_family_embedding.astype(jnp.float32))
    availability_real = aligned_slot_available.astype(jnp.float32)
    shrunk_availability = aligned_slot_available.astype(jnp.bfloat16)
    opm_input = (standardized_features * averaging_layernorm_stretch).astype(jnp.bfloat16)
    left_flat = project_rows(opm_input, lefthand_linear_kernel, availability_real).reshape(
        homolog_number, amino_position_number * opm_width
    )
    right_flat = project_rows(opm_input, righthand_linear_kernel, availability_real).reshape(
        homolog_number, amino_position_number * opm_width
    )
    left_wide, mask_wide = one_gather((left_flat, shrunk_availability), "col", (1, 1))
    left_block, left_mask = (
        lax.all_to_all(left_wide, "row", split_axis=1, concat_axis=0, tiled=True),
        lax.all_to_all(mask_wide, "row", split_axis=1, concat_axis=0, tiled=True),
    )
    right_all, mask_all = in_one_piece((right_flat, shrunk_availability), "row", 0, 1)
    outer_sum = lax.dot_general(
        left_block, right_all, CONTRACT_FIRST, preferred_element_type=jnp.float32
    )
    counts = lax.dot_general(
        left_mask, mask_all, CONTRACT_FIRST, preferred_element_type=jnp.float32
    )
    outer_narrow = outer_sum.astype(jnp.bfloat16).reshape(
        res_rows, opm_width, amino_position_number, opm_width
    )
    mixing = kronecker_linear_kernel.reshape(opm_width, opm_width, kronecker_linear_kernel.shape[1])
    update = jnp.einsum("iajb,abk->ijk", outer_narrow, mixing, preferred_element_type=jnp.float32)
    residue_float = chain_site_available.astype(jnp.float32)
    residue_rows = lax.dynamic_slice_in_dim(residue_float, row_index * res_rows, res_rows)
    residue_cols = lax.dynamic_slice_in_dim(
        residue_float, col_index * amino_position_number, amino_position_number
    )
    update = (
        update
        / (counts + 0.001)[:, :, None]
        * (residue_rows[:, None] * residue_cols[None, :])[:, :, None]
    )
    duo_after_averaging = duo_embedding + update
    pair_input = (standardize_features(duo_after_averaging) * duo_layernorm_stretch).astype(
        jnp.bfloat16
    )
    bias_tile = jnp.einsum(
        "ijc,ch->hij", pair_input, duo_logit_kernel, preferred_element_type=jnp.float32
    ).astype(jnp.bfloat16)
    bias_cols = gather_directly(bias_tile, "col", 2)
    exponential_probabilities = (standardized_features * lineup_layernorm_stretch).astype(
        jnp.bfloat16
    )
    rows_input, rows_mask = sent_together(
        (exponential_probabilities, shrunk_availability), "col", 0, 1, 2
    )
    bias_whole = lax.all_gather(bias_cols, "row", axis=1, tiled=True)
    projected = jnp.einsum(
        "src,cd->srd", rows_input, asker_lookup_sigmoid_kernel, preferred_element_type=jnp.float32
    ).astype(jnp.bfloat16)
    gated_whole = attend(
        projected[..., :inner_width],
        projected[..., 3 * inner_width :],
        projected[..., inner_width : 2 * inner_width],
        projected[..., 2 * inner_width : 3 * inner_width],
        rows_mask,
        bias_whole,
        head_count,
    )
    gated_local = lax.all_to_all(gated_whole, "col", split_axis=1, concat_axis=0, tiled=True)
    summed_increment = jnp.einsum(
        "sqd,dc->sqc", gated_local, closing_linear_kernel, preferred_element_type=jnp.float32
    )
    refreshed_family_embedding = (
        aligned_family_embedding.astype(jnp.float32) + summed_increment
    ).astype(jnp.bfloat16)
    return (refreshed_family_embedding, duo_after_averaging)


def solution(mesh):
    placed = (
        P("row", "col", None),
        P("row", "col"),
        P(),
        P("row", "col", None),
        P(),
        P(),
        P(),
        P(),
        P(),
        P(),
        P(),
        P(),
        P(),
    )
    return jax.shard_map(
        shards,
        mesh=mesh,
        in_specs=placed,
        out_specs=(P("row", "col", None), P("row", "col", None)),
        check_vma=False,
    )
```

profile of v0, /device:TPU:1, one launch (start us, length us, event | category | flops | bytes accessed | tf_op | source)
XLA Modules:
  0.0 554.2 jit_solution(972236072395999321)
XLA Ops:
  7.3 2.2 convert_reduce_fusion
  10.6 1.3 fusion.16
  13.5 1.3 fusion.17
  16.7 42.0 %all-gather.9.cloned.1.call-done = bf16[811008]{0:T(1024)(128)(2,1)} async-done(((bf16[101376]{0:T(1024)(128)(2,1)}), bf16[811008]{0:T(1024)(128)(2,1)}) %all-gather.9.cloned.1.call-update) | async-done | bytes 1622032 | tf_op jit(solution)/shard_map/all_gather | solution.py:18
  58.7 3.3 reshape.216
  63.9 8.8 %all-to-all-start.2 = ((bf16[16,2,768]{2,1,0:T(2,128)(2,1)}), bf16[16,2,768]{2,1,0:T(2,128)(2,1)S(1)}, u32[]{:S(2)}, u32[]{:S(2)}) async-start(bf16[16,2,768]{2,1,0:T(2,128)(2,1)} %reshape.227), calls=%async_computation.2 | async-start | bytes 98304 | tf_op jit(solution)/shard_map/all_to_all | solution.py:159
  72.7 2.7 slice.36
  75.4 3.6 all_to_all.61
  79.0 3.4 copy.83
  82.4 7.4 %all-to-all-start.1 = ((bf16[32,16,1536]{2,0,1:T(8,128)(2,1)}), bf16[32,16,1536]{2,0,1:T(8,128)(2,1)}, u32[]{:S(2)}, u32[]{:S(2)}) async-start(bf16[32,16,1536]{2,0,1:T(8,128)(2,1)} %copy.83), calls=%async_computation.1 | async-start | bytes 3145728 | tf_op jit(solution)/shard_map/all_to_all | solution.py:158
  90.4 24.9 %all-to-all-done.1 = bf16[32,16,1536]{2,0,1:T(8,128)(2,1)} async-done(((bf16[32,16,1536]{2,0,1:T(8,128)(2,1)}), bf16[32,16,1536]{2,0,1:T(8,128)(2,1)}, u32[]{:S(2)}, u32[]{:S(2)}) %all-to-all-start.1) | async-done | bytes 1572896 | tf_op jit(solution)/shard_map/all_to_all | solution.py:158
  115.3 14.0 %all-gather.5.cloned.1.call-done = bf16[512,3168]{1,0:T(8,128)(2,1)} async-done(((bf16[32,3168]{1,0:T(8,128)(2,1)}), bf16[512,3168]{1,0:T(8,128)(2,1)}) %all-gather.5.cloned.1.call-update) | async-done | bytes 3244048 | tf_op jit(solution)/shard_map/all_gather | solution.py:32
  129.3 9.5 %convolution_convert_fusion = bf16[1536,3072]{1,0:T(8,128)(2,1)} fusion(bf16[512,1536]{1,0:T(8,128)(2,1)} %bitcast.18, bf16[512,3168]{1,0:T(8,128)(2,1)} %all-gather.5.cloned.1.call-done), kind=kOutput, calls=%fused_computation.13 | convolution fusion | flops 4836556800 | bytes 14155776 | tf_op jit(solution)/shard_map/dot_general | solution.py:162
  138.8 41.0 %reshape.210 = bf16[48,32,96,32]{3,2,1,0:T(8,128)(2,1)} reshape(bf16[1536,3072]{1,0:T(8,128)(2,1)} %convolution_convert_fusion) | data formatting | bytes 18874368 | tf_op jit(solution)/shard_map/reshape | solution.py:168
  180.9 17.1 %fusion.31 = (f32[48,96]{1,0:T(8,128)S(1)}, f32[48,96,128]{2,1,0:T(8,128)S(1)}) fusion(f32[48,96,128]{2,1,0:T(8,128)} %param.18, f32[48,96]{1,0:T(8,128)S(1)} %broadcast_multiply_fusion.1, f32[48,96]{1,0:T(8,128)S(1)} %convolution_add_fusion, bf16[48,32,96,32]{3,2,1,0:T(8,128)(2,1)} %reshape.210, bf16[32,32,128,1]{2,1,0,3:T(8,128)(2,1)S(1)} %bitcast.115), kind=kOutput, calls=%fused_computation.62 | convolution fusion | flops 1210314240 | bytes 14473216 | tf_op jit(solution)/shard_map/iajb,abk->ijk/dot_general | solution.py:172
  198.1 1.7 multiply_reduce_fusion.1
  199.8 2.0 fusion.20
  201.9 14.9 %all_to_all.79 = bf16[8,8,48,96]{3,2,1,0:T(8,128)(2,1)S(1)} all-to-all(bf16[8,8,48,96]{3,2,1,0:T(8,128)(2,1)S(1)} %broadcast_in_dim.6), channel_id=1, replica_groups=mesh['row'=16,'col'=8] {'col'}, dimensions={0} | all-to-all | bytes 1179648 | tf_op jit(solution)/shard_map/all_to_all | solution.py:37
  217.3 1.5 reshape.224
  220.2 1.8 pad_maximum_fusion
  222.0 4.3 copy.80
  226.3 4.6 all-to-all-start
  230.9 30.1 %all-to-all-done = bf16[32,96,257]{1,2,0:T(8,128)(2,1)} async-done(((bf16[32,96,257]{1,2,0:T(8,128)(2,1)}), bf16[32,96,257]{1,2,0:T(8,128)(2,1)}, u32[]{:S(2)}, u32[]{:S(2)}) %all-to-all-start) | async-done | bytes 1579040 | tf_op jit(solution)/shard_map/all_to_all | solution.py:48
  261.1 4.3 copy.81
  265.4 1.4 slice_reduce_fusion
  266.8 3.2 convolution_convert_fusion.1
  270.1 2.8 slice_bitcast_fusion
  272.9 43.3 %all-gather.7.cloned.1.call-done = bf16[8,768,768]{2,0,1:T(8,128)(2,1)} async-done(((bf16[8,48,768]{2,0,1:T(8,128)(2,1)}), bf16[8,768,768]{2,0,1:T(8,128)(2,1)}) %all-gather.7.cloned.1.call-update) | async-done | bytes 9437200 | tf_op jit(solution)/shard_map/all_gather | solution.py:197
  316.2 15.4 %copy.95 = f32[8,768,768]{1,2,0:T(8,128)} copy(bf16[8,768,768]{2,0,1:T(8,128)(2,1)} %all-gather.7.cloned.1.call-done) | data formatting | bytes 28311552 | tf_op jit(solution)/shard_map/while | solution.py:111
  331.6 186.1 %while.12 = (s32[]{:T(128)}, bf16[4,1,768,256]{2,3,1,0:T(8,128)(2,1)}, bf16[4,1,768,256]{3,2,0,1:T(8,128)(2,1)}, bf16[4,1,768,256]{3,2,0,1:T(8,128)(2,1)}, bf16[...) while((s32[]{:T(128)}, ...), condition=%wide.region_7.8_spmd, body=%wide.region_4.7_spmd.sunk | while | flops 642918144 | bytes 85385320 | solution.py:111
  333.0 1.2 constant_dynamic-slice_fusion.7
  334.3 12.1 %add_add_fusion.2 = f32[8,768,768]{1,2,0:T(8,128)} fusion(f32[8,768,768]{1,2,0:T(8,128)} %get-tuple-element.252, f32[768]{0:T(1024)S(1)} %multiply_reduce_fusion.3, bf16[768,8,32]{0,2,1:T(8,128)(2,1)S(1)} %bitcast.100, bf16[768,8,32]{0,2,1:T(8,128)(2,1)S(1)} %bitcast.101), kind=kOutput, calls=%fused_computation.3.clone.1 | convolution fusion | flops 316145664 | bytes 38538240 | tf_op jit(solution)/shard_map/while/body/eval_jaxpr/bqhd,bkhd->bhqk/dot_general | solution.py:91
  346.4 13.7 %fusion.55 = f32[8,768]{1,0:T(8,128)S(1)} fusion(f32[8,768,768]{1,2,0:T(8,128)} %add_add_fusion.2), kind=kOutput, calls=%fused_computation.60.clone.1 | output fusion | flops 9437951 | bytes 18898944 | tf_op jit(solution)/shard_map/while/body/eval_jaxpr/sub | solution.py:100
  360.4 16.6 %fusion.56 = f32[8,32,768]{2,1,0:T(8,128)S(1)} fusion(bf16[768,8,32]{0,2,1:T(8,128)(2,1)S(1)} %bitcast.103, f32[8,768]{1,0:T(8,128)S(1)} %fusion.55, f32[8,768,768]{1,2,0:T(8,128)} %add_add_fusion.2), kind=kOutput, calls=%fused_computation.4.clone.1 | convolution fusion | flops 316152576 | bytes 20078592 | tf_op jit(solution)/shard_map/while/body/eval_jaxpr/bhqk,bkhd->bqhd/dot_general | solution.py:102
  379.5 1.2 constant_dynamic-slice_fusion.7
  380.9 12.1 %add_add_fusion.2 = f32[8,768,768]{1,2,0:T(8,128)} fusion(f32[8,768,768]{1,2,0:T(8,128)} %get-tuple-element.252, f32[768]{0:T(1024)S(1)} %multiply_reduce_fusion.3, bf16[768,8,32]{0,2,1:T(8,128)(2,1)S(1)} %bitcast.100, bf16[768,8,32]{0,2,1:T(8,128)(2,1)S(1)} %bitcast.101), kind=kOutput, calls=%fused_computation.3.clone.1 | convolution fusion | flops 316145664 | bytes 38538240 | tf_op jit(solution)/shard_map/while/body/eval_jaxpr/bqhd,bkhd->bhqk/dot_general | solution.py:91
  393.0 13.7 %fusion.55 = f32[8,768]{1,0:T(8,128)S(1)} fusion(f32[8,768,768]{1,2,0:T(8,128)} %add_add_fusion.2), kind=kOutput, calls=%fused_computation.60.clone.1 | output fusion | flops 9437951 | bytes 18898944 | tf_op jit(solution)/shard_map/while/body/eval_jaxpr/sub | solution.py:100
  406.9 16.6 %fusion.56 = f32[8,32,768]{2,1,0:T(8,128)S(1)} fusion(bf16[768,8,32]{0,2,1:T(8,128)(2,1)S(1)} %bitcast.103, f32[8,768]{1,0:T(8,128)S(1)} %fusion.55, f32[8,768,768]{1,2,0:T(8,128)} %add_add_fusion.2), kind=kOutput, calls=%fused_computation.4.clone.1 | convolution fusion | flops 316152576 | bytes 20078592 | tf_op jit(solution)/shard_map/while/body/eval_jaxpr/bhqk,bkhd->bqhd/dot_general | solution.py:102
  427.4 12.1 %add_add_fusion.2 = f32[8,768,768]{1,2,0:T(8,128)} fusion(f32[8,768,768]{1,2,0:T(8,128)} %get-tuple-element.252, f32[768]{0:T(1024)S(1)} %multiply_reduce_fusion.3, bf16[768,8,32]{0,2,1:T(8,128)(2,1)S(1)} %bitcast.100, bf16[768,8,32]{0,2,1:T(8,128)(2,1)S(1)} %bitcast.101), kind=kOutput, calls=%fused_computation.3.clone.1 | convolution fusion | flops 316145664 | bytes 38538240 | tf_op jit(solution)/shard_map/while/body/eval_jaxpr/bqhd,bkhd->bhqk/dot_general | solution.py:91
  439.5 13.7 %fusion.55 = f32[8,768]{1,0:T(8,128)S(1)} fusion(f32[8,768,768]{1,2,0:T(8,128)} %add_add_fusion.2), kind=kOutput, calls=%fused_computation.60.clone.1 | output fusion | flops 9437951 | bytes 18898944 | tf_op jit(solution)/shard_map/while/body/eval_jaxpr/sub | solution.py:100
  453.4 16.6 %fusion.56 = f32[8,32,768]{2,1,0:T(8,128)S(1)} fusion(bf16[768,8,32]{0,2,1:T(8,128)(2,1)S(1)} %bitcast.103, f32[8,768]{1,0:T(8,128)S(1)} %fusion.55, f32[8,768,768]{1,2,0:T(8,128)} %add_add_fusion.2), kind=kOutput, calls=%fused_computation.4.clone.1 | convolution fusion | flops 316152576 | bytes 20078592 | tf_op jit(solution)/shard_map/while/body/eval_jaxpr/bhqk,bkhd->bqhd/dot_general | solution.py:102
  473.9 12.1 %add_add_fusion.2 = f32[8,768,768]{1,2,0:T(8,128)} fusion(f32[8,768,768]{1,2,0:T(8,128)} %get-tuple-element.252, f32[768]{0:T(1024)S(1)} %multiply_reduce_fusion.3, bf16[768,8,32]{0,2,1:T(8,128)(2,1)S(1)} %bitcast.100, bf16[768,8,32]{0,2,1:T(8,128)(2,1)S(1)} %bitcast.101), kind=kOutput, calls=%fused_computation.3.clone.1 | convolution fusion | flops 316145664 | bytes 38538240 | tf_op jit(solution)/shard_map/while/body/eval_jaxpr/bqhd,bkhd->bhqk/dot_general | solution.py:91
  486.0 13.7 %fusion.55 = f32[8,768]{1,0:T(8,128)S(1)} fusion(f32[8,768,768]{1,2,0:T(8,128)} %add_add_fusion.2), kind=kOutput, calls=%fused_computation.60.clone.1 | output fusion | flops 9437951 | bytes 18898944 | tf_op jit(solution)/shard_map/while/body/eval_jaxpr/sub | solution.py:100
  499.9 16.6 %fusion.56 = f32[8,32,768]{2,1,0:T(8,128)S(1)} fusion(bf16[768,8,32]{0,2,1:T(8,128)(2,1)S(1)} %bitcast.103, f32[8,768]{1,0:T(8,128)S(1)} %fusion.55, f32[8,768,768]{1,2,0:T(8,128)} %add_add_fusion.2), kind=kOutput, calls=%fused_computation.4.clone.1 | convolution fusion | flops 316152576 | bytes 20078592 | tf_op jit(solution)/shard_map/while/body/eval_jaxpr/bhqk,bkhd->bqhd/dot_general | solution.py:102
  517.7 2.7 copy.98
  520.5 23.8 %all_to_all.80 = bf16[4,768,256]{2,0,1:T(4,128)(2,1)S(1)} all-to-all(bf16[4,768,256]{2,0,1:T(4,128)(2,1)S(1)} %bitcast.107), channel_id=1, replica_groups=mesh['row'=16,'col'=8] {'col'}, dimensions={1} | all-to-all | bytes 3145728 | tf_op jit(solution)/shard_map/all_to_all | solution.py:210
  544.7 1.2 copy-done.3
  545.9 1.7 fusion.11
  (100 shorter events, 24.4 us)
Async XLA Ops:
  7.2 259.7 %copy-start = (bf16[256,1024]{1,0:T(8,128)(2,1)S(1)}, bf16[256,1024]{1,0:T(8,128)(2,1)}, u32[]{:S(2)}) copy-start(bf16[256,1024]{1,0:T(8,128)(2,1)} %param.26) | copy-start | bytes 1572868
  7.2 2.3 copy-start.2
  7.2 3.3 copy-start.6
  7.2 3.3 copy-start.14
  7.2 3.3 copy-start.12
  7.2 51.5 %all-gather.9.cloned.1.call-start = ((), (), s32[]{:S(2)}) async-start(), calls=%async_computation.7 | async-start | bytes 1824768 | tf_op jit(solution)/shard_map/all_gather | solution.py:18
  10.6 2.9 copy-start.13
  13.4 115.9 %all-gather.5.cloned.1.call-start = ((), (), s32[]{:S(2)}) async-start(), calls=%async_computation.5 | async-start | bytes 3481600 | tf_op jit(solution)/shard_map/all_gather | solution.py:32
  63.9 18.5 %all-to-all-start.2 = ((bf16[16,2,768]{2,1,0:T(2,128)(2,1)}), bf16[16,2,768]{2,1,0:T(2,128)(2,1)S(1)}, u32[]{:S(2)}, u32[]{:S(2)}) async-start(bf16[16,2,768]{2,1,0:T(2,128)(2,1)} %reshape.227), calls=%async_computation.2 | async-start | bytes 98304 | tf_op jit(solution)/shard_map/all_to_all | solution.py:159
  82.4 7.6 %copy-start.7 = (s32[768]{0:T(1024)S(1)}, s32[768]{0:T(1024)}, u32[]{:S(2)}) copy-start(s32[768]{0:T(1024)} %param.17) | copy-start | bytes 9220
  82.4 32.9 %all-to-all-start.1 = ((bf16[32,16,1536]{2,0,1:T(8,128)(2,1)}), bf16[32,16,1536]{2,0,1:T(8,128)(2,1)}, u32[]{:S(2)}, u32[]{:S(2)}) async-start(bf16[32,16,1536]{2,0,1:T(8,128)(2,1)} %copy.83), calls=%async_computation.1 | async-start | bytes 3145728 | tf_op jit(solution)/shard_map/all_to_all | solution.py:158
  89.8 226.5 %all-gather.7.cloned.1.call-start = ((), (), s32[]{:S(2)}) async-start(), calls=%async_computation.6 | async-start | bytes 10027008 | tf_op jit(solution)/shard_map/all_gather | solution.py:197
  138.8 42.1 %copy-start.11 = (bf16[1024,128]{1,0:T(8,128)(2,1)S(1)}, bf16[1024,128]{1,0:T(8,128)(2,1)}, u32[]{:S(2)}) copy-start(bf16[1024,128]{1,0:T(8,128)(2,1)} %param.24) | copy-start | bytes 786436
  198.0 3.7 copy-start.4
  198.0 1.7 copy-start.8
  198.0 1.7 copy-start.10
  216.8 2.4 copy-start.9
  226.3 34.8 %all-to-all-start = ((bf16[32,96,257]{1,2,0:T(8,128)(2,1)}), bf16[32,96,257]{1,2,0:T(8,128)(2,1)}, u32[]{:S(2)}, u32[]{:S(2)}) async-start(bf16[32,96,257]{1,2,0:T(8,128)(2,1)} %copy.80), calls=%async_computation | async-start | bytes 4325376 | tf_op jit(solution)/shard_map/all_to_all | solution.py:48
  544.5 1.4 copy-start.3
  544.5 1.4 copy-start.5
  544.6 3.0 copy-start.1
Sparse Core Ops, SparseCore 0:
  13.6 45.1 all-gather.8
  61.1 68.1 all-gather.4
  218.9 97.2 all-gather.6
where the time goes:
time: 557 us; the launch traced here: 554 us
  waiting for transfers between devices  154 us (28%)
  matrix products  152 us (27%)
  local copies, waits for them, and re-layouts  105 us (19%)
  other arithmetic  68 us (12%)
  blocking collectives  38.7 us (7%)
  starting transfers between devices  21.1 us (4%)
  between operations  14.2 us (3%)
    dot_general x4, matrix products, one_block(): jnp.einsum('bhqk,bkhd->bqhd', weights, value_heads, preferred_element_typ...  66.6 us
    sub x4, other arithmetic, one_block(): exponent = jnp.exp(scores - highest)  54.9 us
    dot_general x4, matrix products, one_block(): jnp.einsum('bqhd,bkhd->bhqk', query_heads, key_heads, preferred_element_t...  48.4 us
    all_gather x1, waiting for transfers between devices, shards(): bias_whole = lax.all_gather(bias_cols, 'row', axis=1, tiled=True)  43.3 us
    all_gather x1, waiting for transfers between devices, one_gather(): lines, at, outs = (lax.all_gather(line, axis), 0, [])  42 us
    reshape x1, local copies, waits for them, and re-layouts, shards(): outer_sum.astype(jnp.bfloat16)  41 us
    all_to_all x1, waiting for transfers between devices, sent_together(): lax.all_to_all(both, axis, split_axis=split_dim, concat_axis=concat_dim,...  30.1 us
    all_to_all x1, waiting for transfers between devices, shards(): lax.all_to_all(left_wide, 'row', split_axis=1, concat_axis=0, tiled=True)  24.9 us
  transfers between devices with their start and end apart: 6, of which 5 were waited for; matrix products, arithmetic and copies ran while one was open for 6% of the time, Pallas kernels for 0%

commit v1 on v0

v1 whole, which is shorter than its diff:
```python
import jax
import jax.numpy as jnp
from jax import lax
from jax.experimental import pallas as pl
from jax.experimental.pallas import tpu as pltpu
from jax.sharding import PartitionSpec as P

EPSILON = 1e-05
CONTRACT_FIRST = (((0,), (0,)), ((), ()))
LAST_LAST = (((1,), (1,)), ((), ()))
HEAD_DIM = 32


def laid_out(pieces, dim):
    lengths = list(pieces.shape[1:])
    lengths[dim] *= pieces.shape[0]
    return jnp.moveaxis(pieces, 0, dim).reshape(lengths)


def one_gather(arrays, axis, dims):
    line = jnp.concatenate([a.reshape(-1) for a in arrays])
    lines, at, outs = (lax.all_gather(line, axis), 0, [])
    for a, dim in zip(arrays, dims):
        pieces = lines[:, at : at + a.size].reshape(-1, *a.shape)
        outs.append(laid_out(pieces, dim))
        at += a.size
    return tuple(outs)


def in_one_piece(arrays, axis, dim, along):
    ends, at = ([], 0)
    for a in arrays[:-1]:
        at += a.shape[along]
        ends.append(at)
    both = jnp.concatenate(arrays, axis=along)
    return tuple(jnp.split(lax.all_gather(both, axis, axis=dim, tiled=True), ends, axis=along))


def sent_to_all(x, axis):
    copies = jnp.broadcast_to(x, (lax.axis_size(axis), *x.shape))
    return lax.all_to_all(copies, axis, split_axis=0, concat_axis=0, tiled=True)


def gather_directly(x, axis, dim):
    return laid_out(sent_to_all(x, axis), dim)


def sent_together(arrays, axis, split_dim, concat_dim, along):
    columns = [a.reshape(*a.shape[:along], -1) for a in arrays]
    both = jnp.concatenate(columns, axis=along)
    whole, at, outs = (
        lax.all_to_all(both, axis, split_axis=split_dim, concat_axis=concat_dim, tiled=True),
        0,
        [],
    )
    for a, column in zip(arrays, columns):
        section = whole[..., at : at + column.shape[along]]
        outs.append(section.reshape(*section.shape[:along], *a.shape[along:]))
        at += column.shape[along]
    return tuple(outs)


def standardize_features(values):
    average = jnp.mean(values, axis=-1, keepdims=True)
    centred = values - average
    variance = jnp.mean(centred * centred, axis=-1, keepdims=True)
    return centred * lax.rsqrt(variance + EPSILON)


def project_rows(inputs, weight, availability_real):
    projected = jnp.einsum("src,ca->sra", inputs, weight, preferred_element_type=jnp.float32)
    return (projected * availability_real[:, :, None]).astype(jnp.bfloat16)


LOG2E = 1.4426950408889634


def attn_kernel(x_ref, mb_ref, hm_ref, bias_ref, wq_ref, wk_ref, wv_ref, wg_ref, o_ref, q_s, kt_s, v_s, bf_s, acc_s):
    blk = pl.program_id(0)
    seqs = x_ref.shape[0]
    rows = o_ref.shape[1]
    heads = bias_ref.shape[0]
    scale = float(HEAD_DIM) ** -0.5

    @pl.when(blk == 0)
    def _():
        def project(b, carry):
            x = x_ref[b]
            q_s[b] = jnp.dot(x, wq_ref[...], preferred_element_type=jnp.float32).astype(jnp.bfloat16)
            v_s[b] = jnp.dot(x, wv_ref[...], preferred_element_type=jnp.float32).astype(jnp.bfloat16)
            kt_s[b] = lax.dot_general(
                wk_ref[...], x, LAST_LAST, preferred_element_type=jnp.float32
            ).astype(jnp.bfloat16)
            return carry

        lax.fori_loop(0, seqs, project, 0)

    at = pl.multiple_of(blk * rows, rows)

    def one_head(h, carry):
        bf_s[...] = bias_ref[h].astype(jnp.float32) * (1.0 / scale)
        own = hm_ref[h]
        own_f = own.astype(jnp.float32)
        other = (1.0 - own_f).astype(jnp.bfloat16)

        def one_seq(b, carry):
            q = q_s[b, pl.ds(at, rows), :] * own
            s = jnp.dot(q, kt_s[b], preferred_element_type=jnp.float32) + bf_s[...] + mb_ref[b]
            top = jnp.max(s, axis=1, keepdims=True)
            p = jnp.exp2(((s - top) * (scale * LOG2E)).astype(jnp.bfloat16))
            r = jnp.dot(p, v_s[b] * own + other, preferred_element_type=jnp.float32)
            mixed = r / pltpu.roll(r, HEAD_DIM, 1)
            acc_s[b] = jnp.where(own_f > 0.0, mixed, acc_s[b])
            return carry

        return lax.fori_loop(0, seqs, one_seq, carry)

    lax.fori_loop(0, heads, one_head, 0)

    def gate(b, carry):
        g = jnp.dot(x_ref[b, pl.ds(at, rows), :], wg_ref[...], preferred_element_type=jnp.float32)
        g = g.astype(jnp.bfloat16).astype(jnp.float32)
        o_ref[b] = (acc_s[b] * jax.nn.sigmoid(g)).astype(jnp.bfloat16)
        return carry

    lax.fori_loop(0, seqs, gate, 0)


def attention(x, mask, bias, w):
    seqs, length, channels = x.shape
    heads = bias.shape[0]
    lanes = heads * HEAD_DIM
    rows = 256
    scale = float(HEAD_DIM) ** -0.5
    mb = (1e9 / scale) * (mask.astype(jnp.float32) - 1.0)[:, None, :]
    hm = (jnp.arange(lanes)[None, None, :] // HEAD_DIM == jnp.arange(heads)[:, None, None]).astype(jnp.bfloat16)
    wq, wk, wv, wg = w
    whole = lambda a: pl.BlockSpec(a.shape, lambda i: (0,) * a.ndim)
    wk = wk.T
    return pl.pallas_call(
        attn_kernel,
        grid=(length // rows,),
        out_shape=jax.ShapeDtypeStruct((seqs, length, lanes), jnp.bfloat16),
        in_specs=[
            whole(x), whole(mb), whole(hm),
            pl.BlockSpec((heads, rows, length), lambda i: (0, i, 0)),
            whole(wq), whole(wk), whole(wv), whole(wg),
        ],
        out_specs=pl.BlockSpec((seqs, rows, lanes), lambda i: (0, i, 0)),
        scratch_shapes=[
            pltpu.VMEM((seqs, length, lanes), jnp.bfloat16),
            pltpu.VMEM((seqs, lanes, length), jnp.bfloat16),
            pltpu.VMEM((seqs, length, lanes), jnp.bfloat16),
            pltpu.VMEM((rows, length), jnp.float32),
            pltpu.VMEM((seqs, rows, lanes), jnp.float32),
        ],
        compiler_params=pltpu.CompilerParams(vmem_limit_bytes=48 << 20),
        name="attn",
    )(x, mb, hm, bias, wq, wk, wv, wg)


def opm_kernel(left_ref, right_ref, lmask_ref, rmask_ref, rrow_ref, rcol_ref, pair_ref, gain_ref, w_ref, wd_ref,
               out_ref, bias_ref, rt_s, wb_s, m_s):
    step = pl.program_id(0)
    opm = w_ref.shape[0]
    cols = pair_ref.shape[1]
    group = out_ref.shape[0] // 4
    chunk = 4 * cols

    @pl.when(step == 0)
    def _():
        wb_s[...] = jnp.zeros_like(wb_s)

        def fill(b, carry):
            for i in range(4):
                wb_s[pl.ds(pl.multiple_of(b * 128 + i * 32, 32), 32), i * 128 : (i + 1) * 128] = w_ref[b]
            return carry

        lax.fori_loop(0, opm, fill, 0)

        def flip(n, carry):
            at = pl.multiple_of(n * chunk, chunk)
            rt_s[pl.ds(at, chunk), :] = right_ref[:, pl.ds(at, chunk)].T
            return carry

        lax.fori_loop(0, opm // 4, flip, 0)

    def outer(n, carry):
        at = pl.multiple_of(n * chunk, chunk)
        m = jnp.dot(rt_s[pl.ds(at, chunk), :], left_ref[...], preferred_element_type=jnp.float32)
        m = m.astype(jnp.bfloat16)
        for bb in range(4):
            for g in range(group):
                m_s[g * cols : (g + 1) * cols, pl.ds(pl.multiple_of((n * 4 + bb) * 128, 128), 128)] = m[
                    bb * cols : (bb + 1) * cols, g * 128 : (g + 1) * 128
                ]
        return carry

    lax.fori_loop(0, opm // 4, outer, 0)
    counts = lax.dot_general(rmask_ref[...], lmask_ref[0], CONTRACT_FIRST, preferred_element_type=jnp.float32)
    factor = rcol_ref[...] * rrow_ref[0] / (counts + 0.001)
    update = jnp.dot(m_s[...], wb_s[...], preferred_element_type=jnp.float32)
    for g in range(group):
        for ii in range(4):
            i = 4 * g + ii
            u = update[g * cols : (g + 1) * cols, ii * 128 : (ii + 1) * 128]
            x = pair_ref[i] + u * factor[:, i : i + 1]
            out_ref[i] = x
            x = (standardize_features(x) * gain_ref[...]).astype(jnp.bfloat16)
            bias_ref[:, i, :] = lax.dot_general(wd_ref[...], x, LAST_LAST, preferred_element_type=jnp.float32)


def opm(left, right, lmask, rmask, rrow, rcol, pair, gain, kron, logit):
    rows, cols, channels = pair.shape
    seqs = left.shape[0]
    width = left.shape[1] // rows
    heads = logit.shape[1]
    per = 16
    steps = rows // per
    lm = lmask.reshape(seqs, steps, per).transpose(1, 0, 2)
    rr = rrow.reshape(steps, 1, per)
    rc = rcol.reshape(cols, 1)
    w = kron.reshape(width, width, channels).transpose(1, 0, 2)
    gain = gain.reshape(1, channels)
    wd = logit.T
    whole = lambda a: pl.BlockSpec(a.shape, lambda i: (0,) * a.ndim)
    return pl.pallas_call(
        opm_kernel,
        grid=(steps,),
        out_shape=(
            jax.ShapeDtypeStruct(pair.shape, jnp.float32),
            jax.ShapeDtypeStruct((heads, rows, cols), jnp.float32),
        ),
        in_specs=[
            pl.BlockSpec((seqs, per * width), lambda i: (0, i)),
            whole(right),
            pl.BlockSpec((1, seqs, per), lambda i: (i, 0, 0)),
            whole(rmask),
            pl.BlockSpec((1, 1, per), lambda i: (i, 0, 0)),
            whole(rc),
            pl.BlockSpec((per, cols, channels), lambda i: (i, 0, 0)),
            whole(gain), whole(w), whole(wd),
        ],
        out_specs=(
            pl.BlockSpec((per, cols, channels), lambda i: (i, 0, 0)),
            pl.BlockSpec((heads, per, cols), lambda i: (0, i, 0)),
        ),
        scratch_shapes=[
            pltpu.VMEM((cols * width, seqs), jnp.bfloat16),
            pltpu.VMEM((128 * width, 4 * channels), jnp.bfloat16),
            pltpu.VMEM((per // 4 * cols, 128 * width), jnp.bfloat16),
        ],
        compiler_params=pltpu.CompilerParams(vmem_limit_bytes=52 << 20),
        name="opm",
    )(left, right, lm, rmask, rr, rc, pair, gain, w, wd)


def shards(
    aligned_family_embedding,
    aligned_slot_available,
    chain_site_available,
    duo_embedding,
    averaging_layernorm_stretch,
    lineup_layernorm_stretch,
    duo_layernorm_stretch,
    lefthand_linear_kernel,
    righthand_linear_kernel,
    kronecker_linear_kernel,
    duo_logit_kernel,
    asker_lookup_sigmoid_kernel,
    closing_linear_kernel,
):
    homolog_number, amino_position_number, discarded_carry = aligned_family_embedding.shape
    res_rows = duo_embedding.shape[0]
    opm_width = lefthand_linear_kernel.shape[1]
    head_count = duo_logit_kernel.shape[1]
    inner_width = closing_linear_kernel.shape[0]
    row_index = lax.axis_index("row")
    col_index = lax.axis_index("col")
    standardized_features = standardize_features(aligned_family_embedding.astype(jnp.float32))
    availability_real = aligned_slot_available.astype(jnp.float32)
    shrunk_availability = aligned_slot_available.astype(jnp.bfloat16)
    opm_input = (standardized_features * averaging_layernorm_stretch).astype(jnp.bfloat16)
    left_flat = project_rows(opm_input, lefthand_linear_kernel, availability_real).reshape(
        homolog_number, amino_position_number * opm_width
    )
    right_flat = jnp.einsum(
        "src,ca->sar", opm_input, righthand_linear_kernel, preferred_element_type=jnp.float32
    )
    right_flat = (right_flat * availability_real[:, None, :]).astype(jnp.bfloat16)
    right_flat = right_flat.reshape(homolog_number, amino_position_number * opm_width)
    left_wide, mask_wide = one_gather((left_flat, shrunk_availability), "col", (1, 1))
    left_block, left_mask = (
        lax.all_to_all(left_wide, "row", split_axis=1, concat_axis=0, tiled=True),
        lax.all_to_all(mask_wide, "row", split_axis=1, concat_axis=0, tiled=True),
    )
    right_all, mask_all = in_one_piece((right_flat, shrunk_availability), "row", 0, 1)
    residue_float = chain_site_available.astype(jnp.float32)
    residue_rows = lax.dynamic_slice_in_dim(residue_float, row_index * res_rows, res_rows)
    residue_cols = lax.dynamic_slice_in_dim(
        residue_float, col_index * amino_position_number, amino_position_number
    )
    duo_after_averaging, bias_tile = opm(
        left_block, right_all, left_mask, mask_all, residue_rows, residue_cols, duo_embedding,
        duo_layernorm_stretch, kronecker_linear_kernel, duo_logit_kernel,
    )
    bias_tile = bias_tile.astype(jnp.bfloat16)
    bias_cols = gather_directly(bias_tile, "col", 2)
    exponential_probabilities = (standardized_features * lineup_layernorm_stretch).astype(
        jnp.bfloat16
    )
    rows_input, rows_mask = sent_together(
        (exponential_probabilities, shrunk_availability), "col", 0, 1, 2
    )
    bias_whole = lax.all_gather(bias_cols, "row", axis=1, tiled=True)
    half = inner_width // 2
    parts = []
    for k in range(2):
        w = [
            asker_lookup_sigmoid_kernel[:, n * inner_width + k * half : n * inner_width + (k + 1) * half]
            for n in range(4)
        ]
        parts.append(attention(rows_input, rows_mask, bias_whole[k * (head_count // 2) : (k + 1) * (head_count // 2)], w))
    gated_whole = jnp.concatenate(parts, axis=2)
    gated_local = lax.all_to_all(gated_whole, "col", split_axis=1, concat_axis=0, tiled=True)
    summed_increment = jnp.einsum(
        "sqd,dc->sqc", gated_local, closing_linear_kernel, preferred_element_type=jnp.float32
    )
    refreshed_family_embedding = (
        aligned_family_embedding.astype(jnp.float32) + summed_increment
    ).astype(jnp.bfloat16)
    return (refreshed_family_embedding, duo_after_averaging)


def solution(mesh):
    placed = (
        P("row", "col", None),
        P("row", "col"),
        P(),
        P("row", "col", None),
        P(),
        P(),
        P(),
        P(),
        P(),
        P(),
        P(),
        P(),
        P(),
    )
    return jax.shard_map(
        shards,
        mesh=mesh,
        in_specs=placed,
        out_specs=(P("row", "col", None), P("row", "col", None)),
        check_vma=False,
    )
```

time: 557 us -> 388 us (0.70)
  matrix products: 152 us -> 4.29 us
  Pallas kernels: 0 us -> 98 us
  other arithmetic: 68 us -> 8.34 us
  local copies, waits for them, and re-layouts: 105 us -> 46.9 us
    dot_general x13 -> x1, matrix products: 148 us -> 1.28 us  [shards(): jnp.einsum('src,ca->sar', opm_input, righthand_linear_kernel, preferred_e...]
    pallas_call x0 -> x3, Pallas kernels: none -> 98 us  [the longest x2 76.9 us: attention(): pl.pallas_call(attn_kernel, grid=(length // rows,), out_shape=jax.ShapeDt...]
    sub x4 -> x0, other arithmetic: 54.9 us -> none  [one_block(): exponent = jnp.exp(scores - highest)]
    reshape x3 -> x7, local copies, waits for them, and re-layouts: 44.7 us -> 1.16 us  [the longest x2 0.45 us: opm(): lm = lmask.reshape(seqs, steps, per).transpose(1, 0, 2)]
    all_to_all x1, waiting for transfers between devices: 24.9 us -> 0.01 us  [shards(): lax.all_to_all(left_wide, 'row', split_axis=1, concat_axis=0, tiled=True)]
    all_gather x1, waiting for transfers between devices: 14 us -> 38.2 us  [in_one_piece(): lax.all_gather(both, axis, axis=dim, tiled=True)]
    while x2 -> x0, local copies, waits for them, and re-layouts: 18.1 us -> none  [attend(): lax.map(one_block, (grouped(queries), grouped(gate_pre), grouped(keys_all...]
    dynamic_slice x25 -> x0, local copies, waits for them, and re-layouts: 12.2 us -> none  [the longest x24 12.1 us: attend(): lax.map(one_block, (grouped(queries), grouped(gate_pre), grouped(keys_all...]
  transfers between devices with their start and end apart: 6 -> 6, of which waited for: 5 -> 5; matrix products, arithmetic and copies ran while one was open for 6% -> 8% of each run, Pallas kernels for 0% -> 0%
where the time goes in v1:
time: 388 us; the launch traced here: 386 us
  waiting for transfers between devices  157 us (40%)
  Pallas kernels  98 us (25%)
  local copies, waits for them, and re-layouts  46.9 us (12%)
  blocking collectives  38.8 us (10%)
  starting transfers between devices  19.1 us (5%)
  between operations  14.2 us (4%)
  other arithmetic  8.34 us (2%)
  matrix products  4.29 us (1%)
    pallas_call x2, Pallas kernels, attention(): pl.pallas_call(attn_kernel, grid=(length // rows,), out_shape=jax.ShapeDt...  76.9 us
    all_gather x1, waiting for transfers between devices, shards(): bias_whole = lax.all_gather(bias_cols, 'row', axis=1, tiled=True)  44.2 us
    all_gather x1, waiting for transfers between devices, one_gather(): lines, at, outs = (lax.all_gather(line, axis), 0, [])  42.9 us
    all_gather x1, waiting for transfers between devices, in_one_piece(): lax.all_gather(both, axis, axis=dim, tiled=True)  38.2 us
    all_to_all x1, waiting for transfers between devices, sent_together(): lax.all_to_all(both, axis, split_axis=split_dim, concat_axis=concat_dim,...  29.9 us
    all_to_all x1, blocking collectives, shards(): lax.all_to_all(gated_whole, 'col', split_axis=1, concat_axis=0, tiled=True)  23.8 us
    pallas_call x1, Pallas kernels, opm(): pl.pallas_call(opm_kernel, grid=(steps,), out_shape=(jax.ShapeDtypeStruct...  21 us
    all_to_all x1, blocking collectives, sent_to_all(): return lax.all_to_all(copies, axis, split_axis=0, concat_axis=0, tiled=True)  15 us
  transfers between devices with their start and end apart: 6, of which 5 were waited for; matrix products, arithmetic and copies ran while one was open for 8% of the time, Pallas kernels for 0%

profile of v1, /device:TPU:1, one launch (start us, length us, event | category | flops | bytes accessed | tf_op | source)
XLA Modules:
  0.0 386.5 jit_solution(8893450524412393945)
XLA Ops:
  7.3 2.1 convert_reduce_fusion
  9.4 1.0 fusion.6
  10.6 1.3 fusion.8
  11.8 0.4 copy.56
  12.2 0.4 reshape_reshape.3
  12.7 0.7 pad_maximum_fusion.3
  13.5 1.3 fusion.10
  14.8 0.3 reshape.163
  15.1 0.7 pad_maximum_fusion.2
  15.8 42.9 %all-gather.9.cloned.1.call-done = bf16[811008]{0:T(1024)(128)(2,1)} async-done(((bf16[101376]{0:T(1024)(128)(2,1)}), bf16[811008]{0:T(1024)(128)(2,1)}) %all-gather.9.cloned.1.call-update) | async-done | bytes 1622032 | tf_op jit(solution)/shard_map/all_gather | solution.py:22
  58.7 2.1 reshape.171
  61.1 0.7 copy.79
  61.8 1.7 reshape.176
  63.5 8.8 %all-to-all-start.2 = ((bf16[16,2,768]{2,1,0:T(2,128)(2,1)}), bf16[16,2,768]{2,1,0:T(2,128)(2,1)S(1)}, u32[]{:S(2)}, u32[]{:S(2)}) async-start(bf16[16,2,768]{2,1,0:T(2,128)(2,1)} %reshape.176), calls=%async_computation.2 | async-start | bytes 98304 | tf_op jit(solution)/shard_map/all_to_all | solution.py:295
  72.3 1.2 slice.58
  73.5 2.5 all_to_all.59
  76.0 2.0 copy.57
  78.0 1.6 all-to-all-done.2
  79.7 5.7 %all-to-all-start.1 = ((bf16[32,16,1536]{2,0,1:T(8,128)(2,1)}), bf16[32,16,1536]{2,0,1:T(8,128)(2,1)}, u32[]{:S(2)}, u32[]{:S(2)}) async-start(bf16[32,16,1536]{2,0,1:T(8,128)(2,1)} %copy.57), calls=%async_computation.1 | async-start | bytes 3145728 | tf_op jit(solution)/shard_map/all_to_all | solution.py:294
  86.5 0.3 copy.61
  86.8 38.2 %all-gather.5.cloned.1.call-done = bf16[512,3168]{1,0:T(8,128)(2,1)} async-done(((bf16[32,3168]{1,0:T(8,128)(2,1)}), bf16[512,3168]{1,0:T(8,128)(2,1)}) %all-gather.5.cloned.1.call-update) | async-done | bytes 3244048 | tf_op jit(solution)/shard_map/all_gather | solution.py:36
  125.0 3.8 split.8.right_ref
  128.7 0.9 split.9.rmask_ref
  129.7 21.0 %opm.1 = (f32[48,96,128]{2,1,0:T(8,128)}, f32[8,48,96]{2,1,0:T(8,128)S(1)}) custom-call(bf16[512,1536]{1,0:T(8,128)(2,1)} %bitcast.8.left_ref, bf16[512,3072]{1,0:T(8,128)(2,1)} %split.8.right_ref, bf16[3,512,16]{2,1,0:T(8,128)(2,1)S(1)} %bitcast.57, bf16[512,96]{1,0:T(8,128)(2,1)S(1)} %split.9.rmask_ref, f32[3,1,16]{2,1,0:T(1,128)S(1)} %reshape.175.rrow_ref, ...), custom_call_target="tpu_custom_call" | custom-call | tf_op jit(solution)/shard_map/opm/pallas_call | solution.py:227
  150.8 15.0 %all_to_all.76 = bf16[8,8,48,96]{3,2,1,0:T(8,128)(2,1)S(1)} all-to-all(bf16[8,8,48,96]{3,2,1,0:T(8,128)(2,1)S(1)} %broadcast_in_dim.2), channel_id=1, replica_groups=mesh['row'=16,'col'=8] {'col'}, dimensions={0} | all-to-all | bytes 1179648 | tf_op jit(solution)/shard_map/all_to_all | solution.py:41
  165.9 0.5 copy.65
  166.4 1.5 reshape.170
  167.9 0.4 copy.53
  168.3 1.0 fusion.4
  169.3 1.7 pad_maximum_fusion
  171.1 4.3 %copy.54 = bf16[32,96,257]{1,2,0:T(8,128)(2,1)} copy(bf16[32,96,257]{2,1,0:T(8,128)(2,1)} %pad_maximum_fusion) | data formatting | bytes 3158016 | tf_op jit(solution)/shard_map/concatenate | solution.py:50
  175.4 4.5 %all-to-all-start = ((bf16[32,96,257]{1,2,0:T(8,128)(2,1)}), bf16[32,96,257]{1,2,0:T(8,128)(2,1)}, u32[]{:S(2)}, u32[]{:S(2)}) async-start(bf16[32,96,257]{1,2,0:T(8,128)(2,1)} %copy.54), calls=%async_computation | async-start | bytes 4325376 | tf_op jit(solution)/shard_map/all_to_all | solution.py:52
  180.3 29.9 %all-to-all-done = bf16[32,96,257]{1,2,0:T(8,128)(2,1)} async-done(((bf16[32,96,257]{1,2,0:T(8,128)(2,1)}), bf16[32,96,257]{1,2,0:T(8,128)(2,1)}, u32[]{:S(2)}, u32[]{:S(2)}) %all-to-all-start) | async-done | bytes 1579040 | tf_op jit(solution)/shard_map/all_to_all | solution.py:52
  210.1 3.8 copy.77
  214.0 3.5 all_to_all.58
  217.5 1.2 copy-done.5
  218.7 1.2 slice.56
  219.9 1.7 copy.67.x_ref
  221.6 0.8 fusion.18.mb_ref
  222.4 44.2 %all-gather.7.cloned.1.call-done = bf16[8,768,768]{2,1,0:T(8,128)(2,1)} async-done(((bf16[8,48,768]{2,1,0:T(8,128)(2,1)}), bf16[8,768,768]{2,1,0:T(8,128)(2,1)}) %all-gather.7.cloned.1.call-update) | async-done | bytes 9437200 | tf_op jit(solution)/shard_map/all_gather | solution.py:315
  266.6 8.0 %fusion.19 = (bf16[4,768,768]{2,1,0:T(8,128)(2,1)}, bf16[4,768,768]{2,1,0:T(8,128)(2,1)}) fusion(bf16[8,768,768]{2,1,0:T(8,128)(2,1)} %all-gather.7.cloned.1.call-done), kind=kLoop, calls=%fused_computation.37 | loop fusion | bytes 18874368 | tf_op jit(solution)/shard_map/slice | solution.py:323
  274.6 38.5 %attn.2 = bf16[4,768,128]{2,1,0:T(8,128)(2,1)S(1)} custom-call(bf16[4,768,256]{2,1,0:T(8,128)(2,1)S(1)} %copy.67.x_ref, f32[4,1,768]{2,1,0:T(1,128)S(1)} %fusion.18.mb_ref, bf16[4,1,128]{2,1,0:T(2,128)(2,1)S(1)} %compare_convert_fusion.hm_ref, bf16[4,768,768]{2,1,0:T(8,128)(2,1)} %get-tuple-element.6.bias_ref, ...), custom_call_target="tpu_custom_call" | custom-call | tf_op jit(solution)/shard_map/attn/pallas_call | solution.py:140
  313.1 38.5 %attn.3 = bf16[4,768,128]{2,1,0:T(8,128)(2,1)S(1)} custom-call(bf16[4,768,256]{2,1,0:T(8,128)(2,1)S(1)} %copy.67.x_ref, f32[4,1,768]{2,1,0:T(1,128)S(1)} %fusion.18.mb_ref, bf16[4,1,128]{2,1,0:T(2,128)(2,1)S(1)} %compare_convert_fusion.hm_ref, bf16[4,768,768]{2,1,0:T(8,128)(2,1)} %get-tuple-element.7.bias_ref, ...), custom_call_target="tpu_custom_call" | custom-call | tf_op jit(solution)/shard_map/attn/pallas_call | solution.py:140
  351.7 1.2 copy.70
  353.0 23.8 %all_to_all.77 = bf16[4,768,256]{2,0,1:T(4,128)(2,1)S(1)} all-to-all(bf16[4,768,256]{2,0,1:T(4,128)(2,1)S(1)} %copy.70), channel_id=1, replica_groups=mesh['row'=16,'col'=8] {'col'}, dimensions={1} | all-to-all | bytes 3145728 | tf_op jit(solution)/shard_map/all_to_all | solution.py:325
  376.8 0.3 copy.71
  377.1 1.1 copy-done.4
  378.2 1.7 fusion.7
  (63 shorter events, 2.2 us)
Async XLA Ops:
  7.2 369.9 %copy-start = (bf16[256,256]{1,0:T(8,128)(2,1)S(1)}, bf16[256,256]{1,0:T(8,128)(2,1)}, u32[]{:S(2)}) copy-start(bf16[256,256]{1,0:T(8,128)(2,1)} %param.25) | copy-start | bytes 393220
  7.2 2.2 copy-start.3
  7.2 3.3 copy-start.10
  7.2 3.3 copy-start.15
  7.2 3.3 copy-start.13
  7.2 51.5 %all-gather.9.cloned.1.call-start = ((), (), s32[]{:S(2)}) async-start(), calls=%async_computation.7 | async-start | bytes 1824768 | tf_op jit(solution)/shard_map/all_gather | solution.py:22
  10.5 3.0 copy-start.8
  10.5 2.9 copy-start.14
  13.4 111.5 %all-gather.5.cloned.1.call-start = ((), (), s32[]{:S(2)}) async-start(), calls=%async_computation.5 | async-start | bytes 3481600 | tf_op jit(solution)/shard_map/all_gather | solution.py:36
  63.5 16.1 %all-to-all-start.2 = ((bf16[16,2,768]{2,1,0:T(2,128)(2,1)}), bf16[16,2,768]{2,1,0:T(2,128)(2,1)S(1)}, u32[]{:S(2)}, u32[]{:S(2)}) async-start(bf16[16,2,768]{2,1,0:T(2,128)(2,1)} %reshape.176), calls=%async_computation.2 | async-start | bytes 98304 | tf_op jit(solution)/shard_map/all_to_all | solution.py:295
  78.0 7.4 %copy-start.11 = (s32[768]{0:T(1024)S(1)}, s32[768]{0:T(1024)}, u32[]{:S(2)}) copy-start(s32[768]{0:T(1024)} %param.15) | copy-start | bytes 9220
  78.0 7.8 %copy-start.7 = (bf16[1024,128]{1,0:T(8,128)(2,1)S(1)}, bf16[1024,128]{1,0:T(8,128)(2,1)}, u32[]{:S(2)}) copy-start(bf16[1024,128]{1,0:T(8,128)(2,1)} %param.22) | copy-start | bytes 786436
  79.7 50.0 %all-to-all-start.1 = ((bf16[32,16,1536]{2,0,1:T(8,128)(2,1)}), bf16[32,16,1536]{2,0,1:T(8,128)(2,1)}, u32[]{:S(2)}, u32[]{:S(2)}) async-start(bf16[32,16,1536]{2,0,1:T(8,128)(2,1)} %copy.57), calls=%async_computation.1 | async-start | bytes 3145728 | tf_op jit(solution)/shard_map/all_to_all | solution.py:294
  85.4 181.2 %all-gather.7.cloned.1.call-start = ((), (), s32[]{:S(2)}) async-start(), calls=%async_computation.6 | async-start | bytes 10027008 | tf_op jit(solution)/shard_map/all_gather | solution.py:315
  86.8 42.9 %copy-start.1 = (bf16[128,8]{0,1:T(8,128)(2,1)S(1)}, bf16[128,8]{0,1:T(8,128)(2,1)}, u32[]{:S(2)}) copy-start(bf16[128,8]{0,1:T(8,128)(2,1)} %param.23) | copy-start | bytes 6148
  86.8 42.9 %copy-start.2 = (f32[128]{0:T(128)S(1)}, f32[128]{0:T(128)}, u32[]{:S(2)}) copy-start(f32[128]{0:T(128)} %param.19) | copy-start | bytes 1540
  165.8 2.5 copy-start.9
  165.8 2.5 copy-start.12
  175.4 4.5 %copy-start.6 = (bf16[256,1024]{1,0:T(8,128)(2,1)S(1)}, bf16[256,1024]{1,0:T(8,128)(2,1)}, u32[]{:S(2)}) copy-start(bf16[256,1024]{1,0:T(8,128)(2,1)} %param.24) | copy-start | bytes 1572868
  175.4 34.8 %all-to-all-start = ((bf16[32,96,257]{1,2,0:T(8,128)(2,1)}), bf16[32,96,257]{1,2,0:T(8,128)(2,1)}, u32[]{:S(2)}, u32[]{:S(2)}) async-start(bf16[32,96,257]{1,2,0:T(8,128)(2,1)} %copy.54), calls=%async_computation | async-start | bytes 4325376 | tf_op jit(solution)/shard_map/all_to_all | solution.py:52
  217.5 1.2 copy-start.5
  376.8 1.4 copy-start.4
Sparse Core Ops, SparseCore 0:
  13.5 45.1 all-gather.8
  61.7 63.2 all-gather.4
  168.0 98.5 all-gather.6

commit v2 on v1

v2 whole, which is shorter than its diff:
```python
import jax
import jax.numpy as jnp
from jax import lax
from jax.experimental import pallas as pl
from jax.experimental.pallas import tpu as pltpu
from jax.sharding import PartitionSpec as P

EPSILON = 1e-05
CONTRACT_FIRST = (((0,), (0,)), ((), ()))
LAST_LAST = (((1,), (1,)), ((), ()))
HEAD_DIM = 32


def standardize_features(values):
    average = jnp.mean(values, axis=-1, keepdims=True)
    centred = values - average
    variance = jnp.mean(centred * centred, axis=-1, keepdims=True)
    return centred * lax.rsqrt(variance + EPSILON)


MESH = pl.DeviceIdType.MESH


def place():
    r, c = lax.axis_index("row"), lax.axis_index("col")
    return r, c


def row_of(y, zh, core):
    return y * 4 + zh * 2 + core


def remote(src, dst, send, recv, device):
    return pltpu.make_async_remote_copy(
        src_ref=src, dst_ref=dst, send_sem=send, recv_sem=recv, device_id=device, device_id_type=MESH
    )


def signal(barrier, device):
    pl.semaphore_signal(barrier, inc=1, device_id=device, device_id_type=MESH)


def spread_kernel(left_ref, right_ref, left_out, right_out, lsend, lrecv, rsend, rrecv, fsend, frecv):
    r, c = place()
    chip, core = r // 2, r % 2
    seqs = right_ref.shape[0]
    here = pl.ds(pl.multiple_of(r * seqs, seqs), seqs)
    partner = (chip * 2 + 1 - core, c)
    mine = chip == c
    barrier = pltpu.get_barrier_semaphore()
    for d in range(1, 8):
        signal(barrier, ((r + 2 * d) % 16, c))
    signal(barrier, partner)
    for n in range(16):

        @pl.when(jnp.logical_not(jnp.logical_and(mine, r == n)))
        def _():
            signal(barrier, (n, chip))

    pl.semaphore_wait(barrier, 24 - mine.astype(jnp.int32))

    rights = [None]
    for d in range(1, 8):
        cp = remote(right_ref, right_out.at[here], rsend.at[d], rrecv.at[d], ((r + 2 * d) % 16, c))
        cp.start()
        rights.append(cp)
    own = pltpu.make_async_copy(right_ref, right_out.at[here], rrecv.at[0])
    own.start()
    forwards = [remote(right_ref, right_out.at[here], fsend.at[0], frecv.at[0], partner)]
    forwards[0].start()
    lefts = []
    for j in range(8):
        for h in range(2):
            cd = (c + j) % 8
            cp = remote(left_ref.at[h], left_out.at[here], lsend.at[2 * j + h], lrecv.at[r], (2 * c + h, cd))
            lefts.append((cp, h, j))
            if j == 0:
                own_left = jnp.logical_and(mine, core == h)

                @pl.when(jnp.logical_not(own_left))
                def _():
                    cp.start()

                @pl.when(own_left)
                def _():
                    pltpu.make_async_copy(left_ref.at[h], left_out.at[here], lrecv.at[r]).start()
            else:
                cp.start()
    for d in range(1, 8):
        rights[d].wait_recv()
        block = pl.ds(pl.multiple_of(((r + 16 - 2 * d) % 16) * seqs, seqs), seqs)
        fw = remote(right_out.at[block], right_out.at[block], fsend.at[d], frecv.at[d], partner)
        fw.start()
        forwards.append(fw)
    own.wait()
    for n in range(16):
        pltpu.make_async_copy(left_ref.at[0], left_out.at[pl.ds(n * seqs, seqs)], lrecv.at[n]).wait()
    for d in range(8):
        forwards[d].wait()
    for d in range(1, 8):
        rights[d].wait_send()
    for cp, h, j in lefts:
        if j == 0:

            @pl.when(jnp.logical_not(jnp.logical_and(mine, core == h)))
            def _():
                cp.wait_send()
        else:
            cp.wait_send()


def spread(left, right):
    seqs = right.shape[0]
    vmem = pl.BlockSpec(memory_space=pltpu.VMEM)
    hbm = pl.BlockSpec(memory_space=pl.ANY)
    dma = pltpu.SemaphoreType.DMA
    return pl.pallas_call(
        spread_kernel,
        out_shape=(
            jax.ShapeDtypeStruct((16 * seqs, left.shape[2]), jnp.bfloat16),
            jax.ShapeDtypeStruct((16 * seqs, right.shape[1]), jnp.bfloat16),
        ),
        in_specs=[vmem, vmem],
        out_specs=(hbm, hbm),
        scratch_shapes=[dma((16,)), dma((16,)), dma((8,)), dma((8,)), dma((8,)), dma((8,))],
        compiler_params=pltpu.CompilerParams(collective_id=1, has_side_effects=True),
        name="spread",
    )(left, right)


def share_kernel(tile_ref, x_ref, m_ref, a_out, b_out, c_out, x_out, m_out, block,
                 csend, crecv, csem, s1, r1, l1, s2, r2, s3, r3):
    r, c = place()
    spot = {"x": c // 2, "y": r // 4, "z": ((r // 2) % 2) * 2 + c % 2}
    core = r % 2

    def peer(dim, d):
        to = dict(spot)
        to[dim] = (spot[dim] + d) % 4
        return (row_of(to["y"], to["z"] // 2, core), to["x"] * 2 + to["z"] % 2)

    partner = ((r // 2) * 2 + 1 - core, c)
    barrier = pltpu.get_barrier_semaphore()
    signal(barrier, partner)
    for dim in "xyz":
        for d in range(1, 4):
            signal(barrier, peer(dim, d))
    pl.semaphore_wait(barrier, 10)

    rows, lanes = tile_ref.shape[0], tile_ref.shape[1] // 2
    here = pl.ds(pl.multiple_of(core * rows, rows), rows)
    give = tile_ref.at[:, pl.ds(pl.multiple_of((1 - core) * lanes, lanes), lanes)]
    keep = tile_ref.at[:, pl.ds(pl.multiple_of(core * lanes, lanes), lanes)]
    swap = remote(give, block.at[here], csend.at[0], crecv.at[0], partner)
    swap.start()
    own = pltpu.make_async_copy(keep, block.at[here], csem.at[0])
    own.start()
    xs = remote(x_ref, x_out, csend.at[1], crecv.at[1], partner)
    ms = remote(m_ref, m_out, csend.at[2], crecv.at[2], partner)
    own.wait()
    swap.wait_recv()

    orders = ((a_out, "xzy"), (b_out, "yxz"), (c_out, "zyx"))
    part = block.shape[0] // 3
    sent = []
    first = []
    for o, (out, dims) in enumerate(orders):
        d1, d2, d3 = dims
        slot = out.at[spot[d3], spot[d2], spot[d1]]
        piece = block.at[pl.ds(o * part, part)]
        mine = pltpu.make_async_copy(piece, slot, l1.at[o])
        mine.start()
        cps = []
        for d in range(1, 4):
            cp = remote(piece, slot, s1.at[o * 4 + d], r1.at[o * 4 + d], peer(d1, d))
            cp.start()
            cps.append(cp)
        first.append((mine, cps))
        sent += cps
    xs.start()
    ms.start()
    second = []
    for o, (out, dims) in enumerate(orders):
        d1, d2, d3 = dims
        mine, cps = first[o]
        mine.wait()
        for cp in cps:
            cp.wait_recv()
        slot = out.at[spot[d3], spot[d2]]
        cps = []
        for d in range(1, 4):
            cp = remote(slot, slot, s2.at[o * 4 + d], r2.at[o * 4 + d], peer(d2, d))
            cp.start()
            cps.append(cp)
        second.append(cps)
        sent += cps
        for d in range(1, 4):
            cp = remote(slot, slot, s3.at[o * 16 + d], r3.at[o * 16 + d], peer(d3, d))
            cp.start()
            sent.append(cp)
    for e in range(1, 4):
        for o, (out, dims) in enumerate(orders):
            d1, d2, d3 = dims
            second[o][e - 1].wait_recv()
            slot = out.at[spot[d3], (spot[d2] + 4 - e) % 4]
            for d in range(1, 4):
                cp = remote(slot, slot, s3.at[o * 16 + e * 4 + d], r3.at[o * 16 + e * 4 + d], peer(d3, d))
                cp.start()
                sent.append(cp)
    for o, (out, dims) in enumerate(orders):
        d1, d2, d3 = dims
        for e in range(4):
            for d in range(1, 4):
                slot = out.at[(spot[d3] + 4 - d) % 4, (spot[d2] + 4 - e) % 4]
                remote(slot, slot, s3.at[o * 16 + e * 4 + d], r3.at[o * 16 + e * 4 + d], peer(d3, d)).wait_recv()
    for cp in sent:
        cp.wait_send()
    swap.wait_send()
    xs.wait()
    ms.wait()


def share(tile, x, m):
    vmem = pl.BlockSpec(memory_space=pltpu.VMEM)
    hbm = pl.BlockSpec(memory_space=pl.ANY)
    dma = pltpu.SemaphoreType.DMA
    rows, lanes = 2 * tile.shape[0], tile.shape[1] // 2
    table = jax.ShapeDtypeStruct((4, 4, 4, rows // 3, lanes), jnp.bfloat16)
    return pl.pallas_call(
        share_kernel,
        out_shape=(
            table, table, table,
            jax.ShapeDtypeStruct(x.shape, x.dtype),
            jax.ShapeDtypeStruct(m.shape, m.dtype),
        ),
        in_specs=[vmem, hbm, vmem],
        out_specs=(hbm,) * 5,
        scratch_shapes=[
            pltpu.VMEM((rows, lanes), jnp.bfloat16),
            dma((3,)), dma((3,)), dma((1,)),
            dma((12,)), dma((12,)), dma((3,)),
            dma((12,)), dma((12,)),
            dma((48,)), dma((48,)),
        ],
        compiler_params=pltpu.CompilerParams(collective_id=3, has_side_effects=True),
        name="share",
    )(tile, x, m)


LOG2E = 1.4426950408889634


def attn_kernel(x0_ref, x1_ref, mb_ref, hm_ref, ta_ref, tb_ref, tc_ref, wq_ref, wk_ref, wv_ref, wg_ref, o_ref,
                q_s, kt_s, v_s, bf_s, acc_s, out_s, send, recv):
    blk = pl.program_id(0)
    r, c = place()
    chip, core = r // 2, r % 2
    half = x0_ref.shape[0]
    seqs, rows = acc_s.shape[0], acc_s.shape[1]
    heads = hm_ref.shape[0]
    cols = o_ref.shape[2]
    scale = float(HEAD_DIM) ** -0.5

    @pl.when(blk == 0)
    def _():
        barrier = pltpu.get_barrier_semaphore()
        for j in range(8):
            for k in range(2):
                if j == 0:

                    @pl.when(core != k)
                    def _():
                        signal(barrier, (chip * 2 + k, c))
                else:
                    signal(barrier, (chip * 2 + k, (c + j) % 8))
        pl.semaphore_wait(barrier, 15)
        for n, x_ref in enumerate((x0_ref, x1_ref)):

            def project(b, carry):
                x = x_ref[b]
                at = n * half + b
                q_s[at] = jnp.dot(x, wq_ref[...], preferred_element_type=jnp.float32).astype(jnp.bfloat16)
                v_s[at] = jnp.dot(x, wv_ref[...], preferred_element_type=jnp.float32).astype(jnp.bfloat16)
                kt_s[at] = lax.dot_general(
                    wk_ref[...], x, LAST_LAST, preferred_element_type=jnp.float32
                ).astype(jnp.bfloat16)
                return carry

            lax.fori_loop(0, half, project, 0)

    at = pl.multiple_of(blk * rows, rows)

    def assemble(n, carry):
        y = blk * 2 + n // 2
        zh = n % 2
        for o in range(3):
            pieces = []
            for cc in range(8):
                x, z = cc // 2, zh * 2 + cc % 2
                if o == 0:
                    piece = ta_ref[y, z, x]
                elif o == 1:
                    piece = tb_ref[z, x, y]
                else:
                    piece = tc_ref[x, y, z]
                pieces.append(piece.astype(jnp.float32) * (1.0 / scale))
            for h in range(heads):
                bf_s[h, pl.ds(pl.multiple_of(n * cols + o * 32, 32), 32), :] = jnp.concatenate(
                    [p[:, h * cols : (h + 1) * cols] for p in pieces], axis=1
                )
        return carry

    lax.fori_loop(0, rows // cols, assemble, 0)

    def one_head(h, carry):
        own = hm_ref[h]
        own_f = own.astype(jnp.float32)
        other = (1.0 - own_f).astype(jnp.bfloat16)

        def one_seq(b, carry):
            q = q_s[b, pl.ds(at, rows), :] * own
            s = jnp.dot(q, kt_s[b], preferred_element_type=jnp.float32) + bf_s[h] + mb_ref[b]
            top = jnp.max(s, axis=1, keepdims=True)
            p = jnp.exp2(((s - top) * (scale * LOG2E)).astype(jnp.bfloat16))
            w = jnp.dot(p, v_s[b] * own + other, preferred_element_type=jnp.float32)
            mixed = w / pltpu.roll(w, HEAD_DIM, 1)
            acc_s[b] = jnp.where(own_f > 0.0, mixed, acc_s[b])
            return carry

        return lax.fori_loop(0, seqs, one_seq, carry, unroll=4)

    lax.fori_loop(0, heads, one_head, 0)

    for n, x_ref in enumerate((x0_ref, x1_ref)):

        def gate(b, carry):
            g = jnp.dot(x_ref[b, pl.ds(at, rows), :], wg_ref[...], preferred_element_type=jnp.float32)
            g = g.astype(jnp.bfloat16).astype(jnp.float32)
            gated = (acc_s[n * half + b] * jax.nn.sigmoid(g)).astype(jnp.bfloat16)
            for t in range(rows // cols):
                out_s[blk, t, n * half + b] = gated[t * cols : (t + 1) * cols]
            return carry

        lax.fori_loop(0, half, gate, 0)

    def message(n, k, t):
        cd = blk * (rows // cols) + t
        dst = o_ref.at[core, pl.ds(pl.multiple_of(c * half, half), half)]
        src = out_s.at[blk, t, pl.ds(n * half, half)]
        cp = remote(src, dst, send.at[(cd * 2 + n)], recv.at[c * 2 + core], (chip * 2 + k, cd))
        return cp, src, dst, cd

    for t in range(rows // cols):
        for n in range(2):
            k = core if n == 0 else 1 - core
            cp, src, dst, cd = message(n, k, t)
            if n == 0:

                @pl.when(cd != c)
                def _():
                    cp.start()

                @pl.when(cd == c)
                def _():
                    pltpu.make_async_copy(src, dst, recv.at[c * 2 + core]).start()
            else:
                cp.start()

    @pl.when(blk == pl.num_programs(0) - 1)
    def _():
        for cs in range(8):
            for k in range(2):
                pltpu.make_async_copy(
                    out_s.at[0, 0, pl.ds(0, half)], o_ref.at[k, pl.ds(cs * half, half)], recv.at[cs * 2 + k]
                ).wait()
        for cd in range(8):
            for n in range(2):
                k = core if n == 0 else 1 - core
                cp = remote(
                    out_s.at[0, 0, pl.ds(0, half)], o_ref.at[core, pl.ds(0, half)],
                    send.at[cd * 2 + n], recv.at[0], (chip * 2 + 1 - core, cd),
                )
                if n == 0:

                    @pl.when(cd != c)
                    def _():
                        cp.wait_send()
                else:
                    cp.wait_send()


def attention(x0, x1, mask, tables, w, cols, home):
    half, length, channels = x0.shape
    seqs = 2 * half
    lanes = w[0].shape[1]
    heads = lanes // HEAD_DIM
    rows = length // 2
    scale = float(HEAD_DIM) ** -0.5
    mb = (1e9 / scale) * (mask.astype(jnp.float32) - 1.0)[:, None, :]
    hm = (jnp.arange(lanes)[None, None, :] // HEAD_DIM == jnp.arange(heads)[:, None, None]).astype(jnp.bfloat16)
    wq, wk, wv, wg = w
    whole = lambda a: pl.BlockSpec(a.shape, lambda i: (0,) * a.ndim, pipeline_mode=pl.Buffered(1))
    operands = (x0, x1, mb, hm, *tables, wq, wk.T, wv, wg)
    dma = pltpu.SemaphoreType.DMA
    return pl.pallas_call(
        attn_kernel,
        grid=(length // rows,),
        out_shape=jax.ShapeDtypeStruct((2, home, cols, lanes), jnp.bfloat16),
        in_specs=[whole(a) for a in operands],
        out_specs=pl.BlockSpec(memory_space=pl.ANY),
        scratch_shapes=[
            pltpu.VMEM((seqs, length, lanes), jnp.bfloat16),
            pltpu.VMEM((seqs, lanes, length), jnp.bfloat16),
            pltpu.VMEM((seqs, length, lanes), jnp.bfloat16),
            pltpu.VMEM((heads, rows, length), jnp.float32),
            pltpu.VMEM((seqs, rows, lanes), jnp.float32),
            pltpu.VMEM((2, rows // cols, seqs, cols, lanes), jnp.bfloat16),
            dma((16,)), dma((16,)),
        ],
        compiler_params=pltpu.CompilerParams(
            vmem_limit_bytes=56 << 20, collective_id=4, has_side_effects=True
        ),
        name="attn",
    )(*operands)


def opm_kernel(left_ref, lmask_ref, right_ref, rrow_ref, rcol_ref, pair_ref, gain_ref, w_ref, wd_ref, x_ref, mk_ref,
               out_ref, bias_ref, x_out, m_out, rt_s, wb_s, m_s, f_s, b_s, xsend, xrecv, msend, mrecv):
    step = pl.program_id(0)
    r, c = place()
    opm = w_ref.shape[0]
    per, cols = out_ref.shape[0], out_ref.shape[1]
    steps = f_s.shape[0]
    heads = wd_ref.shape[0]
    group = per // 4
    chunk = 4 * cols
    half = x_out.shape[0]
    width = cols * opm
    here = pl.ds(pl.multiple_of(c * cols, cols), cols)

    def moves(d):
        to = (r, (c + d) % 8)
        block = pl.ds(pl.multiple_of(to[1] * half, half), half)
        return (
            remote(x_ref.at[block], x_out.at[:, here], xsend.at[d], xrecv.at[d], to),
            remote(mk_ref.at[to[1]], m_out.at[c], msend.at[d], mrecv.at[d], to),
        )

    def kept():
        return (
            pltpu.make_async_copy(
                x_ref.at[pl.ds(pl.multiple_of(c * half, half), half)], x_out.at[:, here], xrecv.at[0]
            ),
            pltpu.make_async_copy(mk_ref.at[c], m_out.at[c], mrecv.at[0]),
        )

    @pl.when(step == 0)
    def _():
        barrier = pltpu.get_barrier_semaphore()
        for d in range(1, 8):
            signal(barrier, (r, (c + d) % 8))
        pl.semaphore_wait(barrier, 7)
        for d in range(1, 8):
            for cp in moves(d):
                cp.start()
        for cp in kept():
            cp.start()
        wb_s[...] = jnp.zeros_like(wb_s)

        def fill(b, carry):
            for i in range(4):
                wb_s[pl.ds(pl.multiple_of(b * 128 + i * 32, 32), 32), i * 128 : (i + 1) * 128] = w_ref[b]
            return carry

        lax.fori_loop(0, opm, fill, 0)

        def flip(n, carry):
            at = pl.multiple_of(n * chunk, chunk)
            rt_s[pl.ds(at, chunk), :] = right_ref[:, pl.ds(at, chunk)].T
            return carry

        lax.fori_loop(0, opm // 4, flip, 0)
        counts = lax.dot_general(
            right_ref[:, width:], lmask_ref[...], CONTRACT_FIRST, preferred_element_type=jnp.float32
        )[:cols, : steps * per]
        factor = rcol_ref[...] * rrow_ref[...] / (counts + 0.001)
        for n in range(steps):
            f_s[n] = factor[:, n * per : (n + 1) * per]

    def outer(n, carry):
        at = pl.multiple_of(n * chunk, chunk)
        m = jnp.dot(rt_s[pl.ds(at, chunk), :], left_ref[...], preferred_element_type=jnp.float32)
        m = m.astype(jnp.bfloat16)
        for bb in range(4):
            for g in range(group):
                m_s[g * cols : (g + 1) * cols, pl.ds(pl.multiple_of((n * 4 + bb) * 128, 128), 128)] = m[
                    bb * cols : (bb + 1) * cols, g * 128 : (g + 1) * 128
                ]
        return carry

    lax.fori_loop(0, opm // 4, outer, 0)
    factor = f_s[step]
    update = jnp.dot(m_s[...], wb_s[...], preferred_element_type=jnp.float32)
    for g in range(group):
        for ii in range(4):
            i = 4 * g + ii
            u = update[g * cols : (g + 1) * cols, ii * 128 : (ii + 1) * 128]
            x = pair_ref[i] + u * factor[:, i : i + 1]
            out_ref[i] = x
            x = (standardize_features(x) * gain_ref[...]).astype(jnp.bfloat16)
            b_s[:, i, :] = lax.dot_general(wd_ref[...], x, LAST_LAST, preferred_element_type=jnp.float32)
    bias_ref[...] = jnp.concatenate([b_s[h] for h in range(heads)], axis=1).astype(jnp.bfloat16)

    @pl.when(step == steps - 1)
    def _():
        for d in range(1, 8):
            for cp in moves(d):
                cp.wait()
        for cp in kept():
            cp.wait()


def opm(left, right, rrow, rcol, pair, gain, kron, logit, x, mk):
    rows, cols, channels = pair.shape
    seqs = left.shape[0]
    heads = logit.shape[1]
    per = 16
    steps = rows // per
    width = kron.shape[0] // 32
    rr = rrow.reshape(1, rows)
    rc = rcol.reshape(cols, 1)
    w = kron.reshape(width, width, channels).transpose(1, 0, 2)
    gain = gain.reshape(1, channels)
    wd = logit.T
    whole = lambda a: pl.BlockSpec(a.shape, lambda i: (0,) * a.ndim, pipeline_mode=pl.Buffered(1))
    hbm = pl.BlockSpec(memory_space=pl.ANY)
    dma = pltpu.SemaphoreType.DMA
    return pl.pallas_call(
        opm_kernel,
        grid=(steps,),
        out_shape=(
            jax.ShapeDtypeStruct(pair.shape, jnp.float32),
            jax.ShapeDtypeStruct((rows, heads * cols), jnp.bfloat16),
            jax.ShapeDtypeStruct((x.shape[0] // 8, 8 * cols, x.shape[2]), jnp.bfloat16),
            jax.ShapeDtypeStruct(mk.shape, mk.dtype),
        ),
        in_specs=[
            pl.BlockSpec((seqs, per * width), lambda i: (0, i)),
            pl.BlockSpec((seqs, 128), lambda i: (0, rows * width // 128)),
            whole(right), whole(rr), whole(rc),
            pl.BlockSpec((per, cols, channels), lambda i: (i, 0, 0)),
            whole(gain), whole(w), whole(wd), whole(x), whole(mk),
        ],
        out_specs=(
            pl.BlockSpec((per, cols, channels), lambda i: (i, 0, 0)),
            pl.BlockSpec((per, heads * cols), lambda i: (i, 0)),
            hbm, hbm,
        ),
        scratch_shapes=[
            pltpu.VMEM((cols * width, seqs), jnp.bfloat16),
            pltpu.VMEM((128 * width, 4 * channels), jnp.bfloat16),
            pltpu.VMEM((per // 4 * cols, 128 * width), jnp.bfloat16),
            pltpu.VMEM((steps, cols, per), jnp.float32),
            pltpu.VMEM((heads, per, cols), jnp.float32),
            dma((8,)), dma((8,)), dma((8,)), dma((8,)),
        ],
        compiler_params=pltpu.CompilerParams(
            vmem_limit_bytes=52 << 20, collective_id=2, has_side_effects=True
        ),
        name="opm",
    )(left, left, right, rr, rc, pair, gain, w, wd, x, mk)


def shards(
    aligned_family_embedding,
    aligned_slot_available,
    chain_site_available,
    duo_embedding,
    averaging_layernorm_stretch,
    lineup_layernorm_stretch,
    duo_layernorm_stretch,
    lefthand_linear_kernel,
    righthand_linear_kernel,
    kronecker_linear_kernel,
    duo_logit_kernel,
    asker_lookup_sigmoid_kernel,
    closing_linear_kernel,
):
    homolog_number, amino_position_number, discarded_carry = aligned_family_embedding.shape
    res_rows = duo_embedding.shape[0]
    opm_width = lefthand_linear_kernel.shape[1]
    head_count = duo_logit_kernel.shape[1]
    inner_width = closing_linear_kernel.shape[0]
    row_index = lax.axis_index("row")
    col_index = lax.axis_index("col")
    standardized_features = standardize_features(aligned_family_embedding.astype(jnp.float32))
    availability_real = aligned_slot_available.astype(jnp.float32)
    half_rows = res_rows
    opm_input = (standardized_features * averaging_layernorm_stretch).astype(jnp.bfloat16)
    left = jnp.einsum("src,ca->sra", opm_input, lefthand_linear_kernel, preferred_element_type=jnp.float32)
    left = (left * availability_real[:, :, None]).astype(jnp.bfloat16)
    left = left.reshape(homolog_number, 2, half_rows * opm_width).transpose(1, 0, 2)
    left_mask = availability_real.reshape(homolog_number, 2, half_rows).transpose(1, 0, 2)
    left_mask = jnp.pad(left_mask, ((0, 0), (0, 0), (0, 128 - half_rows))).astype(jnp.bfloat16)
    left = jnp.concatenate([left, left_mask], axis=2)
    right = jnp.einsum("src,ca->sar", opm_input, righthand_linear_kernel, preferred_element_type=jnp.float32)
    right = (right * availability_real[:, None, :]).astype(jnp.bfloat16)
    right_mask = jnp.pad(availability_real, ((0, 0), (0, 128 - amino_position_number))).astype(jnp.bfloat16)
    right = jnp.concatenate([right.reshape(homolog_number, -1), right_mask], axis=1)
    exponential_probabilities = (standardized_features * lineup_layernorm_stretch).astype(jnp.bfloat16)
    mask_out = jnp.pad(
        availability_real.reshape(8, homolog_number // 8, amino_position_number),
        ((0, 0), (0, 8 - homolog_number // 8), (0, 128 - amino_position_number)),
    )
    left_all, right_all = spread(left, right)
    residue_float = chain_site_available.astype(jnp.float32)
    residue_rows = lax.dynamic_slice_in_dim(residue_float, row_index * res_rows, res_rows)
    residue_cols = lax.dynamic_slice_in_dim(
        residue_float, col_index * amino_position_number, amino_position_number
    )
    duo_after_averaging, bias_tile, own_rows, own_mask = opm(
        left_all, right_all, residue_rows, residue_cols, duo_embedding,
        duo_layernorm_stretch, kronecker_linear_kernel, duo_logit_kernel, exponential_probabilities, mask_out,
    )
    *tables, other_rows, other_mask = share(bias_tile, own_rows, own_mask)
    masks = jnp.concatenate([own_mask, other_mask], axis=1).reshape(8, 2, 8, 128)
    masks = masks[:, :, : homolog_number // 8, :amino_position_number].transpose(1, 2, 0, 3)
    masks = masks.reshape(homolog_number // 4, 8 * amino_position_number)
    lanes = inner_width // 2
    by_half = asker_lookup_sigmoid_kernel.reshape(-1, 4, 2, lanes)
    mine = lax.dynamic_index_in_dim(by_half, row_index % 2, 2, keepdims=False)
    gated = attention(
        own_rows, other_rows, masks, tables, [mine[:, n] for n in range(4)], amino_position_number, homolog_number
    )
    closing = closing_linear_kernel.reshape(2, lanes, -1)
    summed_increment = jnp.einsum("hsqd,hdc->sqc", gated, closing, preferred_element_type=jnp.float32)
    refreshed_family_embedding = (
        aligned_family_embedding.astype(jnp.float32) + summed_increment
    ).astype(jnp.bfloat16)
    return (refreshed_family_embedding, duo_after_averaging)


def solution(mesh):
    placed = (
        P("row", "col", None),
        P("row", "col"),
        P(),
        P("row", "col", None),
        P(),
        P(),
        P(),
        P(),
        P(),
        P(),
        P(),
        P(),
        P(),
    )
    return jax.shard_map(
        shards,
        mesh=mesh,
        in_specs=placed,
        out_specs=(P("row", "col", None), P("row", "col", None)),
        check_vma=False,
    )
```

time: 388 us -> 236 us (0.61)
  waiting for transfers between devices: 157 us -> 0 us
  Pallas kernels: 98 us -> 208 us
  blocking collectives: 38.8 us -> 0 us
  local copies, waits for them, and re-layouts: 46.9 us -> 9.4 us
  starting transfers between devices: 19.1 us -> 0 us
  between operations: 14.2 us -> 0.96 us
    all_gather x3 -> x0, waiting for transfers between devices: 125 us -> none  [the longest x1 44.2 us: shards(): bias_whole = lax.all_gather(bias_cols, 'row', axis=1, tiled=True)]
    pallas_call x0 -> x2, Pallas kernels: none -> 110 us  [the longest x1 68.1 us: spread(): pl.pallas_call(spread_kernel, out_shape=(jax.ShapeDtypeStruct((16 * seqs,...]
    all_to_all x2 -> x0, blocking collectives: 38.8 us -> none  [the longest x1 23.8 us: shards(): lax.all_to_all(gated_whole, 'col', split_axis=1, concat_axis=0, tiled=True)]
    all_to_all x3 -> x0, waiting for transfers between devices: 31.5 us -> none  [the longest x1 29.9 us: sent_together(): lax.all_to_all(both, axis, split_axis=split_dim, concat_axis=concat_dim,...]
    all_to_all x3 -> x0, starting transfers between devices: 19 us -> none  [the longest x1 8.78 us: shards(): lax.all_to_all(mask_wide, 'row', split_axis=1, concat_axis=0, tiled=True)]
    all_to_all x9 -> x0, local copies, waits for them, and re-layouts: 13.1 us -> none  [the longest x2 7.34 us: sent_together(): lax.all_to_all(both, axis, split_axis=split_dim, concat_axis=concat_dim,...]
    slice x6 -> x1, local copies, waits for them, and re-layouts: 12.3 us -> 0.01 us  [shards(): masks[:, :, :homolog_number // 8, :amino_position_number]]
    pallas_call x1, Pallas kernels: 21 us -> 28.8 us  [opm(): pl.pallas_call(opm_kernel, grid=(steps,), out_shape=(jax.ShapeDtypeStruct...]
  transfers between devices with their start and end apart: 6 -> 0, of which waited for: 5 -> 0; matrix products, arithmetic and copies ran while one was open for 8% -> 0% of each run, Pallas kernels for 0% -> 0%
where the time goes in v2:
time: 236 us; the launch traced here: 234 us
  Pallas kernels  208 us (88%)
  other arithmetic  9.8 us (4%)
  local copies, waits for them, and re-layouts  9.4 us (4%)
  matrix products  5.82 us (2%)
    pallas_call x1, Pallas kernels, attention(): pl.pallas_call(attn_kernel, grid=(length // rows,), out_shape=jax.ShapeDt...  69.2 us
    pallas_call x1, Pallas kernels, spread(): pl.pallas_call(spread_kernel, out_shape=(jax.ShapeDtypeStruct((16 * seqs,...  68.1 us
    pallas_call x1, Pallas kernels, share(): pl.pallas_call(share_kernel, out_shape=(table, table, table, jax.ShapeDty...  41.6 us
    pallas_call x1, Pallas kernels, opm(): pl.pallas_call(opm_kernel, grid=(steps,), out_shape=(jax.ShapeDtypeStruct...  28.8 us

profile of v2, /device:TPU:1, one launch (start us, length us, event | category | flops | bytes accessed | tf_op | source)
XLA Modules:
  0.0 233.8 jit_solution(13684132724904087418)
XLA Ops:
  0.6 0.0 copy-start
  0.6 0.0 copy-start.5
  0.7 0.0 copy-start.12
  0.7 0.0 copy-start.10
  0.7 0.0 copy-start.8
  0.7 0.8 copy-done
  1.5 0.6 compare_convert_fusion.hm_ref
  2.1 0.7 convert_element_type.45
  2.8 0.1 dynamic-slice_bitcast_fusion
  2.9 0.1 dynamic-slice_bitcast_fusion.1.rrow_ref
  3.0 2.0 convert_reduce_fusion
  5.0 0.0 copy-start.11
  5.0 2.5 %fusion.6 = f32[32,96]{1,0:T(8,128)S(1)} fusion(bf16[32,96,256]{2,1,0:T(8,128)(2,1)} %param.13, f32[32,96]{1,0:T(8,128)S(1)} %broadcast_multiply_fusion), kind=kLoop, calls=%fused_computation.9 | loop fusion | flops 3142656 | bytes 1597440 | tf_op jit(solution)/shard_map/reduce_sum | solution.py:17
  7.5 0.0 copy-done.8
  7.5 0.1 reshape.147
  7.6 0.1 copy.25.rcol_ref
  7.7 0.0 copy-done.5
  7.7 0.0 copy-done.12
  7.8 1.3 fusion.10
  9.0 0.0 copy-start.7
  9.1 0.3 reshape.148
  9.4 0.7 fusion.16.right_ref
  10.1 1.3 fusion.8
  11.4 0.0 copy-done.7
  11.4 0.1 copy.44
  11.5 0.0 copy-start.9
  11.5 0.4 copy.21
  11.9 0.6 reshape.146
  12.5 0.7 fusion.15.left_ref
  13.2 1.4 reshape.155
  14.6 0.0 copy-start.3
  14.6 0.0 copy-start.4
  14.6 0.5 constant_dynamic-slice_fusion
  15.2 0.7 slice_bitcast_fusion
  15.9 0.7 copy.28.wk_ref
  16.6 1.8 fusion.5.x_ref
  18.5 68.1 %spread.1 = (bf16[512,1664]{1,0:T(8,128)(2,1)}, bf16[512,3200]{1,0:T(8,128)(2,1)}) custom-call(bf16[2,32,1664]{2,1,0:T(8,128)(2,1)} %fusion.15.left_ref, bf16[32,3200]{1,0:T(8,128)(2,1)} %fusion.16.right_ref), custom_call_target="tpu_custom_call" | custom-call | tf_op jit(solution)/shard_map/spread/pallas_call | solution.py:117
  86.6 28.8 %opm.1 = (f32[48,96,128]{2,1,0:T(8,128)}, bf16[48,768]{1,0:T(8,128)(2,1)S(1)}, bf16[4,768,256]{2,1,0:T(8,128)(2,1)}, f32[8,8,128]{2,1,0:T(8,128)S(1)}) custom-call(bf16[512,1664]{1,0:T(8,128)(2,1)} %get-tuple-element.13.left_ref.lmask_ref, bf16[512,1664]{1,0:T(8,128)(2,1)} %get-tuple-element.13.left_ref.lmask_ref, ...), custom_call_target="tpu_custom_call" | custom-call | tf_op jit(solution)/shard_map/opm/pallas_call | solution.py:538
  115.4 0.0 copy-start.1
  115.5 0.6 copy-done.1
  116.1 0.6 copy-done.2
  116.7 41.6 %share.1 = (bf16[4,4,4,32,384]{4,3,2,1,0:T(8,128)(2,1)}, bf16[4,4,4,32,384]{4,3,2,1,0:T(8,128)(2,1)}, bf16[4,4,4,32,384]{4,3,2,1,0:T(8,128)(2,1)}, bf16[4,768,256]{2,1,0:T(8,128)(2,1)}, f32[8,8,128]{2,1,0:T(8,128)}) custom-call(bf16[48,768]{1,0:T(8,128)(2,1)} %copy-done.2, bf16[4,768,256]{2,1,0:T(8,128)(2,1)} %get-tuple-element.15.x_ref.x0_ref, ...), custom_call_target="tpu_custom_call" | custom-call | tf_op jit(solution)/shard_map/share/pallas_call | solution.py:229
  158.3 0.8 maximum_bitcast_fusion
  159.1 0.7 mul.73.mb_ref
  159.8 69.2 %attn.1 = bf16[2,32,96,128]{3,2,1,0:T(8,128)(2,1)} custom-call(bf16[4,768,256]{2,1,0:T(8,128)(2,1)} %get-tuple-element.15.x_ref.x0_ref, bf16[4,768,256]{2,1,0:T(8,128)(2,1)} %get-tuple-element.18.x1_ref, f32[8,1,768]{2,1,0:T(1,128)} %mul.73.mb_ref, bf16[4,1,128]{2,1,0:T(2,128)(2,1)} %compare_convert_fusion.hm_ref, ...), custom_call_target="tpu_custom_call" | custom-call | tf_op jit(solution)/shard_map/attn/pallas_call | solution.py:405
  229.1 0.0 copy-start.6
  229.1 3.3 %fusion.7 = bf16[32,96,256]{2,1,0:T(8,128)(2,1)} fusion(bf16[32,96,256]{2,1,0:T(8,128)(2,1)S(1)} %copy-done.5, bf16[2,32,96,128]{3,2,1,0:T(8,128)(2,1)} %attn.1, bf16[2,128,256,1]{2,1,3,0:T(8,128)(2,1)S(1)} %bitcast.53), kind=kOutput, calls=%fused_computation.10 | convolution fusion | flops 405012480 | bytes 4849664 | tf_op jit(solution)/shard_map/hsqd,hdc->sqc/dot_general | solution.py:636
  232.4 1.4 copy.48
  (17 shorter events, 0.1 us)
Async XLA Ops:
  0.6 0.9 copy-start
  0.6 7.1 %copy-start.5 = (bf16[32,96,256]{2,1,0:T(8,128)(2,1)S(1)}, bf16[32,96,256]{2,1,0:T(8,128)(2,1)}, u32[]{:S(2)}) copy-start(bf16[32,96,256]{2,1,0:T(8,128)(2,1)} %param.13) | copy-start | bytes 4718596
  0.7 7.1 %copy-start.12 = (f32[256]{0:T(256)S(1)}, f32[256]{0:T(256)}, u32[]{:S(2)}) copy-start(f32[256]{0:T(256)} %param.17) | copy-start | bytes 3076
  0.7 7.1 %copy-start.10 = (bf16[256,32]{0,1:T(8,128)(2,1)S(1)}, bf16[256,32]{0,1:T(8,128)(2,1)}, u32[]{:S(2)}) copy-start(bf16[256,32]{0,1:T(8,128)(2,1)} %param.21) | copy-start | bytes 49156
  0.7 6.8 %copy-start.8 = (s32[32,96]{1,0:T(8,128)S(1)}, s32[32,96]{1,0:T(8,128)}, u32[]{:S(2)}) copy-start(s32[32,96]{1,0:T(8,128)} %param.14) | copy-start | bytes 36868
  5.0 5.1 %copy-start.11 = (bf16[256,32]{0,1:T(8,128)(2,1)S(1)}, bf16[256,32]{0,1:T(8,128)(2,1)}, u32[]{:S(2)}) copy-start(bf16[256,32]{0,1:T(8,128)(2,1)} %param.20) | copy-start | bytes 49156
  9.0 2.3 copy-start.7
  11.5 5.1 %copy-start.9 = (f32[256]{0:T(256)S(1)}, f32[256]{0:T(256)}, u32[]{:S(2)}) copy-start(f32[256]{0:T(256)} %param.18) | copy-start | bytes 3076
  14.6 72.0 %copy-start.3 = (bf16[128,8]{0,1:T(8,128)(2,1)S(1)}, bf16[128,8]{0,1:T(8,128)(2,1)}, u32[]{:S(2)}) copy-start(bf16[128,8]{0,1:T(8,128)(2,1)} %param.23) | copy-start | bytes 6148
  14.6 72.0 %copy-start.4 = (f32[128]{0:T(128)S(1)}, f32[128]{0:T(128)}, u32[]{:S(2)}) copy-start(f32[128]{0:T(128)} %param.19) | copy-start | bytes 1540
  115.4 0.6 copy-start.1
  116.1 0.6 copy-start.2
  229.1 3.3 %copy-start.6 = (f32[48,96,128]{2,1,0:T(8,128)S(1)}, f32[48,96,128]{2,1,0:T(8,128)}, u32[]{:S(2)}) copy-start(f32[48,96,128]{2,1,0:T(8,128)} %get-tuple-element.33) | copy-start | bytes 7077892

commit v3 on v2

--- a/solution.py
+++ b/solution.py
@@ -128,300 +128,291 @@
     )(left, right)
 
 
-def share_kernel(tile_ref, x_ref, m_ref, a_out, b_out, c_out, x_out, m_out, block,
-                 csend, crecv, csem, s1, r1, l1, s2, r2, s3, r3):
+LOG2E = 1.4426950408889634
+
+
+def attn_kernel(tile_ref, xin_ref, mask_ref, hm_ref, wq_ref, wk_ref, wv_ref, wg_ref, o_ref,
+                block, ta, tb, tc, x_s, m_s, mb_s, q_s, kt_s, v_s, g_s, bf_s, acc_s, out_s,
+                csem, csend, crecv, l1, s1, r1, s2, r2, s3, r3, send, recv):
     r, c = place()
-    spot = {"x": c // 2, "y": r // 4, "z": ((r // 2) % 2) * 2 + c % 2}
-    core = r % 2
+    chip, core = r // 2, r % 2
+    spot = {"x": c // 2, "y": r // 4, "z": (chip % 2) * 2 + c % 2}
+    half, length = x_s.shape[1], x_s.shape[2]
+    heads, rows = bf_s.shape[0], bf_s.shape[1]
+    cols = length // 8
+    sub = cols // 6
+    scale = float(HEAD_DIM) ** -0.5
+    partner = (chip * 2 + 1 - core, c)
+    orders = ((ta, "xzy"), (tb, "yxz"), (tc, "zyx"))
 
     def peer(dim, d):
         to = dict(spot)
         to[dim] = (spot[dim] + d) % 4
         return (row_of(to["y"], to["z"] // 2, core), to["x"] * 2 + to["z"] % 2)
 
-    partner = ((r // 2) * 2 + 1 - core, c)
     barrier = pltpu.get_barrier_semaphore()
     signal(barrier, partner)
     for dim in "xyz":
         for d in range(1, 4):
             signal(barrier, peer(dim, d))
-    pl.semaphore_wait(barrier, 10)
-
-    rows, lanes = tile_ref.shape[0], tile_ref.shape[1] // 2
-    here = pl.ds(pl.multiple_of(core * rows, rows), rows)
+    for j in range(8):
+        if j > 0:
+            signal(barrier, (r, (c + j) % 8))
+        signal(barrier, (partner[0], (c + j) % 8))
+
+    trows, lanes = tile_ref.shape[0], tile_ref.shape[1] // 2
+    here = pl.ds(pl.multiple_of(core * trows, trows), trows)
     give = tile_ref.at[:, pl.ds(pl.multiple_of((1 - core) * lanes, lanes), lanes)]
     keep = tile_ref.at[:, pl.ds(pl.multiple_of(core * lanes, lanes), lanes)]
+    own = pltpu.make_async_copy(keep, block.at[here], csem.at[0])
+    own.start()
+    xl = pltpu.make_async_copy(xin_ref, x_s.at[0], csem.at[1])
+    xl.start()
+    ml = pltpu.make_async_copy(mask_ref, m_s.at[0], csem.at[2])
+    ml.start()
+    pl.semaphore_wait(barrier, 25)
     swap = remote(give, block.at[here], csend.at[0], crecv.at[0], partner)
     swap.start()
-    own = pltpu.make_async_copy(keep, block.at[here], csem.at[0])
-    own.start()
-    xs = remote(x_ref, x_out, csend.at[1], crecv.at[1], partner)
-    ms = remote(m_ref, m_out, csend.at[2], crecv.at[2], partner)
+    xs = remote(xin_ref, x_s.at[1], csend.at[1], crecv.at[1], partner)
+    ms = remote(mask_ref, m_s.at[1], csend.at[2], crecv.at[2], partner)
     own.wait()
     swap.wait_recv()
 
-    orders = ((a_out, "xzy"), (b_out, "yxz"), (c_out, "zyx"))
-    part = block.shape[0] // 3
-    sent = []
-    first = []
-    for o, (out, dims) in enumerate(orders):
-        d1, d2, d3 = dims
-        slot = out.at[spot[d3], spot[d2], spot[d1]]
-        piece = block.at[pl.ds(o * part, part)]
-        mine = pltpu.make_async_copy(piece, slot, l1.at[o])
-        mine.start()
-        cps = []
-        for d in range(1, 4):
-            cp = remote(piece, slot, s1.at[o * 4 + d], r1.at[o * 4 + d], peer(d1, d))
-            cp.start()
-            cps.append(cp)
-        first.append((mine, cps))
-        sent += cps
+    def one(hf, o, d):
+        out, dims = orders[o]
+        slot = out.at[hf, spot[dims[2]], spot[dims[1]], spot[dims[0]]]
+        piece = block.at[pl.ds(o * 2 * sub + hf * sub, sub)]
+        if d == 0:
+            return pltpu.make_async_copy(piece, slot, l1.at[hf * 3 + o])
+        at = (hf * 3 + o) * 4 + d
+        return remote(piece, slot, s1.at[at], r1.at[at], peer(dims[0], d))
+
+    def two(hf, o, d):
+        out, dims = orders[o]
+        slot = out.at[hf, spot[dims[2]], spot[dims[1]]]
+        at = (hf * 3 + o) * 4 + d
+        return remote(slot, slot, s2.at[at], r2.at[at], peer(dims[1], d))
+
+    def three(hf, o, e, d):
+        out, dims = orders[o]
+        slot = out.at[hf, spot[dims[2]], (spot[dims[1]] + 4 - e) % 4]
+        at = (hf * 3 + o) * 16 + e * 4 + d
+        return remote(slot, slot, s3.at[at], r3.at[at], peer(dims[2], d))
+
+    def middle(hf):
+        for o in range(3):
+            for d in range(4):
+                if d == 0:
+                    one(hf, o, d).wait()
+                else:
+                    one(hf, o, d).wait_recv()
+            for d in range(1, 4):
+                two(hf, o, d).start()
+            for d in range(1, 4):
+                three(hf, o, 0, d).start()
+
+    def last(hf):
+        for e in range(1, 4):
+            for o in range(3):
+                two(hf, o, e).wait_recv()
+                for d in range(1, 4):
+                    three(hf, o, e, d).start()
+
+    for hf in range(2):
+        for o in range(3):
+            for d in range(4):
+                one(hf, o, d).start()
     xs.start()
     ms.start()
-    second = []
-    for o, (out, dims) in enumerate(orders):
-        d1, d2, d3 = dims
-        mine, cps = first[o]
-        mine.wait()
-        for cp in cps:
-            cp.wait_recv()
-        slot = out.at[spot[d3], spot[d2]]
-        cps = []
-        for d in range(1, 4):
-            cp = remote(slot, slot, s2.at[o * 4 + d], r2.at[o * 4 + d], peer(d2, d))
-            cp.start()
-            cps.append(cp)
-        second.append(cps)
-        sent += cps
-        for d in range(1, 4):
-            cp = remote(slot, slot, s3.at[o * 16 + d], r3.at[o * 16 + d], peer(d3, d))
-            cp.start()
-            sent.append(cp)
-    for e in range(1, 4):
-        for o, (out, dims) in enumerate(orders):
-            d1, d2, d3 = dims
-            second[o][e - 1].wait_recv()
-            slot = out.at[spot[d3], (spot[d2] + 4 - e) % 4]
-            for d in range(1, 4):
-                cp = remote(slot, slot, s3.at[o * 16 + e * 4 + d], r3.at[o * 16 + e * 4 + d], peer(d3, d))
-                cp.start()
-                sent.append(cp)
-    for o, (out, dims) in enumerate(orders):
-        d1, d2, d3 = dims
-        for e in range(4):
-            for d in range(1, 4):
-                slot = out.at[(spot[d3] + 4 - d) % 4, (spot[d2] + 4 - e) % 4]
-                remote(slot, slot, s3.at[o * 16 + e * 4 + d], r3.at[o * 16 + e * 4 + d], peer(d3, d)).wait_recv()
-    for cp in sent:
-        cp.wait_send()
-    swap.wait_send()
-    xs.wait()
-    ms.wait()
-
-
-def share(tile, x, m):
-    vmem = pl.BlockSpec(memory_space=pltpu.VMEM)
-    hbm = pl.BlockSpec(memory_space=pl.ANY)
-    dma = pltpu.SemaphoreType.DMA
-    rows, lanes = 2 * tile.shape[0], tile.shape[1] // 2
-    table = jax.ShapeDtypeStruct((4, 4, 4, rows // 3, lanes), jnp.bfloat16)
-    return pl.pallas_call(
-        share_kernel,
-        out_shape=(
-            table, table, table,
-            jax.ShapeDtypeStruct(x.shape, x.dtype),
-            jax.ShapeDtypeStruct(m.shape, m.dtype),
-        ),
-        in_specs=[vmem, hbm, vmem],
-        out_specs=(hbm,) * 5,
-        scratch_shapes=[
-            pltpu.VMEM((rows, lanes), jnp.bfloat16),
-            dma((3,)), dma((3,)), dma((1,)),
-            dma((12,)), dma((12,)), dma((3,)),
-            dma((12,)), dma((12,)),
-            dma((48,)), dma((48,)),
-        ],
-        compiler_params=pltpu.CompilerParams(collective_id=3, has_side_effects=True),
-        name="share",
-    )(tile, x, m)
-
-
-LOG2E = 1.4426950408889634
-
-
-def attn_kernel(x0_ref, x1_ref, mb_ref, hm_ref, ta_ref, tb_ref, tc_ref, wq_ref, wk_ref, wv_ref, wg_ref, o_ref,
-                q_s, kt_s, v_s, bf_s, acc_s, out_s, send, recv):
-    blk = pl.program_id(0)
-    r, c = place()
-    chip, core = r // 2, r % 2
-    half = x0_ref.shape[0]
-    seqs, rows = acc_s.shape[0], acc_s.shape[1]
-    heads = hm_ref.shape[0]
-    cols = o_ref.shape[2]
-    scale = float(HEAD_DIM) ** -0.5
-
-    @pl.when(blk == 0)
-    def _():
-        barrier = pltpu.get_barrier_semaphore()
-        for j in range(8):
-            for k in range(2):
+
+    def project(n):
+        def body(b, carry):
+            x = x_s[n, b]
+            at = n * half + b
+            p = jnp.dot(x, wq_ref[...], preferred_element_type=jnp.float32).astype(jnp.bfloat16)
+            g = jnp.dot(x, wg_ref[...], preferred_element_type=jnp.float32).astype(jnp.bfloat16)
+            for hf in range(2):
+                q_s[at, hf] = jnp.concatenate(
+                    [p[(2 * i + hf) * sub : (2 * i + hf + 1) * sub] for i in range(rows // sub)], axis=0
+                )
+                g_s[at, hf] = jnp.concatenate(
+                    [g[(2 * i + hf) * sub : (2 * i + hf + 1) * sub] for i in range(rows // sub)], axis=0
+                )
+            v_s[at] = jnp.dot(x, wv_ref[...], preferred_element_type=jnp.float32).astype(jnp.bfloat16)
+            kt_s[at] = lax.dot_general(
+                wk_ref[...], x, LAST_LAST, preferred_element_type=jnp.float32
+            ).astype(jnp.bfloat16)
+            return carry
+
+        lax.fori_loop(0, half, body, 0)
+        for b in range(half):
+            line = jnp.concatenate([m_s[n, cc, b : b + 1, :cols] for cc in range(8)], axis=1)
+            mb_s[n * half + b] = (1e9 / scale) * (line - 1.0)
+
+    middle(0)
+    xl.wait()
+    ml.wait()
+    project(0)
+    last(0)
+    middle(1)
+    xs.wait_recv()
+    ms.wait_recv()
+    project(1)
+
+    def block_of_rows(hf, carry):
+        for o in range(3):
+            for e in range(4):
+                for d in range(1, 4):
+                    out, dims = orders[o]
+                    at = (hf * 3 + o) * 16 + e * 4 + d
+                    slot = out.at[hf, (spot[dims[2]] + 4 - d) % 4, (spot[dims[1]] + 4 - e) % 4]
+                    remote(slot, slot, s3.at[at], r3.at[at], peer(dims[2], d)).wait_recv()
+
+        def assemble(p, carry):
+            y, zh = p // 2, p % 2
+            for o in range(3):
+                pieces = []
+                for cc in range(8):
+                    x, z = cc // 2, zh * 2 + cc % 2
+                    if o == 0:
+                        piece = ta[hf, y, z, x]
+                    elif o == 1:
+                        piece = tb[hf, z, x, y]
+                    else:
+                        piece = tc[hf, x, y, z]
+                    pieces.append(piece.astype(jnp.float32) * (1.0 / scale))
+                for h in range(heads):
+                    bf_s[h, pl.ds(pl.multiple_of(p * 3 * sub + o * sub, sub), sub), :] = jnp.concatenate(
+                        [piece[:, h * cols : (h + 1) * cols] for piece in pieces], axis=1
+                    )
+            return carry
+
+        lax.fori_loop(0, 8, assemble, 0)
+
+        def group(n, carry):
+            def one_head(h, carry):
+                @pl.when(jnp.logical_and(hf == 0, jnp.logical_and(n == 0, h == 1)))
+                def _():
+                    last(1)
+
+                mine = hm_ref[h]
+                mine_f = mine.astype(jnp.float32)
+                other = (1.0 - mine_f).astype(jnp.bfloat16)
+                for b in range(half):
+                    at = n * half + b
+                    q = q_s[at, hf] * mine
+                    s = jnp.dot(q, kt_s[at], preferred_element_type=jnp.float32) + bf_s[h] + mb_s[at]
+                    top = jnp.max(s, axis=1, keepdims=True)
+                    p = jnp.exp2(((s - top) * (scale * LOG2E)).astype(jnp.bfloat16))
+                    w = jnp.dot(p, v_s[at] * mine + other, preferred_element_type=jnp.float32)
+                    mixed = w / pltpu.roll(w, HEAD_DIM, 1)
+                    acc_s[b] = jnp.where(mine_f > 0.0, mixed, acc_s[b])
+                return carry
+
+            lax.fori_loop(0, heads, one_head, 0)
+
+            def gate(b, carry):
+                g = g_s[n * half + b, hf].astype(jnp.float32)
+                gated = (acc_s[b] * jax.nn.sigmoid(g)).astype(jnp.bfloat16)
+                for p in range(8):
+                    for o in range(3):
+                        at = (p * 3 + o) * sub
+                        out_s[hf, n, p, b, o] = gated[at : at + sub]
+                return carry
+
+            lax.fori_loop(0, half, gate, 0)
+            for j in range(8):
+                p = (c + j) % 8
+                src = out_s.at[hf, n, p]
+                dst = o_ref.at[core, pl.ds(pl.multiple_of(c * half, half), half), :, hf]
+                arrived = recv.at[hf * 16 + c * 2 + core]
+                row = jnp.where(n == 0, r, partner[0])
+                cp = remote(src, dst, send.at[(hf * 2 + n) * 8 + p], arrived, (row, p))
                 if j == 0:
 
-                    @pl.when(core != k)
+                    @pl.when(n > 0)
                     def _():
-                        signal(barrier, (chip * 2 + k, c))
+                        cp.start()
+
+                    @pl.when(n == 0)
+                    def _():
+                        pltpu.make_async_copy(src, dst, arrived).start()
                 else:
-                    signal(barrier, (chip * 2 + k, (c + j) % 8))
-        pl.semaphore_wait(barrier, 15)
-        for n, x_ref in enumerate((x0_ref, x1_ref)):
-
-            def project(b, carry):
-                x = x_ref[b]
-                at = n * half + b
-                q_s[at] = jnp.dot(x, wq_ref[...], preferred_element_type=jnp.float32).astype(jnp.bfloat16)
-                v_s[at] = jnp.dot(x, wv_ref[...], preferred_element_type=jnp.float32).astype(jnp.bfloat16)
-                kt_s[at] = lax.dot_general(
-                    wk_ref[...], x, LAST_LAST, preferred_element_type=jnp.float32
-                ).astype(jnp.bfloat16)
-                return carry
-
-            lax.fori_loop(0, half, project, 0)
-
-    at = pl.multiple_of(blk * rows, rows)
-
-    def assemble(n, carry):
-        y = blk * 2 + n // 2
-        zh = n % 2
-        for o in range(3):
-            pieces = []
-            for cc in range(8):
-                x, z = cc // 2, zh * 2 + cc % 2
-                if o == 0:
-                    piece = ta_ref[y, z, x]
-                elif o == 1:
-                    piece = tb_ref[z, x, y]
-                else:
-                    piece = tc_ref[x, y, z]
-                pieces.append(piece.astype(jnp.float32) * (1.0 / scale))
-            for h in range(heads):
-                bf_s[h, pl.ds(pl.multiple_of(n * cols + o * 32, 32), 32), :] = jnp.concatenate(
-                    [p[:, h * cols : (h + 1) * cols] for p in pieces], axis=1
-                )
-        return carry
-
-    lax.fori_loop(0, rows // cols, assemble, 0)
-
-    def one_head(h, carry):
-        own = hm_ref[h]
-        own_f = own.astype(jnp.float32)
-        other = (1.0 - own_f).astype(jnp.bfloat16)
-
-        def one_seq(b, carry):
-            q = q_s[b, pl.ds(at, rows), :] * own
-            s = jnp.dot(q, kt_s[b], preferred_element_type=jnp.float32) + bf_s[h] + mb_ref[b]
-            top = jnp.max(s, axis=1, keepdims=True)
-            p = jnp.exp2(((s - top) * (scale * LOG2E)).astype(jnp.bfloat16))
-            w = jnp.dot(p, v_s[b] * own + other, preferred_element_type=jnp.float32)
-            mixed = w / pltpu.roll(w, HEAD_DIM, 1)
-            acc_s[b] = jnp.where(own_f > 0.0, mixed, acc_s[b])
+                    cp.start()
             return carry
 
-        return lax.fori_loop(0, seqs, one_seq, carry, unroll=4)
-
-    lax.fori_loop(0, heads, one_head, 0)
-
-    for n, x_ref in enumerate((x0_ref, x1_ref)):
-
-        def gate(b, carry):
-            g = jnp.dot(x_ref[b, pl.ds(at, rows), :], wg_ref[...], preferred_element_type=jnp.float32)
-            g = g.astype(jnp.bfloat16).astype(jnp.float32)
-            gated = (acc_s[n * half + b] * jax.nn.sigmoid(g)).astype(jnp.bfloat16)
-            for t in range(rows // cols):
-                out_s[blk, t, n * half + b] = gated[t * cols : (t + 1) * cols]
-            return carry
-
-        lax.fori_loop(0, half, gate, 0)
-
-    def message(n, k, t):
-        cd = blk * (rows // cols) + t
-        dst = o_ref.at[core, pl.ds(pl.multiple_of(c * half, half), half)]
-        src = out_s.at[blk, t, pl.ds(n * half, half)]
-        cp = remote(src, dst, send.at[(cd * 2 + n)], recv.at[c * 2 + core], (chip * 2 + k, cd))
-        return cp, src, dst, cd
-
-    for t in range(rows // cols):
-        for n in range(2):
-            k = core if n == 0 else 1 - core
-            cp, src, dst, cd = message(n, k, t)
-            if n == 0:
-
-                @pl.when(cd != c)
-                def _():
-                    cp.start()
-
-                @pl.when(cd == c)
-                def _():
-                    pltpu.make_async_copy(src, dst, recv.at[c * 2 + core]).start()
-            else:
-                cp.start()
-
-    @pl.when(blk == pl.num_programs(0) - 1)
-    def _():
+        return lax.fori_loop(0, 2, group, carry)
+
+    lax.fori_loop(0, 2, block_of_rows, 0)
+
+    for hf in range(2):
         for cs in range(8):
             for k in range(2):
                 pltpu.make_async_copy(
-                    out_s.at[0, 0, pl.ds(0, half)], o_ref.at[k, pl.ds(cs * half, half)], recv.at[cs * 2 + k]
+                    out_s.at[0, 0, 0], o_ref.at[k, pl.ds(cs * half, half), :, hf], recv.at[hf * 16 + cs * 2 + k]
                 ).wait()
-        for cd in range(8):
-            for n in range(2):
-                k = core if n == 0 else 1 - core
-                cp = remote(
-                    out_s.at[0, 0, pl.ds(0, half)], o_ref.at[core, pl.ds(0, half)],
-                    send.at[cd * 2 + n], recv.at[0], (chip * 2 + 1 - core, cd),
-                )
-                if n == 0:
-
-                    @pl.when(cd != c)
-                    def _():
-                        cp.wait_send()
-                else:
-                    cp.wait_send()
-
-
-def attention(x0, x1, mask, tables, w, cols, home):
-    half, length, channels = x0.shape
+        for n in range(2):
+            for j in range(8):
+                p = (c + j) % 8
+                if n == 0 and j == 0:
+                    continue
+                row = r if n == 0 else partner[0]
+                remote(
+                    out_s.at[hf, n, p], o_ref.at[core, pl.ds(pl.multiple_of(c * half, half), half), :, hf],
+                    send.at[(hf * 2 + n) * 8 + p], recv.at[0], (row, p),
+                ).wait_send()
+        for o in range(3):
+            for d in range(1, 4):
+                one(hf, o, d).wait_send()
+                two(hf, o, d).wait_send()
+                for e in range(4):
+                    three(hf, o, e, d).wait_send()
+    swap.wait_send()
+    xs.wait_send()
+    ms.wait_send()
+
+
+def attention(tile, x, mask, w, cols, home):
+    half, length, channels = x.shape
     seqs = 2 * half
     lanes = w[0].shape[1]
     heads = lanes // HEAD_DIM
     rows = length // 2
-    scale = float(HEAD_DIM) ** -0.5
-    mb = (1e9 / scale) * (mask.astype(jnp.float32) - 1.0)[:, None, :]
+    sub = cols // 6
     hm = (jnp.arange(lanes)[None, None, :] // HEAD_DIM == jnp.arange(heads)[:, None, None]).astype(jnp.bfloat16)
     wq, wk, wv, wg = w
-    whole = lambda a: pl.BlockSpec(a.shape, lambda i: (0,) * a.ndim, pipeline_mode=pl.Buffered(1))
-    operands = (x0, x1, mb, hm, *tables, wq, wk.T, wv, wg)
+    vmem = pl.BlockSpec(memory_space=pltpu.VMEM)
+    hbm = pl.BlockSpec(memory_space=pl.ANY)
     dma = pltpu.SemaphoreType.DMA
-    return pl.pallas_call(
+    table = pltpu.VMEM((2, 4, 4, 4, sub, tile.shape[1] // 2), jnp.bfloat16)
+    out = pl.pallas_call(
         attn_kernel,
-        grid=(length // rows,),
-        out_shape=jax.ShapeDtypeStruct((2, home, cols, lanes), jnp.bfloat16),
-        in_specs=[whole(a) for a in operands],
-        out_specs=pl.BlockSpec(memory_space=pl.ANY),
+        out_shape=jax.ShapeDtypeStruct((2, home, 3, 2, sub, lanes), jnp.bfloat16),
+        in_specs=[vmem, hbm, vmem] + [vmem] * 5,
+        out_specs=hbm,
         scratch_shapes=[
-            pltpu.VMEM((seqs, length, lanes), jnp.bfloat16),
+            pltpu.VMEM((2 * tile.shape[0], tile.shape[1] // 2), jnp.bfloat16),
+            table, table, table,
+            pltpu.VMEM((2,) + x.shape, jnp.bfloat16),
+            pltpu.VMEM((2,) + mask.shape, jnp.float32),
+            pltpu.VMEM((seqs, 1, length), jnp.float32),
+            pltpu.VMEM((seqs, 2, rows, lanes), jnp.bfloat16),
             pltpu.VMEM((seqs, lanes, length), jnp.bfloat16),
             pltpu.VMEM((seqs, length, lanes), jnp.bfloat16),
+            pltpu.VMEM((seqs, 2, rows, lanes), jnp.bfloat16),
             pltpu.VMEM((heads, rows, length), jnp.float32),
-            pltpu.VMEM((seqs, rows, lanes), jnp.float32),
-            pltpu.VMEM((2, rows // cols, seqs, cols, lanes), jnp.bfloat16),
-            dma((16,)), dma((16,)),
+            pltpu.VMEM((half, rows, lanes), jnp.float32),
+            pltpu.VMEM((2, 2, 8, half, 3, sub, lanes), jnp.bfloat16),
+            dma((3,)), dma((3,)), dma((3,)), dma((6,)),
+            dma((24,)), dma((24,)), dma((24,)), dma((24,)), dma((96,)), dma((96,)),
+            dma((32,)), dma((32,)),
         ],
         compiler_params=pltpu.CompilerParams(
-            vmem_limit_bytes=56 << 20, collective_id=4, has_side_effects=True
+            vmem_limit_bytes=56 << 20, collective_id=3, has_side_effects=True
         ),
         name="attn",
-    )(*operands)
+    )(tile, x, mask, hm, wq, wk.T, wv, wg)
+    return out.reshape(2, home, cols, lanes)
 
 
 def opm_kernel(left_ref, lmask_ref, right_ref, rrow_ref, rcol_ref, pair_ref, gain_ref, w_ref, wd_ref, x_ref, mk_ref,
@@ -622,15 +613,11 @@
         left_all, right_all, residue_rows, residue_cols, duo_embedding,
         duo_layernorm_stretch, kronecker_linear_kernel, duo_logit_kernel, exponential_probabilities, mask_out,
     )
-    *tables, other_rows, other_mask = share(bias_tile, own_rows, own_mask)
-    masks = jnp.concatenate([own_mask, other_mask], axis=1).reshape(8, 2, 8, 128)
-    masks = masks[:, :, : homolog_number // 8, :amino_position_number].transpose(1, 2, 0, 3)
-    masks = masks.reshape(homolog_number // 4, 8 * amino_position_number)
     lanes = inner_width // 2
     by_half = asker_lookup_sigmoid_kernel.reshape(-1, 4, 2, lanes)
     mine = lax.dynamic_index_in_dim(by_half, row_index % 2, 2, keepdims=False)
     gated = attention(
-        own_rows, other_rows, masks, tables, [mine[:, n] for n in range(4)], amino_position_number, homolog_number
+        bias_tile, own_rows, own_mask, [mine[:, n] for n in range(4)], amino_position_number, homolog_number
     )
     closing = closing_linear_kernel.reshape(2, lanes, -1)
     summed_increment = jnp.einsum("hsqd,hdc->sqc", gated, closing, preferred_element_type=jnp.float32)

time: 236 us -> 202 us (0.86)
  Pallas kernels: 208 us -> 179 us
  local copies, waits for them, and re-layouts: 9.4 us -> 6.83 us
    pallas_call x2 -> x1, Pallas kernels: 111 us -> 81.5 us  [attention(): pl.pallas_call(attn_kernel, out_shape=jax.ShapeDtypeStruct((2, home, 3, 2...]
where the time goes in v3:
time: 202 us; the launch traced here: 201 us
  Pallas kernels  179 us (89%)
  other arithmetic  9.2 us (5%)
  local copies, waits for them, and re-layouts  6.83 us (3%)
  matrix products  5.83 us (3%)
    pallas_call x1, Pallas kernels, attention(): pl.pallas_call(attn_kernel, out_shape=jax.ShapeDtypeStruct((2, home, 3, 2...  81.5 us
    pallas_call x1, Pallas kernels, spread(): pl.pallas_call(spread_kernel, out_shape=(jax.ShapeDtypeStruct((16 * seqs,...  68.1 us
    pallas_call x1, Pallas kernels, opm(): pl.pallas_call(opm_kernel, grid=(steps,), out_shape=(jax.ShapeDtypeStruct...  28.9 us

profile of v3, /device:TPU:1, one launch (start us, length us, event | category | flops | bytes accessed | tf_op | source)
XLA Modules:
  0.0 201.3 jit_solution(5499100352402620511)
XLA Ops:
  0.6 0.0 copy-start
  0.6 0.0 copy-start.5
  0.7 0.0 copy-start.13
  0.7 0.0 copy-start.11
  0.7 0.8 fusion.19
  1.5 0.1 reshape.128
  1.6 2.0 %convert_reduce_fusion = f32[32,96]{1,0:T(8,128)S(1)} fusion(bf16[32,96,256]{2,1,0:T(8,128)(2,1)} %param.13), kind=kLoop, calls=%fused_computation.2 | loop fusion | flops 1569792 | bytes 1585152 | tf_op jit(solution)/shard_map/reduce_sum | solution.py:15
  3.7 2.4 %fusion.6 = f32[32,96]{1,0:T(8,128)S(1)} fusion(bf16[32,96,256]{2,1,0:T(8,128)(2,1)} %param.13, f32[32,96]{1,0:T(8,128)S(1)} %broadcast_multiply_fusion), kind=kLoop, calls=%fused_computation.9 | loop fusion | flops 3142656 | bytes 1597440 | tf_op jit(solution)/shard_map/reduce_sum | solution.py:17
  6.1 0.0 copy-done.5
  6.1 0.0 copy-done.13
  6.1 0.0 copy-done.11
  6.2 0.0 copy-start.12
  6.2 1.3 fusion.8
  7.5 0.4 copy.20
  7.8 0.6 reshape.127
  8.4 0.0 copy-start.9
  8.4 0.0 copy-start.8
  8.5 0.0 copy-start.10
  8.5 0.7 fusion.15.left_ref
  9.2 0.0 copy-done.12
  9.2 1.3 fusion.10
  10.4 0.0 copy-start.3
  10.5 0.0 copy-start.4
  10.5 0.3 reshape.129
  10.8 0.7 fusion.16.right_ref
  11.5 68.1 %spread.1 = (bf16[512,1664]{1,0:T(8,128)(2,1)}, bf16[512,3200]{1,0:T(8,128)(2,1)}) custom-call(bf16[2,32,1664]{2,1,0:T(8,128)(2,1)} %fusion.15.left_ref, bf16[32,3200]{1,0:T(8,128)(2,1)} %fusion.16.right_ref), custom_call_target="tpu_custom_call" | custom-call | tf_op jit(solution)/shard_map/spread/pallas_call | solution.py:117
  79.6 0.0 copy-done.9
  79.6 0.1 dynamic-slice_bitcast_fusion.1.rrow_ref
  79.7 0.1 dynamic-slice_bitcast_fusion
  79.8 0.1 copy.24.rcol_ref
  79.9 0.0 copy-done.8
  79.9 0.1 copy.36
  80.0 0.0 copy-done.10
  80.0 1.9 fusion.5.x_ref
  81.9 0.0 copy-done.3
  81.9 0.0 copy-start.7
  81.9 28.9 %opm.1 = (f32[48,96,128]{2,1,0:T(8,128)}, bf16[48,768]{1,0:T(8,128)(2,1)S(1)}, bf16[4,768,256]{2,1,0:T(8,128)(2,1)}, f32[8,8,128]{2,1,0:T(8,128)S(1)}) custom-call(bf16[512,1664]{1,0:T(8,128)(2,1)} %get-tuple-element.8.left_ref.lmask_ref, bf16[512,1664]{1,0:T(8,128)(2,1)} %get-tuple-element.8.left_ref.lmask_ref, ...), custom_call_target="tpu_custom_call" | custom-call | tf_op jit(solution)/shard_map/opm/pallas_call | solution.py:529
  110.8 0.0 copy-start.1
  110.8 0.6 copy-done.1
  111.5 0.6 copy-done.2
  112.1 0.6 compare_convert_fusion.hm_ref
  112.7 0.4 reshape.135
  113.0 0.5 constant_dynamic-slice_fusion
  113.7 0.7 slice_bitcast_fusion
  114.3 0.7 copy.26.wk_ref
  115.1 81.5 %attn.1 = bf16[2,32,3,2,16,128]{5,4,3,2,1,0:T(8,128)(2,1)} custom-call(bf16[48,768]{1,0:T(8,128)(2,1)} %copy-done.1, bf16[4,768,256]{2,1,0:T(8,128)(2,1)} %get-tuple-element.11.xin_ref, f32[8,8,128]{2,1,0:T(8,128)} %copy-done.2, bf16[4,1,128]{2,1,0:T(2,128)(2,1)} %compare_convert_fusion.hm_ref, bf16[256,128]{1,0:T(8,128)(2,1)} %get-tuple-element.17.wq_ref, ...), custom_call_target="tpu_custom_call" | custom-call | tf_op jit(solution)/shard_map/attn/pallas_call | solution.py:388
  196.6 3.3 %fusion.7 = bf16[32,96,256]{2,1,0:T(8,128)(2,1)} fusion(bf16[32,96,256]{2,1,0:T(8,128)(2,1)S(1)} %copy-done.5, bf16[2,32,96,128]{3,2,1,0:T(8,128)(2,1)} %bitcast.52, bf16[2,128,256,1]{2,1,3,0:T(8,128)(2,1)S(1)} %bitcast.48), kind=kOutput, calls=%fused_computation.10 | convolution fusion | flops 405012480 | bytes 4849664 | tf_op jit(solution)/shard_map/hsqd,hdc->sqc/dot_general | solution.py:623
  199.9 1.4 copy.40
  (14 shorter events, 0.1 us)
Async XLA Ops:
  0.6 196.0 %copy-start = (bf16[256,256]{1,0:T(8,128)(2,1)S(1)}, bf16[256,256]{1,0:T(8,128)(2,1)}, u32[]{:S(2)}) copy-start(bf16[256,256]{1,0:T(8,128)(2,1)} %param.25) | copy-start | bytes 393220
  0.6 5.5 %copy-start.5 = (bf16[32,96,256]{2,1,0:T(8,128)(2,1)S(1)}, bf16[32,96,256]{2,1,0:T(8,128)(2,1)}, u32[]{:S(2)}) copy-start(bf16[32,96,256]{2,1,0:T(8,128)(2,1)} %param.13) | copy-start | bytes 4718596
  0.7 5.5 %copy-start.13 = (f32[256]{0:T(256)S(1)}, f32[256]{0:T(256)}, u32[]{:S(2)}) copy-start(f32[256]{0:T(256)} %param.17) | copy-start | bytes 3076
  0.7 5.5 %copy-start.11 = (bf16[256,32]{0,1:T(8,128)(2,1)S(1)}, bf16[256,32]{0,1:T(8,128)(2,1)}, u32[]{:S(2)}) copy-start(bf16[256,32]{0,1:T(8,128)(2,1)} %param.20) | copy-start | bytes 49156
  6.2 3.0 %copy-start.12 = (bf16[256,32]{0,1:T(8,128)(2,1)S(1)}, bf16[256,32]{0,1:T(8,128)(2,1)}, u32[]{:S(2)}) copy-start(bf16[256,32]{0,1:T(8,128)(2,1)} %param.21) | copy-start | bytes 49156
  8.4 71.2 %copy-start.9 = (s32[768]{0:T(1024)S(1)}, s32[768]{0:T(1024)}, u32[]{:S(2)}) copy-start(s32[768]{0:T(1024)} %param.15) | copy-start | bytes 9220
  8.4 71.5 %copy-start.8 = (bf16[1024,128]{1,0:T(8,128)(2,1)S(1)}, bf16[1024,128]{1,0:T(8,128)(2,1)}, u32[]{:S(2)}) copy-start(bf16[1024,128]{1,0:T(8,128)(2,1)} %param.22) | copy-start | bytes 786436
  8.5 71.6 %copy-start.10 = (f32[256]{0:T(256)S(1)}, f32[256]{0:T(256)}, u32[]{:S(2)}) copy-start(f32[256]{0:T(256)} %param.18) | copy-start | bytes 3076
  10.4 71.5 %copy-start.3 = (bf16[128,8]{0,1:T(8,128)(2,1)S(1)}, bf16[128,8]{0,1:T(8,128)(2,1)}, u32[]{:S(2)}) copy-start(bf16[128,8]{0,1:T(8,128)(2,1)} %param.23) | copy-start | bytes 6148
  10.5 71.5 %copy-start.4 = (f32[128]{0:T(128)S(1)}, f32[128]{0:T(128)}, u32[]{:S(2)}) copy-start(f32[128]{0:T(128)} %param.19) | copy-start | bytes 1540
  81.9 30.8 %copy-start.7 = (bf16[256,1024]{1,0:T(8,128)(2,1)S(1)}, bf16[256,1024]{1,0:T(8,128)(2,1)}, u32[]{:S(2)}) copy-start(bf16[256,1024]{1,0:T(8,128)(2,1)} %param.24) | copy-start | bytes 1572868
  110.8 0.6 copy-start.1
  111.5 0.6 copy-start.2
  196.6 3.3 %copy-start.6 = (f32[48,96,128]{2,1,0:T(8,128)S(1)}, f32[48,96,128]{2,1,0:T(8,128)}, u32[]{:S(2)}) copy-start(f32[48,96,128]{2,1,0:T(8,128)} %get-tuple-element.23) | copy-start | bytes 7077892

commit v4 on v3

--- a/solution.py
+++ b/solution.py
@@ -40,73 +40,111 @@
     pl.semaphore_signal(barrier, inc=1, device_id=device, device_id_type=MESH)
 
 
-def spread_kernel(left_ref, right_ref, left_out, right_out, lsend, lrecv, rsend, rrecv, fsend, frecv):
+def spread_kernel(left_ref, right_ref, left_out, right_out, lsend, lrecv, gsend, zsend, zrecv, ysend, yrecv, fsend,
+                  frecv, own_sem):
     r, c = place()
     chip, core = r // 2, r % 2
+    y, zh, x, zl = r // 4, chip % 2, c // 2, c % 2
     seqs = right_ref.shape[0]
-    here = pl.ds(pl.multiple_of(r * seqs, seqs), seqs)
+
+    def rows(n):
+        return pl.ds(pl.multiple_of(n * seqs, seqs), seqs)
+
+    here = rows(r)
     partner = (chip * 2 + 1 - core, c)
-    mine = chip == c
+    across = (row_of(y, 1 - zh, core), c)
+    aside = (r, x * 2 + 1 - zl)
+    mine = jnp.logical_and(chip == c, zh == zl)
+
+    def own_left(h, j):
+        return jnp.logical_and(mine, core == h) if j == 0 else False
+
+    def unless(cond, f):
+        if cond is False:
+            f()
+        else:
+            pl.when(jnp.logical_not(cond))(f)
+
     barrier = pltpu.get_barrier_semaphore()
-    for d in range(1, 8):
-        signal(barrier, ((r + 2 * d) % 16, c))
     signal(barrier, partner)
-    for n in range(16):
-
-        @pl.when(jnp.logical_not(jnp.logical_and(mine, r == n)))
-        def _():
-            signal(barrier, (n, chip))
-
-    pl.semaphore_wait(barrier, 24 - mine.astype(jnp.int32))
-
-    rights = [None]
-    for d in range(1, 8):
-        cp = remote(right_ref, right_out.at[here], rsend.at[d], rrecv.at[d], ((r + 2 * d) % 16, c))
-        cp.start()
-        rights.append(cp)
-    own = pltpu.make_async_copy(right_ref, right_out.at[here], rrecv.at[0])
-    own.start()
-    forwards = [remote(right_ref, right_out.at[here], fsend.at[0], frecv.at[0], partner)]
-    forwards[0].start()
+    signal(barrier, across)
+    signal(barrier, aside)
+    for d in range(1, 4):
+        signal(barrier, (row_of((y + d) % 4, zh, core), c))
+    for ys in range(4):
+        for k in range(2):
+            source = row_of(ys, zl, k)
+            unless(jnp.logical_and(mine, r == source), lambda: signal(barrier, (source, chip)))
+    pl.semaphore_wait(barrier, 14 - mine.astype(jnp.int32))
+
+    over = remote(right_ref, right_out.at[here], zsend.at[0], zrecv.at[0], across)
+    over.start()
+    sends = [over]
     lefts = []
-    for j in range(8):
+    for j in range(4):
         for h in range(2):
-            cd = (c + j) % 8
-            cp = remote(left_ref.at[h], left_out.at[here], lsend.at[2 * j + h], lrecv.at[r], (2 * c + h, cd))
+            to = (2 * c + h, ((x + j) % 4) * 2 + zh)
+            cp = remote(left_ref.at[h], left_out.at[here], lsend.at[2 * j + h], lrecv.at[r], to)
             lefts.append((cp, h, j))
+            unless(own_left(h, j), cp.start)
             if j == 0:
-                own_left = jnp.logical_and(mine, core == h)
-
-                @pl.when(jnp.logical_not(own_left))
-                def _():
-                    cp.start()
-
-                @pl.when(own_left)
+
+                @pl.when(own_left(h, j))
                 def _():
                     pltpu.make_async_copy(left_ref.at[h], left_out.at[here], lrecv.at[r]).start()
-            else:
-                cp.start()
-    for d in range(1, 8):
-        rights[d].wait_recv()
-        block = pl.ds(pl.multiple_of(((r + 16 - 2 * d) % 16) * seqs, seqs), seqs)
-        fw = remote(right_out.at[block], right_out.at[block], fsend.at[d], frecv.at[d], partner)
-        fw.start()
-        forwards.append(fw)
+
+    def along(n, d):
+        block = rows(row_of(y, (zh + n) % 2, core))
+        src = right_ref if n == 0 else right_out.at[block]
+        return remote(src, right_out.at[block], ysend.at[n * 4 + d], yrecv.at[n * 4 + d], (row_of((y + d) % 4, zh, core), c))
+
+    def forward(n, d):
+        block = rows(row_of((y + 4 - d) % 4, (zh + n) % 2, core))
+        src = right_ref if n == 0 and d == 0 else right_out.at[block]
+        return remote(src, right_out.at[block], fsend.at[n * 4 + d], frecv.at[n * 4 + d], partner)
+
+    for d in (1, 3, 2):
+        along(0, d).start()
+    own = pltpu.make_async_copy(right_ref, right_out.at[here], own_sem.at[0])
+    own.start()
+    forward(0, 0).start()
+    over.wait_recv()
+    for d in (1, 3, 2):
+        along(1, d).start()
+    forward(1, 0).start()
+
+    def relay(d, k):
+        source = row_of((y + 4 - d) % 4, zl, k)
+        block = left_out.at[rows(source)]
+        return block, source, remote(block, block, gsend.at[d * 2 + k], lrecv.at[source], aside)
+
+    for d in (0, 1, 3, 2):
+        for k in range(2):
+            block, source, cp = relay(d, k)
+            pltpu.make_async_copy(left_ref.at[0], block, lrecv.at[source]).wait()
+            cp.start()
+        if d > 0:
+            along(0, d).wait_recv()
+            forward(0, d).start()
+    for d in (1, 3, 2):
+        along(1, d).wait_recv()
+        forward(1, d).start()
+    for ys in range(4):
+        for k in range(2):
+            source = row_of(ys, 1 - zl, k)
+            pltpu.make_async_copy(left_ref.at[0], left_out.at[rows(source)], lrecv.at[source]).wait()
     own.wait()
-    for n in range(16):
-        pltpu.make_async_copy(left_ref.at[0], left_out.at[pl.ds(n * seqs, seqs)], lrecv.at[n]).wait()
-    for d in range(8):
-        forwards[d].wait()
-    for d in range(1, 8):
-        rights[d].wait_send()
+    for n in range(2):
+        for d in range(4):
+            forward(n, d).wait()
+            if d > 0:
+                along(n, d).wait_send()
+    over.wait_send()
     for cp, h, j in lefts:
-        if j == 0:
-
-            @pl.when(jnp.logical_not(jnp.logical_and(mine, core == h)))
-            def _():
-                cp.wait_send()
-        else:
-            cp.wait_send()
+        unless(own_left(h, j), cp.wait_send)
+    for d in range(4):
+        for k in range(2):
+            relay(d, k)[2].wait_send()
 
 
 def spread(left, right):
@@ -122,7 +160,9 @@
         ),
         in_specs=[vmem, vmem],
         out_specs=(hbm, hbm),
-        scratch_shapes=[dma((16,)), dma((16,)), dma((8,)), dma((8,)), dma((8,)), dma((8,))],
+        scratch_shapes=[
+            dma((8,)), dma((16,)), dma((8,)), dma((1,)), dma((1,)), dma((8,)), dma((8,)), dma((8,)), dma((8,)), dma((1,))
+        ],
         compiler_params=pltpu.CompilerParams(collective_id=1, has_side_effects=True),
         name="spread",
     )(left, right)
@@ -131,8 +171,7 @@
 LOG2E = 1.4426950408889634
 
 
-def attn_kernel(tile_ref, xin_ref, mask_ref, hm_ref, wq_ref, wk_ref, wv_ref, wg_ref, o_ref,
-                block, ta, tb, tc, x_s, m_s, mb_s, q_s, kt_s, v_s, g_s, bf_s, acc_s, out_s,
+def attn_kernel(tile_ref, xin_ref, mask_ref, gain_ref, w_ref, o_ref, w_s, block, ta, tb, tc, x_s, m_s, mb_s, q_s, kt_s, v_s, g_s, bf_s, acc_s, out_s,
                 csem, csend, crecv, l1, s1, r1, s2, r2, s3, r3, send, recv):
     r, c = place()
     chip, core = r // 2, r % 2
@@ -225,12 +264,18 @@
     xs.start()
     ms.start()
 
+    width = w_ref.shape[1] // 4
+    part = w_s.shape[1] // 4
+    for n in range(4):
+        w_s[:, n * part : (n + 1) * part] = w_ref[:, pl.ds(pl.multiple_of(n * width + core * part, part), part)]
+
     def project(n):
         def body(b, carry):
-            x = x_s[n, b]
+            x = standardize_features(x_s[n, b].astype(jnp.float32))
+            x = (x * gain_ref[...]).astype(jnp.bfloat16)
             at = n * half + b
-            p = jnp.dot(x, wq_ref[...], preferred_element_type=jnp.float32).astype(jnp.bfloat16)
-            g = jnp.dot(x, wg_ref[...], preferred_element_type=jnp.float32).astype(jnp.bfloat16)
+            both = jnp.dot(x, w_s[...], preferred_element_type=jnp.float32).astype(jnp.bfloat16)
+            p, k, v, g = [both[:, i * part : (i + 1) * part] for i in range(4)]
             for hf in range(2):
                 q_s[at, hf] = jnp.concatenate(
                     [p[(2 * i + hf) * sub : (2 * i + hf + 1) * sub] for i in range(rows // sub)], axis=0
@@ -238,10 +283,8 @@
                 g_s[at, hf] = jnp.concatenate(
                     [g[(2 * i + hf) * sub : (2 * i + hf + 1) * sub] for i in range(rows // sub)], axis=0
                 )
-            v_s[at] = jnp.dot(x, wv_ref[...], preferred_element_type=jnp.float32).astype(jnp.bfloat16)
-            kt_s[at] = lax.dot_general(
-                wk_ref[...], x, LAST_LAST, preferred_element_type=jnp.float32
-            ).astype(jnp.bfloat16)
+            v_s[at] = v
+            kt_s[at] = k.T
             return carry
 
         lax.fori_loop(0, half, body, 0)
@@ -280,10 +323,11 @@
                         piece = tb[hf, z, x, y]
                     else:
                         piece = tc[hf, x, y, z]
-                    pieces.append(piece.astype(jnp.float32) * (1.0 / scale))
+                    pieces.append(piece)
                 for h in range(heads):
-                    bf_s[h, pl.ds(pl.multiple_of(p * 3 * sub + o * sub, sub), sub), :] = jnp.concatenate(
-                        [piece[:, h * cols : (h + 1) * cols] for piece in pieces], axis=1
+                    line = jnp.concatenate([piece[:, h * cols : (h + 1) * cols] for piece in pieces], axis=1)
+                    bf_s[h, pl.ds(pl.multiple_of(p * 3 * sub + o * sub, sub), sub), :] = line.astype(jnp.float32) * (
+                        1.0 / scale
                     )
             return carry
 
@@ -295,8 +339,9 @@
                 def _():
                     last(1)
 
-                mine = hm_ref[h]
-                mine_f = mine.astype(jnp.float32)
+                head = lax.broadcasted_iota(jnp.int32, (1, part), 1) // HEAD_DIM
+                mine_f = jnp.where(head == h, 1.0, 0.0)
+                mine = mine_f.astype(jnp.bfloat16)
                 other = (1.0 - mine_f).astype(jnp.bfloat16)
                 for b in range(half):
                     at = n * half + b
@@ -372,15 +417,13 @@
     ms.wait_send()
 
 
-def attention(tile, x, mask, w, cols, home):
+def attention(tile, x, mask, gain, w, cols, home):
     half, length, channels = x.shape
     seqs = 2 * half
-    lanes = w[0].shape[1]
+    lanes = w.shape[1] // 8
     heads = lanes // HEAD_DIM
     rows = length // 2
     sub = cols // 6
-    hm = (jnp.arange(lanes)[None, None, :] // HEAD_DIM == jnp.arange(heads)[:, None, None]).astype(jnp.bfloat16)
-    wq, wk, wv, wg = w
     vmem = pl.BlockSpec(memory_space=pltpu.VMEM)
     hbm = pl.BlockSpec(memory_space=pl.ANY)
     dma = pltpu.SemaphoreType.DMA
@@ -388,9 +431,10 @@
     out = pl.pallas_call(
         attn_kernel,
         out_shape=jax.ShapeDtypeStruct((2, home, 3, 2, sub, lanes), jnp.bfloat16),
-        in_specs=[vmem, hbm, vmem] + [vmem] * 5,
+        in_specs=[vmem, hbm, vmem, vmem, vmem],
         out_specs=hbm,
         scratch_shapes=[
+            pltpu.VMEM((channels, 4 * lanes), jnp.bfloat16),
             pltpu.VMEM((2 * tile.shape[0], tile.shape[1] // 2), jnp.bfloat16),
             table, table, table,
             pltpu.VMEM((2,) + x.shape, jnp.bfloat16),
@@ -411,7 +455,7 @@
             vmem_limit_bytes=56 << 20, collective_id=3, has_side_effects=True
         ),
         name="attn",
-    )(tile, x, mask, hm, wq, wk.T, wv, wg)
+    )(tile, x, mask, gain.reshape(1, channels), w)
     return out.reshape(2, home, cols, lanes)
 
 
@@ -459,8 +503,8 @@
         wb_s[...] = jnp.zeros_like(wb_s)
 
         def fill(b, carry):
-            for i in range(4):
-                wb_s[pl.ds(pl.multiple_of(b * 128 + i * 32, 32), 32), i * 128 : (i + 1) * 128] = w_ref[b]
+            for i in range(2):
+                wb_s[pl.ds(pl.multiple_of(b * 64 + i * 32, 32), 32), i * 128 : (i + 1) * 128] = w_ref[b]
             return carry
 
         lax.fori_loop(0, opm, fill, 0)
@@ -481,20 +525,25 @@
     def outer(n, carry):
         at = pl.multiple_of(n * chunk, chunk)
         m = jnp.dot(rt_s[pl.ds(at, chunk), :], left_ref[...], preferred_element_type=jnp.float32)
-        m = m.astype(jnp.bfloat16)
-        for bb in range(4):
+        low = lax.broadcasted_iota(jnp.int32, (1, 128), 1) < 64
+        for bb in range(2):
+            lanes = pl.ds(pl.multiple_of((n * 2 + bb) * 128, 128), 128)
             for g in range(group):
-                m_s[g * cols : (g + 1) * cols, pl.ds(pl.multiple_of((n * 4 + bb) * 128, 128), 128)] = m[
-                    bb * cols : (bb + 1) * cols, g * 128 : (g + 1) * 128
+                m0, m1 = [
+                    m[(2 * bb + k) * cols : (2 * bb + k + 1) * cols, g * 128 : (g + 1) * 128] for k in range(2)
                 ]
+                one = jnp.where(low, m0, pltpu.roll(m1, 64, 1)).astype(jnp.bfloat16)
+                two = jnp.where(low, pltpu.roll(m0, 64, 1), m1).astype(jnp.bfloat16)
+                m_s[(2 * g) * cols : (2 * g + 1) * cols, lanes] = one
+                m_s[(2 * g + 1) * cols : (2 * g + 2) * cols, lanes] = two
         return carry
 
     lax.fori_loop(0, opm // 4, outer, 0)
     factor = f_s[step]
     update = jnp.dot(m_s[...], wb_s[...], preferred_element_type=jnp.float32)
-    for g in range(group):
-        for ii in range(4):
-            i = 4 * g + ii
+    for g in range(2 * group):
+        for ii in range(2):
+            i = 2 * g + ii
             u = update[g * cols : (g + 1) * cols, ii * 128 : (ii + 1) * 128]
             x = pair_ref[i] + u * factor[:, i : i + 1]
             out_ref[i] = x
@@ -549,8 +598,8 @@
         ),
         scratch_shapes=[
             pltpu.VMEM((cols * width, seqs), jnp.bfloat16),
-            pltpu.VMEM((128 * width, 4 * channels), jnp.bfloat16),
-            pltpu.VMEM((per // 4 * cols, 128 * width), jnp.bfloat16),
+            pltpu.VMEM((64 * width, 2 * channels), jnp.bfloat16),
+            pltpu.VMEM((per // 2 * cols, 64 * width), jnp.bfloat16),
             pltpu.VMEM((steps, cols, per), jnp.float32),
             pltpu.VMEM((heads, per, cols), jnp.float32),
             dma((8,)), dma((8,)), dma((8,)), dma((8,)),
@@ -598,7 +647,6 @@
     right = (right * availability_real[:, None, :]).astype(jnp.bfloat16)
     right_mask = jnp.pad(availability_real, ((0, 0), (0, 128 - amino_position_number))).astype(jnp.bfloat16)
     right = jnp.concatenate([right.reshape(homolog_number, -1), right_mask], axis=1)
-    exponential_probabilities = (standardized_features * lineup_layernorm_stretch).astype(jnp.bfloat16)
     mask_out = jnp.pad(
         availability_real.reshape(8, homolog_number // 8, amino_position_number),
         ((0, 0), (0, 8 - homolog_number // 8), (0, 128 - amino_position_number)),
@@ -611,13 +659,12 @@
     )
     duo_after_averaging, bias_tile, own_rows, own_mask = opm(
         left_all, right_all, residue_rows, residue_cols, duo_embedding,
-        duo_layernorm_stretch, kronecker_linear_kernel, duo_logit_kernel, exponential_probabilities, mask_out,
+        duo_layernorm_stretch, kronecker_linear_kernel, duo_logit_kernel, aligned_family_embedding, mask_out,
     )
     lanes = inner_width // 2
-    by_half = asker_lookup_sigmoid_kernel.reshape(-1, 4, 2, lanes)
-    mine = lax.dynamic_index_in_dim(by_half, row_index % 2, 2, keepdims=False)
     gated = attention(
-        bias_tile, own_rows, own_mask, [mine[:, n] for n in range(4)], amino_position_number, homolog_number
+        bias_tile, own_rows, own_mask, lineup_layernorm_stretch, asker_lookup_sigmoid_kernel,
+        amino_position_number, homolog_number,
     )
     closing = closing_linear_kernel.reshape(2, lanes, -1)
     summed_increment = jnp.einsum("hsqd,hdc->sqc", gated, closing, preferred_element_type=jnp.float32)

time: 202 us -> 182 us (0.901)
  Pallas kernels: 179 us -> 163 us
  other arithmetic: 9.2 us -> 6.58 us
    pallas_call x1, Pallas kernels: 68.1 us -> 51.1 us  [spread(): pl.pallas_call(spread_kernel, out_shape=(jax.ShapeDtypeStruct((16 * seqs,...]
    convert_element_type x2 -> x0, other arithmetic: 2.47 us -> none  [the longest x1 1.87 us: shards(): (standardized_features * lineup_layernorm_stretch).astype(jnp.bfloat16)]
    pallas_call x1, Pallas kernels: 81.5 us -> 84 us  [attention(): pl.pallas_call(attn_kernel, out_shape=jax.ShapeDtypeStruct((2, home, 3, 2...]
where the time goes in v4:
time: 182 us
  Pallas kernels  163 us (90%)
  other arithmetic  6.58 us (4%)
  matrix products  5.81 us (3%)
  local copies, waits for them, and re-layouts  5.29 us (3%)
    pallas_call x1, Pallas kernels, attention(): pl.pallas_call(attn_kernel, out_shape=jax.ShapeDtypeStruct((2, home, 3, 2...  84 us
    pallas_call x1, Pallas kernels, spread(): pl.pallas_call(spread_kernel, out_shape=(jax.ShapeDtypeStruct((16 * seqs,...  51.1 us
    pallas_call x1, Pallas kernels, opm(): pl.pallas_call(opm_kernel, grid=(steps,), out_shape=(jax.ShapeDtypeStruct...  28.5 us

profile of v4, /device:TPU:1, one launch (start us, length us, event | category | flops | bytes accessed | tf_op | source)
XLA Modules:
  0.0 182.1 jit_solution(13817736539039014724)
XLA Ops:
  0.6 0.0 copy-start
  0.6 0.0 copy-start.5
  0.7 0.0 copy-start.12
  0.7 0.0 copy-start.10
  0.7 0.0 copy-start.9
  0.7 0.8 copy-done
  1.5 0.7 convert_element_type.39
  2.2 0.1 dynamic-slice_bitcast_fusion
  2.3 0.1 dynamic-slice_bitcast_fusion.1.rrow_ref
  2.4 2.0 %convert_reduce_fusion = f32[32,96]{1,0:T(8,128)S(1)} fusion(bf16[32,96,256]{2,1,0:T(8,128)(2,1)} %x_ref.1), kind=kLoop, calls=%fused_computation.2 | loop fusion | flops 1569792 | bytes 1585152 | tf_op jit(solution)/shard_map/reduce_sum | solution.py:15
  4.4 0.0 copy-start.11
  4.4 2.5 %fusion.2 = f32[32,96]{1,0:T(8,128)S(1)} fusion(bf16[32,96,256]{2,1,0:T(8,128)(2,1)} %x_ref.1, f32[32,96]{1,0:T(8,128)S(1)} %broadcast_multiply_fusion), kind=kLoop, calls=%fused_computation.5 | loop fusion | flops 3142656 | bytes 1597440 | tf_op jit(solution)/shard_map/reduce_sum | solution.py:17
  6.9 0.0 copy-done.9
  6.9 0.1 reshape.54
  7.0 0.1 copy.22.rcol_ref
  7.1 0.0 copy-done.5
  7.1 0.0 copy-done.12
  7.2 0.0 copy-done.10
  7.2 1.3 fusion.8
  8.5 0.0 copy-start.8
  8.5 0.3 reshape.55
  8.8 0.7 fusion.14.right_ref
  9.5 0.0 copy-done.11
  9.5 0.0 copy-start.3
  9.5 0.0 copy-start.4
  9.5 1.3 fusion.6
  10.8 0.0 copy-done.8
  10.8 0.1 copy.29
  10.9 0.4 copy.18
  11.3 0.6 reshape.53
  11.9 0.7 fusion.13.left_ref
  12.6 51.1 %spread.1 = (bf16[512,1664]{1,0:T(8,128)(2,1)}, bf16[512,3200]{1,0:T(8,128)(2,1)}) custom-call(bf16[2,32,1664]{2,1,0:T(8,128)(2,1)} %fusion.13.left_ref, bf16[32,3200]{1,0:T(8,128)(2,1)} %fusion.14.right_ref), custom_call_target="tpu_custom_call" | custom-call | tf_op jit(solution)/shard_map/spread/pallas_call | solution.py:155
  63.6 0.0 copy-done.3
  63.7 0.0 copy-done.4
  63.7 28.5 %opm.1 = (f32[48,96,128]{2,1,0:T(8,128)}, bf16[48,768]{1,0:T(8,128)(2,1)S(1)}, bf16[4,768,256]{2,1,0:T(8,128)(2,1)}, f32[8,8,128]{2,1,0:T(8,128)S(1)}) custom-call(bf16[512,1664]{1,0:T(8,128)(2,1)} %get-tuple-element.8.left_ref.lmask_ref, bf16[512,1664]{1,0:T(8,128)(2,1)} %get-tuple-element.8.left_ref.lmask_ref, ...), custom_call_target="tpu_custom_call" | custom-call | tf_op jit(solution)/shard_map/opm/pallas_call | solution.py:578
  92.1 0.0 copy-start.1
  92.2 0.6 copy-done.1
  92.8 0.0 copy-start.2
  92.8 0.6 copy-done.2
  93.4 0.0 copy-start.6
  93.4 84.0 %attn.1 = bf16[2,32,3,2,16,128]{5,4,3,2,1,0:T(8,128)(2,1)} custom-call(bf16[48,768]{1,0:T(8,128)(2,1)} %copy-done.1, bf16[4,768,256]{2,1,0:T(8,128)(2,1)} %get-tuple-element.11.xin_ref, f32[8,8,128]{2,1,0:T(8,128)} %copy-done.2, f32[1,256]{1,0:T(1,128)} %bitcast.45, bf16[256,1024]{1,0:T(8,128)(2,1)} %w_ref.1), custom_call_target="tpu_custom_call" | custom-call | tf_op jit(solution)/shard_map/attn/pallas_call | solution.py:431
  177.4 0.0 copy-start.7
  177.4 0.0 copy-done.6
  177.4 3.3 %fusion.5 = bf16[32,96,256]{2,1,0:T(8,128)(2,1)} fusion(bf16[32,96,256]{2,1,0:T(8,128)(2,1)S(1)} %copy-done.6, bf16[2,32,96,128]{3,2,1,0:T(8,128)(2,1)} %bitcast.40, bf16[2,128,256,1]{2,1,3,0:T(8,128)(2,1)S(1)} %bitcast.36), kind=kOutput, calls=%fused_computation.8 | convolution fusion | flops 405012480 | bytes 4849664 | tf_op jit(solution)/shard_map/hsqd,hdc->sqc/dot_general | solution.py:670
  180.7 0.0 copy-done.7
  180.7 1.4 copy.33
  (6 shorter events, 0.1 us)
Async XLA Ops:
  0.6 0.9 copy-start
  0.6 6.5 %copy-start.5 = (bf16[32,96,256]{2,1,0:T(8,128)(2,1)S(1)}, bf16[32,96,256]{2,1,0:T(8,128)(2,1)}, u32[]{:S(2)}) copy-start(bf16[32,96,256]{2,1,0:T(8,128)(2,1)} %x_ref.1) | copy-start | bytes 4718596
  0.7 6.5 %copy-start.12 = (f32[256]{0:T(256)S(1)}, f32[256]{0:T(256)}, u32[]{:S(2)}) copy-start(f32[256]{0:T(256)} %param.17) | copy-start | bytes 3076
  0.7 6.5 %copy-start.10 = (bf16[256,32]{0,1:T(8,128)(2,1)S(1)}, bf16[256,32]{0,1:T(8,128)(2,1)}, u32[]{:S(2)}) copy-start(bf16[256,32]{0,1:T(8,128)(2,1)} %param.21) | copy-start | bytes 49156
  0.7 6.2 %copy-start.9 = (s32[32,96]{1,0:T(8,128)S(1)}, s32[32,96]{1,0:T(8,128)}, u32[]{:S(2)}) copy-start(s32[32,96]{1,0:T(8,128)} %param.14) | copy-start | bytes 36868
  4.4 5.1 %copy-start.11 = (bf16[256,32]{0,1:T(8,128)(2,1)S(1)}, bf16[256,32]{0,1:T(8,128)(2,1)}, u32[]{:S(2)}) copy-start(bf16[256,32]{0,1:T(8,128)(2,1)} %param.20) | copy-start | bytes 49156
  8.5 2.3 %copy-start.8 = (bf16[1024,128]{1,0:T(8,128)(2,1)S(1)}, bf16[1024,128]{1,0:T(8,128)(2,1)}, u32[]{:S(2)}) copy-start(bf16[1024,128]{1,0:T(8,128)(2,1)} %param.22) | copy-start | bytes 786436
  9.5 54.1 %copy-start.3 = (bf16[128,8]{0,1:T(8,128)(2,1)S(1)}, bf16[128,8]{0,1:T(8,128)(2,1)}, u32[]{:S(2)}) copy-start(bf16[128,8]{0,1:T(8,128)(2,1)} %param.23) | copy-start | bytes 6148
  9.5 54.1 %copy-start.4 = (f32[128]{0:T(128)S(1)}, f32[128]{0:T(128)}, u32[]{:S(2)}) copy-start(f32[128]{0:T(128)} %param.19) | copy-start | bytes 1540
  92.1 0.6 copy-start.1
  92.8 0.6 copy-start.2
  93.4 84.0 %copy-start.6 = (bf16[32,96,256]{2,1,0:T(8,128)(2,1)S(1)}, bf16[32,96,256]{2,1,0:T(8,128)(2,1)}, u32[]{:S(2)}) copy-start(bf16[32,96,256]{2,1,0:T(8,128)(2,1)} %x_ref.1) | copy-start | bytes 4718596
  177.4 3.3 %copy-start.7 = (f32[48,96,128]{2,1,0:T(8,128)S(1)}, f32[48,96,128]{2,1,0:T(8,128)}, u32[]{:S(2)}) copy-start(f32[48,96,128]{2,1,0:T(8,128)} %get-tuple-element.19) | copy-start | bytes 7077892

commit v5 on v0

v5 whole, which is shorter than its diff:
```python
import jax
import jax.numpy as jnp
from jax import lax
from jax.experimental import pallas as pl
from jax.experimental.pallas import tpu as pltpu
from jax.sharding import PartitionSpec as P

EPSILON = 1e-05
CONTRACT_FIRST = (((0,), (0,)), ((), ()))
LAST_LAST = (((1,), (1,)), ((), ()))
HEAD_DIM = 32


def standardize_features(values):
    average = jnp.mean(values, axis=-1, keepdims=True)
    centred = values - average
    variance = jnp.mean(centred * centred, axis=-1, keepdims=True)
    return centred * lax.rsqrt(variance + EPSILON)


MESH = pl.DeviceIdType.MESH


def place():
    r, c = lax.axis_index("row"), lax.axis_index("col")
    return r, c


def row_of(y, zh, core):
    return y * 4 + zh * 2 + core


def remote(src, dst, send, recv, device):
    return pltpu.make_async_remote_copy(
        src_ref=src, dst_ref=dst, send_sem=send, recv_sem=recv, device_id=device, device_id_type=MESH
    )


def signal(barrier, device):
    pl.semaphore_signal(barrier, inc=1, device_id=device, device_id_type=MESH)


LOG2E = 1.4426950408889634


def whole_kernel(left_ref, right_ref, rrow_ref, rcol_ref, pair_ref, gain_ref, kron_ref, wd_ref, emb_ref, mask_ref,
                 again_ref, w_ref, out_ref, o_ref,
                 left_s, right_s, pair_s, rt_s, wb_s, mm_s, f_s, b_s, tile_s, w_s, block, ta, tb, tc, x_s, m_s, mb_s,
                 q_s, kt_s, v_s, g_s, bf_s, acc_s, out_s,
                 lsend, lrecv, gsend, zsend, zrecv, ysend, yrecv, fsend, frecv, own_sem, pin, pout,
                 asend, arecv, msend, mrecv, csem, csend, crecv, xsend, xrecv, l1, s1, r1, s2, r2, s3, r3, send, recv):
    r, c = place()
    chip, core = r // 2, r % 2
    y, zh, x, zl = r // 4, chip % 2, c // 2, c % 2
    seqs = right_ref.shape[0]
    opm = kron_ref.shape[0]
    parts, per = tile_s.shape[0], tile_s.shape[1]
    cols = pair_ref.shape[1]
    width = cols * opm
    half, length = x_s.shape[1], x_s.shape[2]
    heads, rows = bf_s.shape[0], bf_s.shape[1]
    spot = {"x": x, "y": y, "z": zh * 2 + zl}
    scale = float(HEAD_DIM) ** -0.5
    orders = ((ta, "xzy"), (tb, "yxz"), (tc, "zyx"))

    def rows_of(n):
        return pl.ds(pl.multiple_of(n * seqs, seqs), seqs)

    here = rows_of(r)
    partner = (chip * 2 + 1 - core, c)
    across = (row_of(y, 1 - zh, core), c)
    aside = (r, x * 2 + 1 - zl)
    mine = jnp.logical_and(chip == c, zh == zl)

    def own_left(h, j):
        return jnp.logical_and(mine, core == h) if j == 0 else False

    def unless(cond, f):
        if cond is False:
            f()
        else:
            pl.when(jnp.logical_not(cond))(f)

    def peer(dim, d):
        to = dict(spot)
        to[dim] = (spot[dim] + d) % 4
        return (row_of(to["y"], to["z"] // 2, core), to["x"] * 2 + to["z"] % 2)

    barrier = pltpu.get_barrier_semaphore()
    signal(barrier, across)
    for dim in "xyz":
        for d in range(1, 4):
            signal(barrier, peer(dim, d))
    for j in range(8):
        if j > 0:
            signal(barrier, (r, (c + j) % 8))
        signal(barrier, (partner[0], (c + j) % 8))
    for ys in range(4):
        for k in range(2):
            source = row_of(ys, zl, k)
            unless(jnp.logical_and(mine, r == source), lambda: signal(barrier, (source, chip)))
    pair_in = pltpu.make_async_copy(pair_ref, pair_s, pin.at[0])
    pair_in.start()
    pl.semaphore_wait(barrier, 33 - mine.astype(jnp.int32))

    over = remote(right_ref, right_s.at[here], zsend.at[0], zrecv.at[0], across)
    over.start()
    lefts = []
    for j in range(4):
        for h in range(2):
            to = (2 * c + h, ((x + j) % 4) * 2 + zh)
            cp = remote(left_ref.at[h], left_s.at[here], lsend.at[2 * j + h], lrecv.at[r], to)
            lefts.append((cp, h, j))
            unless(own_left(h, j), cp.start)
            if j == 0:

                @pl.when(own_left(h, j))
                def _():
                    pltpu.make_async_copy(left_ref.at[h], left_s.at[here], lrecv.at[r]).start()

    def along(n, d):
        blk = rows_of(row_of(y, (zh + n) % 2, core))
        src = right_ref if n == 0 else right_s.at[blk]
        return remote(src, right_s.at[blk], ysend.at[n * 4 + d], yrecv.at[n * 4 + d], (row_of((y + d) % 4, zh, core), c))

    def forward(n, d):
        blk = rows_of(row_of((y + 4 - d) % 4, (zh + n) % 2, core))
        src = right_ref if n == 0 and d == 0 else right_s.at[blk]
        return remote(src, right_s.at[blk], fsend.at[n * 4 + d], frecv.at[n * 4 + d], partner)

    def relay(d, k):
        source = row_of((y + 4 - d) % 4, zl, k)
        blk = left_s.at[rows_of(source)]
        return blk, source, remote(blk, blk, gsend.at[d * 2 + k], lrecv.at[source], aside)

    res = pl.ds(pl.multiple_of(c * cols, cols), cols)

    def moves(d):
        to = (r, (c + d) % 8)
        take = pl.ds(pl.multiple_of(to[1] * half, half), half)
        return (
            remote(emb_ref.at[take], x_s.at[0, :, res], asend.at[d], arecv.at[d], to),
            remote(mask_ref.at[to[1]], m_s.at[0, c], msend.at[d], mrecv.at[d], to),
        )

    def kept():
        return (
            pltpu.make_async_copy(
                emb_ref.at[pl.ds(pl.multiple_of(c * half, half), half)], x_s.at[0, :, res], arecv.at[0]
            ),
            pltpu.make_async_copy(mask_ref.at[c], m_s.at[0, c], mrecv.at[0]),
        )

    for d in (1, 3, 2):
        along(0, d).start()
    own = pltpu.make_async_copy(right_ref, right_s.at[here], own_sem.at[0])
    own.start()
    forward(0, 0).start()
    for d in (2, 4, 6):
        for cp in moves(d):
            cp.start()
    for cp in kept():
        cp.start()
    over.wait_recv()
    for d in (1, 3, 2):
        along(1, d).start()
    forward(1, 0).start()

    wb_s[...] = jnp.zeros_like(wb_s)

    def fill(b, carry):
        for i in range(2):
            wb_s[pl.ds(pl.multiple_of(b * 64 + i * 32, 32), 32), i * 128 : (i + 1) * 128] = kron_ref[b]
        return carry

    lax.fori_loop(0, opm, fill, 0)
    wide = w_ref.shape[1] // 4
    part = w_s.shape[1] // 4
    for n in range(4):
        w_s[:, n * part : (n + 1) * part] = w_ref[:, pl.ds(pl.multiple_of(n * wide + core * part, part), part)]

    for d in (0, 1, 3, 2):
        for k in range(2):
            blk, source, cp = relay(d, k)
            pltpu.make_async_copy(left_ref.at[0], blk, lrecv.at[source]).wait()
            cp.start()
        if d > 0:
            along(0, d).wait_recv()
            forward(0, d).start()
    for d in (1, 3, 2):
        along(1, d).wait_recv()
        forward(1, d).start()
    for d in (1, 3, 5, 7):
        for cp in moves(d):
            cp.start()

    chunk = 4 * cols
    for d in (0, 1, 3, 2):
        if d == 0:
            own.wait()
        for n in range(2):
            forward(n, d).wait_recv()
        ys = (y + 4 - d) % 4
        near = pl.ds(pl.multiple_of(ys * 4 * seqs, 4 * seqs), 4 * seqs)

        def flip(n, carry):
            at = pl.ds(pl.multiple_of(n * chunk, chunk), chunk)
            rt_s[at, near] = right_s[near, at].T
            return carry

        lax.fori_loop(0, opm // 4, flip, 0)
    for ys in range(4):
        for k in range(2):
            source = row_of(ys, 1 - zl, k)
            pltpu.make_async_copy(left_ref.at[0], left_s.at[rows_of(source)], lrecv.at[source]).wait()
    counts = lax.dot_general(
        right_s[:, width:], left_s[:, parts * per * 32 :], CONTRACT_FIRST, preferred_element_type=jnp.float32
    )[:cols, : parts * per]
    f_s[...] = rcol_ref[...] * rrow_ref[...] / (counts + 0.001)
    pair_in.wait()

    lanes = tile_s.shape[2] // 2

    def swap(st):
        spot_rows = pl.ds(pl.multiple_of(core * per, per), per)
        give = tile_s.at[st, :, pl.ds(pl.multiple_of((1 - core) * lanes, lanes), lanes)]
        keep = tile_s.at[st, :, pl.ds(pl.multiple_of(core * lanes, lanes), lanes)]
        return (
            pltpu.make_async_copy(keep, block.at[st, spot_rows], csem.at[st]),
            remote(give, block.at[st, spot_rows], csend.at[st], crecv.at[st], partner),
        )

    def one(st, o, d):
        out, dims = orders[o]
        slot = out.at[st, spot[dims[2]], spot[dims[1]], spot[dims[0]]]
        piece = block.at[st, :, pl.ds(o * 128, 128)]
        if d == 0:
            return pltpu.make_async_copy(piece, slot, l1.at[st * 3 + o])
        at = (st * 3 + o) * 4 + d
        return remote(piece, slot, s1.at[at], r1.at[at], peer(dims[0], d))

    def two(st, o, d):
        out, dims = orders[o]
        slot = out.at[st, spot[dims[2]], spot[dims[1]]]
        at = (st * 3 + o) * 4 + d
        return remote(slot, slot, s2.at[at], r2.at[at], peer(dims[1], d))

    def three(st, o, e, d):
        out, dims = orders[o]
        slot = out.at[st, spot[dims[2]], (spot[dims[1]] + 4 - e) % 4]
        at = (st * 3 + o) * 16 + e * 4 + d
        return remote(slot, slot, s3.at[at], r3.at[at], peer(dims[2], d))

    def begin(st):
        for cp in swap(st):
            cp.start()

    def first(st):
        cps = swap(st)
        cps[0].wait()
        cps[1].wait_recv()
        for o in range(3):
            for d in range(4):
                one(st, o, d).start()

    def middle(st):
        for o in range(3):
            for d in range(4):
                if d == 0:
                    one(st, o, d).wait()
                else:
                    one(st, o, d).wait_recv()
            for d in range(1, 4):
                two(st, o, d).start()
            for d in range(1, 4):
                three(st, o, 0, d).start()

    def last(st):
        for e in range(1, 4):
            for o in range(3):
                two(st, o, e).wait_recv()
                for d in range(1, 4):
                    three(st, o, e, d).start()

    group = per // 4

    def outer(st):
        def body(n, carry):
            at = pl.multiple_of(n * chunk, chunk)
            m = jnp.dot(
                rt_s[pl.ds(at, chunk), :], left_s[:, st * per * 32 : (st + 1) * per * 32],
                preferred_element_type=jnp.float32,
            )
            low = lax.broadcasted_iota(jnp.int32, (1, 128), 1) < 64
            for bb in range(2):
                to = pl.ds(pl.multiple_of((n * 2 + bb) * 128, 128), 128)
                for g in range(group):
                    m0, m1 = [
                        m[(2 * bb + k) * cols : (2 * bb + k + 1) * cols, g * 128 : (g + 1) * 128] for k in range(2)
                    ]
                    lo = jnp.where(low, m0, pltpu.roll(m1, 64, 1)).astype(jnp.bfloat16)
                    hi = jnp.where(low, pltpu.roll(m0, 64, 1), m1).astype(jnp.bfloat16)
                    mm_s[(2 * g) * cols : (2 * g + 1) * cols, to] = lo
                    mm_s[(2 * g + 1) * cols : (2 * g + 2) * cols, to] = hi
            return carry

        lax.fori_loop(0, opm // 4, body, 0)

    def mix(st):
        update = jnp.dot(mm_s[...], wb_s[...], preferred_element_type=jnp.float32)
        for g in range(2 * group):
            for ii in range(2):
                i = 2 * g + ii
                at = st * per + i
                u = update[g * cols : (g + 1) * cols, ii * 128 : (ii + 1) * 128]
                v = pair_s[at] + u * f_s[:, at : at + 1]
                pair_s[at] = v
                v = (standardize_features(v) * gain_ref[...]).astype(jnp.bfloat16)
                b_s[:, i, :] = lax.dot_general(wd_ref[...], v, LAST_LAST, preferred_element_type=jnp.float32)
        tile_s[st] = jnp.concatenate([b_s[h] for h in range(2 * heads)], axis=1).astype(jnp.bfloat16)

    def pair_back(st):
        at = pl.ds(st * per, per)
        return pltpu.make_async_copy(pair_s.at[at], out_ref.at[at], pout.at[st])

    outer(0)
    mix(0)
    begin(0)
    pair_back(0).start()
    outer(1)
    first(0)
    mix(1)
    middle(0)
    begin(1)
    pair_back(1).start()
    outer(2)
    last(0)
    first(1)
    mix(2)
    middle(1)
    begin(2)
    pair_back(2).start()

    for d in range(1, 8):
        for cp in moves(d):
            cp.wait_recv()
    for cp in kept():
        cp.wait()
    xs = remote(x_s.at[0], x_s.at[1], xsend.at[0], xrecv.at[0], partner)
    ms = remote(m_s.at[0], m_s.at[1], xsend.at[1], xrecv.at[1], partner)
    xs.start()
    ms.start()

    def project(n):
        def body(b, carry):
            v = standardize_features(x_s[n, b].astype(jnp.float32))
            v = (v * again_ref[...]).astype(jnp.bfloat16)
            at = n * half + b
            both = jnp.dot(v, w_s[...], preferred_element_type=jnp.float32).astype(jnp.bfloat16)
            q, k, v, g = [both[:, i * part : (i + 1) * part] for i in range(4)]
            for st in range(parts):
                pick = [slice((i * parts + st) * per, (i * parts + st + 1) * per) for i in range(rows // per)]
                q_s[at, st] = jnp.concatenate([q[p] for p in pick], axis=0)
                g_s[at, st] = jnp.concatenate([g[p] for p in pick], axis=0)
            v_s[at] = v
            kt_s[at] = k.T
            return carry

        lax.fori_loop(0, half, body, 0)
        for b in range(half):
            line = jnp.concatenate([m_s[n, cc, b : b + 1, :cols] for cc in range(8)], axis=1)
            mb_s[n * half + b] = (1e9 / scale) * (line - 1.0)

    first(2)
    last(1)
    project(0)
    middle(2)
    xs.wait_recv()
    ms.wait_recv()
    project(1)

    def attend(st, carry):
        for o in range(3):
            for e in range(4):
                for d in range(1, 4):
                    out, dims = orders[o]
                    at = (st * 3 + o) * 16 + e * 4 + d
                    slot = out.at[st, (spot[dims[2]] + 4 - d) % 4, (spot[dims[1]] + 4 - e) % 4]
                    remote(slot, slot, s3.at[at], r3.at[at], peer(dims[2], d)).wait_recv()

        def assemble(p, carry):
            yy, zz = p // 2, p % 2
            pieces = []
            for cc in range(8):
                xx, z = cc // 2, zz * 2 + cc % 2
                pieces.append(
                    jnp.concatenate([ta[st, yy, z, xx], tb[st, z, xx, yy], tc[st, xx, yy, z]], axis=1)
                )
            for h in range(heads):
                line = jnp.concatenate([piece[:, h * cols : (h + 1) * cols] for piece in pieces], axis=1)
                bf_s[h, pl.ds(pl.multiple_of(p * 2 * per, 2 * per), 2 * per), :] = line.astype(jnp.float32) * (
                    1.0 / scale
                )
            return carry

        lax.fori_loop(0, 8, assemble, 0)

        def batch(n, carry):
            def one_head(h, carry):
                @pl.when(jnp.logical_and(st == 0, jnp.logical_and(n == 0, h == 1)))
                def _():
                    last(2)

                head = lax.broadcasted_iota(jnp.int32, (1, part), 1) // HEAD_DIM
                mine_f = jnp.where(head == h, 1.0, 0.0)
                its = mine_f.astype(jnp.bfloat16)
                other = (1.0 - mine_f).astype(jnp.bfloat16)
                for b in range(half):
                    at = n * half + b
                    q = q_s[at, st] * its
                    s = jnp.dot(q, kt_s[at], preferred_element_type=jnp.float32) + bf_s[h] + mb_s[at]
                    top = jnp.max(s, axis=1, keepdims=True)
                    p = jnp.exp2(((s - top) * (scale * LOG2E)).astype(jnp.bfloat16))
                    w = jnp.dot(p, v_s[at] * its + other, preferred_element_type=jnp.float32)
                    mixed = w / pltpu.roll(w, HEAD_DIM, 1)
                    acc_s[b] = jnp.where(mine_f > 0.0, mixed, acc_s[b])
                return carry

            lax.fori_loop(0, heads, one_head, 0)

            def gate(b, carry):
                g = g_s[n * half + b, st].astype(jnp.float32)
                gated = (acc_s[b] * jax.nn.sigmoid(g)).astype(jnp.bfloat16)
                for p in range(8):
                    for k in range(2):
                        at = (p * 2 + k) * per
                        out_s[st, n, p, b, k] = gated[at : at + per]
                return carry

            lax.fori_loop(0, half, gate, 0)
            for j in range(8):
                p = (c + j) % 8
                src = out_s.at[st, n, p]
                dst = o_ref.at[core, pl.ds(pl.multiple_of(c * half, half), half), :, st]
                arrived = recv.at[st * 16 + c * 2 + core]
                row = jnp.where(n == 0, r, partner[0])
                cp = remote(src, dst, send.at[(st * 2 + n) * 8 + p], arrived, (row, p))
                if j == 0:

                    @pl.when(n > 0)
                    def _():
                        cp.start()

                    @pl.when(n == 0)
                    def _():
                        pltpu.make_async_copy(src, dst, arrived).start()
                else:
                    cp.start()
            return carry

        return lax.fori_loop(0, 2, batch, carry)

    lax.fori_loop(0, parts, attend, 0)

    over.wait_send()
    for cp, h, j in lefts:
        unless(own_left(h, j), cp.wait_send)
    for d in range(4):
        for k in range(2):
            relay(d, k)[2].wait_send()
    for n in range(2):
        for d in range(4):
            forward(n, d).wait_send()
            if d > 0:
                along(n, d).wait_send()
    for d in range(1, 8):
        for cp in moves(d):
            cp.wait_send()
    xs.wait_send()
    ms.wait_send()

    def close(st, carry):
        swap(st)[1].wait_send()
        pair_back(st).wait()
        for cs in range(8):
            for k in range(2):
                pltpu.make_async_copy(
                    out_s.at[0, 0, 0], o_ref.at[k, pl.ds(cs * half, half), :, st], recv.at[st * 16 + cs * 2 + k]
                ).wait()
        for n in range(2):
            for j in range(8):
                p = (c + j) % 8
                if n == 0 and j == 0:
                    continue
                row = r if n == 0 else partner[0]
                remote(
                    out_s.at[st, n, p], o_ref.at[core, pl.ds(pl.multiple_of(c * half, half), half), :, st],
                    send.at[(st * 2 + n) * 8 + p], recv.at[0], (row, p),
                ).wait_send()
        for o in range(3):
            for d in range(1, 4):
                one(st, o, d).wait_send()
                two(st, o, d).wait_send()
                for e in range(4):
                    three(st, o, e, d).wait_send()
        return carry

    for st in range(parts):
        close(st, 0)


def whole(left, right, rrow, rcol, pair, gain, kron, logit, emb, mask, again, w):
    rows, cols, channels = pair.shape
    home, _, depth = emb.shape
    seqs = home // 4
    half = seqs // 2
    total = 16 * home
    heads = logit.shape[1] // 2
    lanes = heads * HEAD_DIM
    length = 8 * cols
    width = kron.shape[0] // 32
    per = 16
    parts = rows // per
    block = length // parts
    kr = kron.reshape(width, width, channels).transpose(1, 0, 2)
    vmem = pl.BlockSpec(memory_space=pltpu.VMEM)
    hbm = pl.BlockSpec(memory_space=pl.ANY)
    dma = pltpu.SemaphoreType.DMA
    bf = lambda *s: pltpu.VMEM(s, jnp.bfloat16)
    fl = lambda *s: pltpu.VMEM(s, jnp.float32)
    pair_out, out = pl.pallas_call(
        whole_kernel,
        out_shape=(
            jax.ShapeDtypeStruct(pair.shape, jnp.float32),
            jax.ShapeDtypeStruct((2, home, 2, parts, per, lanes), jnp.bfloat16),
        ),
        in_specs=[vmem, vmem, vmem, vmem, hbm, vmem, vmem, vmem, hbm, vmem, vmem, vmem],
        out_specs=(hbm, hbm),
        scratch_shapes=[
            bf(total, left.shape[2]), bf(total, right.shape[1]), fl(*pair.shape),
            bf(cols * width, total), bf(64 * width, 2 * channels), bf(per // 2 * cols, 64 * width),
            fl(cols, rows), fl(2 * heads, per, cols), bf(parts, per, 2 * heads * cols),
            bf(depth, 4 * lanes), bf(parts, 2 * per, heads * cols),
            bf(parts, 4, 4, 4, 2 * per, 128), bf(parts, 4, 4, 4, 2 * per, 128), bf(parts, 4, 4, 4, 2 * per, 128),
            bf(2, half, length, depth), pltpu.VMEM((2,) + mask.shape, jnp.float32), fl(seqs, 1, length),
            bf(seqs, parts, block, lanes), bf(seqs, lanes, length), bf(seqs, length, lanes),
            bf(seqs, parts, block, lanes), fl(heads, block, length), fl(half, block, lanes),
            bf(parts, 2, 8, half, 2, per, lanes),
            dma((8,)), dma((16,)), dma((8,)), dma((1,)), dma((1,)), dma((8,)), dma((8,)), dma((8,)), dma((8,)),
            dma((1,)), dma((1,)), dma((3,)),
            dma((8,)), dma((8,)), dma((8,)), dma((8,)), dma((3,)), dma((3,)), dma((3,)), dma((2,)), dma((2,)),
            dma((9,)), dma((36,)), dma((36,)), dma((36,)), dma((36,)), dma((144,)), dma((144,)),
            dma((48,)), dma((48,)),
        ],
        compiler_params=pltpu.CompilerParams(
            vmem_limit_bytes=60 << 20, collective_id=1, has_side_effects=True
        ),
        name="whole",
    )(left, right, rrow.reshape(1, rows), rcol.reshape(cols, 1), pair, gain.reshape(1, channels), kr, logit.T, emb, mask,
      again.reshape(1, depth), w)
    return pair_out, out.reshape(2, home, cols, lanes)


def shards(
    aligned_family_embedding,
    aligned_slot_available,
    chain_site_available,
    duo_embedding,
    averaging_layernorm_stretch,
    lineup_layernorm_stretch,
    duo_layernorm_stretch,
    lefthand_linear_kernel,
    righthand_linear_kernel,
    kronecker_linear_kernel,
    duo_logit_kernel,
    asker_lookup_sigmoid_kernel,
    closing_linear_kernel,
):
    homolog_number, amino_position_number, discarded_carry = aligned_family_embedding.shape
    res_rows = duo_embedding.shape[0]
    opm_width = lefthand_linear_kernel.shape[1]
    head_count = duo_logit_kernel.shape[1]
    inner_width = closing_linear_kernel.shape[0]
    row_index = lax.axis_index("row")
    col_index = lax.axis_index("col")
    standardized_features = standardize_features(aligned_family_embedding.astype(jnp.float32))
    availability_real = aligned_slot_available.astype(jnp.float32)
    half_rows = res_rows
    opm_input = (standardized_features * averaging_layernorm_stretch).astype(jnp.bfloat16)
    left = jnp.einsum("src,ca->sra", opm_input, lefthand_linear_kernel, preferred_element_type=jnp.float32)
    left = (left * availability_real[:, :, None]).astype(jnp.bfloat16)
    left = left.reshape(homolog_number, 2, half_rows * opm_width).transpose(1, 0, 2)
    left_mask = availability_real.reshape(homolog_number, 2, half_rows).transpose(1, 0, 2)
    left_mask = jnp.pad(left_mask, ((0, 0), (0, 0), (0, 128 - half_rows))).astype(jnp.bfloat16)
    left = jnp.concatenate([left, left_mask], axis=2)
    right = jnp.einsum("src,ca->sar", opm_input, righthand_linear_kernel, preferred_element_type=jnp.float32)
    right = (right * availability_real[:, None, :]).astype(jnp.bfloat16)
    right_mask = jnp.pad(availability_real, ((0, 0), (0, 128 - amino_position_number))).astype(jnp.bfloat16)
    right = jnp.concatenate([right.reshape(homolog_number, -1), right_mask], axis=1)
    mask_out = jnp.pad(
        availability_real.reshape(8, homolog_number // 8, amino_position_number),
        ((0, 0), (0, 8 - homolog_number // 8), (0, 128 - amino_position_number)),
    )
    residue_float = chain_site_available.astype(jnp.float32)
    residue_rows = lax.dynamic_slice_in_dim(residue_float, row_index * res_rows, res_rows)
    residue_cols = lax.dynamic_slice_in_dim(
        residue_float, col_index * amino_position_number, amino_position_number
    )
    lanes = inner_width // 2
    duo_after_averaging, gated = whole(
        left, right, residue_rows, residue_cols, duo_embedding, duo_layernorm_stretch, kronecker_linear_kernel,
        duo_logit_kernel, aligned_family_embedding, mask_out, lineup_layernorm_stretch, asker_lookup_sigmoid_kernel,
    )
    closing = closing_linear_kernel.reshape(2, lanes, -1)
    summed_increment = jnp.einsum("hsqd,hdc->sqc", gated, closing, preferred_element_type=jnp.float32)
    refreshed_family_embedding = (
        aligned_family_embedding.astype(jnp.float32) + summed_increment
    ).astype(jnp.bfloat16)
    return (refreshed_family_embedding, duo_after_averaging)


def solution(mesh):
    placed = (
        P("row", "col", None),
        P("row", "col"),
        P(),
        P("row", "col", None),
        P(),
        P(),
        P(),
        P(),
        P(),
        P(),
        P(),
        P(),
        P(),
    )
    return jax.shard_map(
        shards,
        mesh=mesh,
        in_specs=placed,
        out_specs=(P("row", "col", None), P("row", "col", None)),
        check_vma=False,
    )
```

time: 557 us -> 191 us (0.34)
  Pallas kernels: 0 us -> 172 us
  waiting for transfers between devices: 154 us -> 0 us
  matrix products: 152 us -> 5.8 us
  local copies, waits for them, and re-layouts: 105 us -> 6.48 us
  other arithmetic: 68 us -> 5.17 us
  blocking collectives: 38.7 us -> 0 us
  starting transfers between devices: 21.1 us -> 0 us
  between operations: 14.2 us -> 0.82 us
    pallas_call x0 -> x1, Pallas kernels: none -> 172 us  [whole(): pl.pallas_call(whole_kernel, out_shape=(jax.ShapeDtypeStruct(pair.shape,...]
    dot_general x16 -> x3, matrix products: 152 us -> 5.8 us  [the longest x1 3.27 us: shards(): jnp.einsum('hsqd,hdc->sqc', gated, closing, preferred_element_type=jnp.fl...]
    all_gather x3 -> x0, waiting for transfers between devices: 99.4 us -> none  [the longest x1 43.3 us: shards(): bias_whole = lax.all_gather(bias_cols, 'row', axis=1, tiled=True)]
    all_to_all x3 -> x0, waiting for transfers between devices: 55 us -> none  [the longest x1 30.1 us: sent_together(): lax.all_to_all(both, axis, split_axis=split_dim, concat_axis=concat_dim,...]
    sub x4 -> x0, other arithmetic: 54.9 us -> none  [one_block(): exponent = jnp.exp(scores - highest)]
    reshape x8 -> x9, local copies, waits for them, and re-layouts: 47.3 us -> 3.22 us  [the longest x1 0.81 us: whole(): kr = kron.reshape(width, width, channels).transpose(1, 0, 2)]
    all_to_all x2 -> x0, blocking collectives: 38.7 us -> none  [the longest x1 23.8 us: shards(): lax.all_to_all(gated_whole, 'col', split_axis=1, concat_axis=0, tiled=True)]
    all_to_all x3 -> x0, starting transfers between devices: 20.8 us -> none  [the longest x1 8.78 us: shards(): lax.all_to_all(mask_wide, 'row', split_axis=1, concat_axis=0, tiled=True)]
  transfers between devices with their start and end apart: 6 -> 0, of which waited for: 5 -> 0; matrix products, arithmetic and copies ran while one was open for 6% -> 0% of each run, Pallas kernels for 0% -> 0%
where the time goes in v5:
time: 191 us; the launch traced here: 190 us
  Pallas kernels  172 us (90%)
  local copies, waits for them, and re-layouts  6.48 us (3%)
  matrix products  5.8 us (3%)
  other arithmetic  5.17 us (3%)
    pallas_call x1, Pallas kernels, whole(): pl.pallas_call(whole_kernel, out_shape=(jax.ShapeDtypeStruct(pair.shape,...  172 us

profile of v5, /device:TPU:1, one launch (start us, length us, event | category | flops | bytes accessed | tf_op | source)
XLA Modules:
  0.0 190.5 jit_solution(4191980163417470112)
XLA Ops:
  0.6 0.0 copy-start
  0.6 0.0 copy-start.1
  0.7 0.0 copy-start.8
  0.7 0.0 copy-start.6
  0.7 0.0 copy-start.5
  0.7 0.8 copy-done
  1.5 0.7 convert_element_type.39
  2.2 0.1 dynamic-slice_bitcast_fusion
  2.3 0.6 dynamic-slice_bitcast_fusion.1.rrow_ref
  2.9 2.0 %convert_reduce_fusion = f32[32,96]{1,0:T(8,128)S(1)} fusion(bf16[32,96,256]{2,1,0:T(8,128)(2,1)} %emb_ref.1), kind=kLoop, calls=%fused_computation.2 | loop fusion | flops 1569792 | bytes 1585152 | tf_op jit(solution)/shard_map/reduce_sum | solution.py:15
  5.0 0.0 copy-done.1
  5.0 1.0 fusion.2
  6.0 0.0 copy-done.5
  6.1 0.1 reshape.54
  6.2 0.6 pad.16.mask_ref
  6.8 0.0 copy-start.7
  6.8 0.7 copy.22.rcol_ref
  7.5 0.0 copy-done.8
  7.5 0.0 copy-done.6
  7.5 1.3 fusion.8
  8.8 0.0 copy-start.4
  8.8 0.3 reshape.55
  9.1 0.7 fusion.14.right_ref
  9.8 0.0 copy-done.7
  9.8 1.3 fusion.6
  11.1 0.0 copy-done.4
  11.1 0.8 copy.29
  11.9 0.4 copy.18
  12.2 0.6 reshape.53
  12.9 0.7 fusion.13.left_ref
  13.6 0.0 copy-start.2
  13.6 172.2 %whole.1 = (f32[48,96,128]{2,1,0:T(8,128)}, bf16[2,32,2,3,16,128]{5,4,3,2,1,0:T(8,128)(2,1)}) custom-call(bf16[2,32,1664]{2,1,0:T(8,128)(2,1)} %fusion.13.left_ref, bf16[32,3200]{1,0:T(8,128)(2,1)} %fusion.14.right_ref, f32[1,48]{1,0:T(1,128)} %dynamic-slice_bitcast_fusion.1.rrow_ref, f32[96,1]{1,0:T(8,128)} %copy.22.rcol_ref, f32[48,96,128]{2,1,0:T(8,128)} %pair_ref.1, ...), custom_call_target="tpu_custom_call" | custom-call | tf_op jit(solution)/shard_map/whole/pallas_call | solution.py:531
  185.8 0.0 copy-done.2
  185.8 0.0 copy-start.3
  185.8 3.3 %fusion.5 = bf16[32,96,256]{2,1,0:T(8,128)(2,1)} fusion(bf16[32,96,256]{2,1,0:T(8,128)(2,1)S(1)} %copy-done.2, bf16[2,32,96,128]{3,2,1,0:T(8,128)(2,1)} %bitcast.37, bf16[2,128,256,1]{2,1,3,0:T(8,128)(2,1)S(1)} %bitcast.36), kind=kOutput, calls=%fused_computation.8 | convolution fusion | flops 405012480 | bytes 4849664 | tf_op jit(solution)/shard_map/hsqd,hdc->sqc/dot_general | solution.py:615
  189.1 0.0 copy-done.3
  189.1 1.4 copy.33
  (5 shorter events, 0.1 us)
Async XLA Ops:
  0.6 0.9 copy-start
  0.6 4.3 %copy-start.1 = (bf16[32,96,256]{2,1,0:T(8,128)(2,1)S(1)}, bf16[32,96,256]{2,1,0:T(8,128)(2,1)}, u32[]{:S(2)}) copy-start(bf16[32,96,256]{2,1,0:T(8,128)(2,1)} %emb_ref.1) | copy-start | bytes 4718596
  0.7 6.8 %copy-start.8 = (f32[256]{0:T(256)S(1)}, f32[256]{0:T(256)}, u32[]{:S(2)}) copy-start(f32[256]{0:T(256)} %param.17) | copy-start | bytes 3076
  0.7 6.8 %copy-start.6 = (bf16[256,32]{0,1:T(8,128)(2,1)S(1)}, bf16[256,32]{0,1:T(8,128)(2,1)}, u32[]{:S(2)}) copy-start(bf16[256,32]{0,1:T(8,128)(2,1)} %param.21) | copy-start | bytes 49156
  0.7 5.4 %copy-start.5 = (s32[32,96]{1,0:T(8,128)S(1)}, s32[32,96]{1,0:T(8,128)}, u32[]{:S(2)}) copy-start(s32[32,96]{1,0:T(8,128)} %param.14) | copy-start | bytes 36868
  6.8 3.0 %copy-start.7 = (bf16[256,32]{0,1:T(8,128)(2,1)S(1)}, bf16[256,32]{0,1:T(8,128)(2,1)}, u32[]{:S(2)}) copy-start(bf16[256,32]{0,1:T(8,128)(2,1)} %param.20) | copy-start | bytes 49156
  8.8 2.3 %copy-start.4 = (bf16[1024,128]{1,0:T(8,128)(2,1)S(1)}, bf16[1024,128]{1,0:T(8,128)(2,1)}, u32[]{:S(2)}) copy-start(bf16[1024,128]{1,0:T(8,128)(2,1)} %param.22) | copy-start | bytes 786436
  13.6 172.2 %copy-start.2 = (bf16[32,96,256]{2,1,0:T(8,128)(2,1)S(1)}, bf16[32,96,256]{2,1,0:T(8,128)(2,1)}, u32[]{:S(2)}) copy-start(bf16[32,96,256]{2,1,0:T(8,128)(2,1)} %emb_ref.1) | copy-start | bytes 4718596
  185.8 3.3 %copy-start.3 = (f32[48,96,128]{2,1,0:T(8,128)S(1)}, f32[48,96,128]{2,1,0:T(8,128)}, u32[]{:S(2)}) copy-start(f32[48,96,128]{2,1,0:T(8,128)} %get-tuple-element.11) | copy-start | bytes 7077892

commit v6 on v4

--- a/solution.py
+++ b/solution.py
@@ -40,7 +40,7 @@
     pl.semaphore_signal(barrier, inc=1, device_id=device, device_id_type=MESH)
 
 
-def spread_kernel(left_ref, right_ref, left_out, right_out, lsend, lrecv, gsend, zsend, zrecv, ysend, yrecv, fsend,
+def spread_kernel(left_ref, right_ref, emb_ref, left_out, right_out, x_out, xsend, xrecv, lsend, lrecv, gsend, zsend, zrecv, ysend, yrecv, fsend,
                   frecv, own_sem):
     r, c = place()
     chip, core = r // 2, r % 2
@@ -75,7 +75,16 @@
         for k in range(2):
             source = row_of(ys, zl, k)
             unless(jnp.logical_and(mine, r == source), lambda: signal(barrier, (source, chip)))
-    pl.semaphore_wait(barrier, 14 - mine.astype(jnp.int32))
+    for d in range(1, 4):
+        signal(barrier, (r, ((x + d) % 4) * 2 + zl))
+    pl.semaphore_wait(barrier, 17 - mine.astype(jnp.int32))
+    half = x_out.shape[1]
+
+    def move(d):
+        xd = (x + d) % 4
+        take = pl.ds(pl.multiple_of((xd * 2 + zl) * half, half), half)
+        return remote(emb_ref.at[take], x_out.at[x], xsend.at[d], xrecv.at[d], (r, xd * 2 + zl))
+
 
     over = remote(right_ref, right_out.at[here], zsend.at[0], zrecv.at[0], across)
     over.start()
@@ -108,6 +117,8 @@
     own = pltpu.make_async_copy(right_ref, right_out.at[here], own_sem.at[0])
     own.start()
     forward(0, 0).start()
+    for d in (1, 3, 2):
+        move(d).start()
     over.wait_recv()
     for d in (1, 3, 2):
         along(1, d).start()
@@ -140,6 +151,8 @@
             if d > 0:
                 along(n, d).wait_send()
     over.wait_send()
+    for d in range(1, 4):
+        move(d).wait()
     for cp, h, j in lefts:
         unless(own_left(h, j), cp.wait_send)
     for d in range(4):
@@ -147,7 +160,7 @@
             relay(d, k)[2].wait_send()
 
 
-def spread(left, right):
+def spread(left, right, emb):
     seqs = right.shape[0]
     vmem = pl.BlockSpec(memory_space=pltpu.VMEM)
     hbm = pl.BlockSpec(memory_space=pl.ANY)
@@ -157,22 +170,24 @@
         out_shape=(
             jax.ShapeDtypeStruct((16 * seqs, left.shape[2]), jnp.bfloat16),
             jax.ShapeDtypeStruct((16 * seqs, right.shape[1]), jnp.bfloat16),
+            jax.ShapeDtypeStruct((4, seqs // 8) + emb.shape[1:], jnp.bfloat16),
         ),
-        in_specs=[vmem, vmem],
-        out_specs=(hbm, hbm),
+        in_specs=[vmem, vmem, hbm],
+        out_specs=(hbm, hbm, hbm),
         scratch_shapes=[
+            dma((4,)), dma((4,)),
             dma((8,)), dma((16,)), dma((8,)), dma((1,)), dma((1,)), dma((8,)), dma((8,)), dma((8,)), dma((8,)), dma((1,))
         ],
         compiler_params=pltpu.CompilerParams(collective_id=1, has_side_effects=True),
         name="spread",
-    )(left, right)
+    )(left, right, emb)
 
 
 LOG2E = 1.4426950408889634
 
 
-def attn_kernel(tile_ref, xin_ref, mask_ref, gain_ref, w_ref, o_ref, w_s, block, ta, tb, tc, x_s, m_s, mb_s, q_s, kt_s, v_s, g_s, bf_s, acc_s, out_s,
-                csem, csend, crecv, l1, s1, r1, s2, r2, s3, r3, send, recv):
+def attn_kernel(tile_ref, emb_ref, near_ref, far_ref, mask_ref, gain_ref, w_ref, o_ref, w_s, block, ta, tb, tc, x_s, m_s, mb_s, q_s, kt_s, v_s, g_s, bf_s, acc_s, out_s,
+                lsem, csem, csend, crecv, l1, s1, r1, s2, r2, s3, r3, send, recv):
     r, c = place()
     chip, core = r // 2, r % 2
     spot = {"x": c // 2, "y": r // 4, "z": (chip % 2) * 2 + c % 2}
@@ -205,14 +220,22 @@
     keep = tile_ref.at[:, pl.ds(pl.multiple_of(core * lanes, lanes), lanes)]
     own = pltpu.make_async_copy(keep, block.at[here], csem.at[0])
     own.start()
-    xl = pltpu.make_async_copy(xin_ref, x_s.at[0], csem.at[1])
-    xl.start()
+    locals_ = []
+    for d in range(8):
+        xd, zd = (c // 2 + d // 2) % 4, (c + d) % 2
+        if d == 0:
+            src = emb_ref.at[pl.ds(pl.multiple_of(c * half, half), half)]
+        else:
+            src = (far_ref if d % 2 else near_ref).at[xd]
+        spot_cols = pl.ds(pl.multiple_of((xd * 2 + zd) * cols, cols), cols)
+        locals_.append(pltpu.make_async_copy(src, x_s.at[0, :, spot_cols], lsem.at[d]))
+        locals_[d].start()
     ml = pltpu.make_async_copy(mask_ref, m_s.at[0], csem.at[2])
     ml.start()
     pl.semaphore_wait(barrier, 25)
     swap = remote(give, block.at[here], csend.at[0], crecv.at[0], partner)
     swap.start()
-    xs = remote(xin_ref, x_s.at[1], csend.at[1], crecv.at[1], partner)
+    xs = remote(x_s.at[0], x_s.at[1], csend.at[1], crecv.at[1], partner)
     ms = remote(mask_ref, m_s.at[1], csend.at[2], crecv.at[2], partner)
     own.wait()
     swap.wait_recv()
@@ -261,6 +284,8 @@
         for o in range(3):
             for d in range(4):
                 one(hf, o, d).start()
+    for cp in locals_:
+        cp.wait()
     xs.start()
     ms.start()
 
@@ -269,7 +294,7 @@
     for n in range(4):
         w_s[:, n * part : (n + 1) * part] = w_ref[:, pl.ds(pl.multiple_of(n * width + core * part, part), part)]
 
-    def project(n):
+    def project(n, lo, hi):
         def body(b, carry):
             x = standardize_features(x_s[n, b].astype(jnp.float32))
             x = (x * gain_ref[...]).astype(jnp.bfloat16)
@@ -287,20 +312,24 @@
             kt_s[at] = k.T
             return carry
 
-        lax.fori_loop(0, half, body, 0)
+        lax.fori_loop(lo, hi, body, 0, unroll=2)
+
+    def mask_lines(n):
         for b in range(half):
             line = jnp.concatenate([m_s[n, cc, b : b + 1, :cols] for cc in range(8)], axis=1)
             mb_s[n * half + b] = (1e9 / scale) * (line - 1.0)
 
+    project(0, 0, 2)
     middle(0)
-    xl.wait()
-    ml.wait()
-    project(0)
+    project(0, 2, half)
     last(0)
     middle(1)
+    ml.wait()
+    mask_lines(0)
     xs.wait_recv()
     ms.wait_recv()
-    project(1)
+    mask_lines(1)
+    project(1, 0, half)
 
     def block_of_rows(hf, carry):
         for o in range(3):
@@ -417,8 +446,9 @@
     ms.wait_send()
 
 
-def attention(tile, x, mask, gain, w, cols, home):
-    half, length, channels = x.shape
+def attention(tile, emb, near, far, mask, gain, w):
+    home, cols, channels = emb.shape
+    half, length = home // 8, 8 * cols
     seqs = 2 * half
     lanes = w.shape[1] // 8
     heads = lanes // HEAD_DIM
@@ -431,13 +461,13 @@
     out = pl.pallas_call(
         attn_kernel,
         out_shape=jax.ShapeDtypeStruct((2, home, 3, 2, sub, lanes), jnp.bfloat16),
-        in_specs=[vmem, hbm, vmem, vmem, vmem],
+        in_specs=[vmem, hbm, hbm, hbm, vmem, vmem, vmem],
         out_specs=hbm,
         scratch_shapes=[
             pltpu.VMEM((channels, 4 * lanes), jnp.bfloat16),
             pltpu.VMEM((2 * tile.shape[0], tile.shape[1] // 2), jnp.bfloat16),
             table, table, table,
-            pltpu.VMEM((2,) + x.shape, jnp.bfloat16),
+            pltpu.VMEM((2, half, length, channels), jnp.bfloat16),
             pltpu.VMEM((2,) + mask.shape, jnp.float32),
             pltpu.VMEM((seqs, 1, length), jnp.float32),
             pltpu.VMEM((seqs, 2, rows, lanes), jnp.bfloat16),
@@ -447,7 +477,7 @@
             pltpu.VMEM((heads, rows, length), jnp.float32),
             pltpu.VMEM((half, rows, lanes), jnp.float32),
             pltpu.VMEM((2, 2, 8, half, 3, sub, lanes), jnp.bfloat16),
-            dma((3,)), dma((3,)), dma((3,)), dma((6,)),
+            dma((8,)), dma((3,)), dma((3,)), dma((3,)), dma((6,)),
             dma((24,)), dma((24,)), dma((24,)), dma((24,)), dma((96,)), dma((96,)),
             dma((32,)), dma((32,)),
         ],
@@ -455,7 +485,7 @@
             vmem_limit_bytes=56 << 20, collective_id=3, has_side_effects=True
         ),
         name="attn",
-    )(tile, x, mask, gain.reshape(1, channels), w)
+    )(tile, emb, near, far, mask, gain.reshape(1, channels), w)
     return out.reshape(2, home, cols, lanes)
 
 
@@ -469,25 +499,20 @@
     heads = wd_ref.shape[0]
     group = per // 4
     chunk = 4 * cols
-    half = x_out.shape[0]
+    half = x_out.shape[1]
     width = cols * opm
-    here = pl.ds(pl.multiple_of(c * cols, cols), cols)
-
-    def moves(d):
-        to = (r, (c + d) % 8)
-        block = pl.ds(pl.multiple_of(to[1] * half, half), half)
-        return (
-            remote(x_ref.at[block], x_out.at[:, here], xsend.at[d], xrecv.at[d], to),
-            remote(mk_ref.at[to[1]], m_out.at[c], msend.at[d], mrecv.at[d], to),
-        )
+
+    def move(d):
+        to = ((c // 2 + d) % 4) * 2 + 1 - c % 2
+        block = pl.ds(pl.multiple_of(to * half, half), half)
+        return remote(x_ref.at[block], x_out.at[c // 2], xsend.at[d], xrecv.at[d], (r, to))
+
+    def note(d):
+        to = (c + d) % 8
+        return remote(mk_ref.at[to], m_out.at[c], msend.at[d], mrecv.at[d], (r, to))
 
     def kept():
-        return (
-            pltpu.make_async_copy(
-                x_ref.at[pl.ds(pl.multiple_of(c * half, half), half)], x_out.at[:, here], xrecv.at[0]
-            ),
-            pltpu.make_async_copy(mk_ref.at[c], m_out.at[c], mrecv.at[0]),
-        )
+        return pltpu.make_async_copy(mk_ref.at[c], m_out.at[c], mrecv.at[0])
 
     @pl.when(step == 0)
     def _():
@@ -495,11 +520,11 @@
         for d in range(1, 8):
             signal(barrier, (r, (c + d) % 8))
         pl.semaphore_wait(barrier, 7)
+        for d in (0, 1, 3, 2):
+            move(d).start()
         for d in range(1, 8):
-            for cp in moves(d):
-                cp.start()
-        for cp in kept():
-            cp.start()
+            note(d).start()
+        kept().start()
         wb_s[...] = jnp.zeros_like(wb_s)
 
         def fill(b, carry):
@@ -553,11 +578,11 @@
 
     @pl.when(step == steps - 1)
     def _():
+        for d in range(4):
+            move(d).wait()
         for d in range(1, 8):
-            for cp in moves(d):
-                cp.wait()
-        for cp in kept():
-            cp.wait()
+            note(d).wait()
+        kept().wait()
 
 
 def opm(left, right, rrow, rcol, pair, gain, kron, logit, x, mk):
@@ -581,7 +606,7 @@
         out_shape=(
             jax.ShapeDtypeStruct(pair.shape, jnp.float32),
             jax.ShapeDtypeStruct((rows, heads * cols), jnp.bfloat16),
-            jax.ShapeDtypeStruct((x.shape[0] // 8, 8 * cols, x.shape[2]), jnp.bfloat16),
+            jax.ShapeDtypeStruct((4, x.shape[0] // 8) + x.shape[1:], jnp.bfloat16),
             jax.ShapeDtypeStruct(mk.shape, mk.dtype),
         ),
         in_specs=[
@@ -589,7 +614,7 @@
             pl.BlockSpec((seqs, 128), lambda i: (0, rows * width // 128)),
             whole(right), whole(rr), whole(rc),
             pl.BlockSpec((per, cols, channels), lambda i: (i, 0, 0)),
-            whole(gain), whole(w), whole(wd), whole(x), whole(mk),
+            whole(gain), whole(w), whole(wd), hbm, whole(mk),
         ],
         out_specs=(
             pl.BlockSpec((per, cols, channels), lambda i: (i, 0, 0)),
@@ -651,20 +676,20 @@
         availability_real.reshape(8, homolog_number // 8, amino_position_number),
         ((0, 0), (0, 8 - homolog_number // 8), (0, 128 - amino_position_number)),
     )
-    left_all, right_all = spread(left, right)
+    left_all, right_all, near_rows = spread(left, right, aligned_family_embedding)
     residue_float = chain_site_available.astype(jnp.float32)
     residue_rows = lax.dynamic_slice_in_dim(residue_float, row_index * res_rows, res_rows)
     residue_cols = lax.dynamic_slice_in_dim(
         residue_float, col_index * amino_position_number, amino_position_number
     )
-    duo_after_averaging, bias_tile, own_rows, own_mask = opm(
+    duo_after_averaging, bias_tile, far_rows, own_mask = opm(
         left_all, right_all, residue_rows, residue_cols, duo_embedding,
         duo_layernorm_stretch, kronecker_linear_kernel, duo_logit_kernel, aligned_family_embedding, mask_out,
     )
     lanes = inner_width // 2
     gated = attention(
-        bias_tile, own_rows, own_mask, lineup_layernorm_stretch, asker_lookup_sigmoid_kernel,
-        amino_position_number, homolog_number,
+        bias_tile, aligned_family_embedding, near_rows, far_rows, own_mask, lineup_layernorm_stretch,
+        asker_lookup_sigmoid_kernel,
     )
     closing = closing_linear_kernel.reshape(2, lanes, -1)
     summed_increment = jnp.einsum("hsqd,hdc->sqc", gated, closing, preferred_element_type=jnp.float32)

time: 182 us -> 177 us (0.973)
  Pallas kernels: 163 us -> 157 us
    pallas_call x1, Pallas kernels: 84 us -> 79.4 us  [attention(): pl.pallas_call(attn_kernel, out_shape=jax.ShapeDtypeStruct((2, home, 3, 2...]
    pallas_call x1, Pallas kernels: 28.5 us -> 26.4 us  [opm(): pl.pallas_call(opm_kernel, grid=(steps,), out_shape=(jax.ShapeDtypeStruct...]
    unnamed x27 -> x29, local copies, waits for them, and re-layouts: 3.55 us -> 4.42 us
where the time goes in v6:
time: 177 us
  Pallas kernels  157 us (89%)
  other arithmetic  6.58 us (4%)
  local copies, waits for them, and re-layouts  6.16 us (3%)
  matrix products  5.81 us (3%)
    pallas_call x1, Pallas kernels, attention(): pl.pallas_call(attn_kernel, out_shape=jax.ShapeDtypeStruct((2, home, 3, 2...  79.4 us
    pallas_call x1, Pallas kernels, spread(): pl.pallas_call(spread_kernel, out_shape=(jax.ShapeDtypeStruct((16 * seqs,...  51.5 us
    pallas_call x1, Pallas kernels, opm(): pl.pallas_call(opm_kernel, grid=(steps,), out_shape=(jax.ShapeDtypeStruct...  26.4 us
    unnamed x29, local copies, waits for them, and re-layouts  4.42 us

profile of v6, /device:TPU:1, one launch (start us, length us, event | category | flops | bytes accessed | tf_op | source)
XLA Modules:
  0.0 176.7 jit_solution(7652150547507207085)
XLA Ops:
  0.6 0.0 copy-start
  0.6 0.0 copy-start.6
  0.7 0.0 copy-start.13
  0.7 0.0 copy-start.11
  0.7 0.0 copy-start.10
  0.7 0.8 copy-done
  1.5 0.7 convert_element_type.39
  2.2 0.1 dynamic-slice_bitcast_fusion
  2.3 0.1 dynamic-slice_bitcast_fusion.1.rrow_ref
  2.4 2.0 %convert_reduce_fusion = f32[32,96]{1,0:T(8,128)S(1)} fusion(bf16[32,96,256]{2,1,0:T(8,128)(2,1)} %emb_ref.3), kind=kLoop, calls=%fused_computation.2 | loop fusion | flops 1569792 | bytes 1585152 | tf_op jit(solution)/shard_map/reduce_sum | solution.py:15
  4.4 0.0 copy-start.12
  4.4 2.5 %fusion.2 = f32[32,96]{1,0:T(8,128)S(1)} fusion(bf16[32,96,256]{2,1,0:T(8,128)(2,1)} %emb_ref.3, f32[32,96]{1,0:T(8,128)S(1)} %broadcast_multiply_fusion), kind=kLoop, calls=%fused_computation.5 | loop fusion | flops 3142656 | bytes 1597440 | tf_op jit(solution)/shard_map/reduce_sum | solution.py:17
  6.9 0.0 copy-done.10
  6.9 0.1 reshape.54
  7.0 0.1 copy.22.rcol_ref
  7.1 0.0 copy-done.6
  7.1 0.0 copy-done.13
  7.2 0.0 copy-done.11
  7.2 1.3 fusion.8
  8.5 0.0 copy-start.9
  8.5 0.3 reshape.55
  8.8 0.7 fusion.14.right_ref
  9.5 0.0 copy-done.12
  9.5 1.3 fusion.6
  10.8 0.0 copy-done.9
  10.8 0.0 copy-start.4
  10.8 0.0 copy-start.5
  10.8 0.1 copy.29
  10.9 0.4 copy.18
  11.3 0.6 reshape.53
  11.9 0.7 fusion.13.left_ref
  12.6 51.5 %spread.1 = (bf16[512,1664]{1,0:T(8,128)(2,1)}, bf16[512,3200]{1,0:T(8,128)(2,1)}, bf16[4,4,96,256]{3,2,1,0:T(8,128)(2,1)}) custom-call(bf16[2,32,1664]{2,1,0:T(8,128)(2,1)} %fusion.13.left_ref, bf16[32,3200]{1,0:T(8,128)(2,1)} %fusion.14.right_ref, bf16[32,96,256]{2,1,0:T(8,128)(2,1)} %emb_ref.3), custom_call_target="tpu_custom_call" | custom-call | tf_op jit(solution)/shard_map/spread/pallas_call | solution.py:168
  64.1 0.0 copy-done.4
  64.1 0.0 copy-done.5
  64.1 26.4 %opm.1 = (f32[48,96,128]{2,1,0:T(8,128)}, bf16[48,768]{1,0:T(8,128)(2,1)S(1)}, bf16[4,4,96,256]{3,2,1,0:T(8,128)(2,1)S(1)}, f32[8,8,128]{2,1,0:T(8,128)S(1)}) custom-call(bf16[512,1664]{1,0:T(8,128)(2,1)} %get-tuple-element.9.left_ref.lmask_ref, bf16[512,1664]{1,0:T(8,128)(2,1)} %get-tuple-element.9.left_ref.lmask_ref, ...), custom_call_target="tpu_custom_call" | custom-call | tf_op jit(solution)/shard_map/opm/pallas_call | solution.py:603
  90.5 0.0 copy-start.1
  90.5 0.9 copy-done.1
  91.4 0.0 copy-start.2
  91.4 0.6 copy-done.2
  92.0 0.0 copy-start.3
  92.0 0.6 copy-done.3
  92.6 0.0 copy-start.7
  92.6 79.4 %attn.1 = bf16[2,32,3,2,16,128]{5,4,3,2,1,0:T(8,128)(2,1)} custom-call(bf16[48,768]{1,0:T(8,128)(2,1)} %copy-done.2, bf16[32,96,256]{2,1,0:T(8,128)(2,1)} %emb_ref.3, bf16[4,4,96,256]{3,2,1,0:T(8,128)(2,1)} %get-tuple-element.12.near_ref, bf16[4,4,96,256]{3,2,1,0:T(8,128)(2,1)} %copy-done.1, f32[8,8,128]{2,1,0:T(8,128)} %copy-done.3, f32[1,256]{1,0:T(1,128)} %bitcast.45, ...), custom_call_target="tpu_custom_call" | custom-call | tf_op jit(solution)/shard_map/attn/pallas_call | solution.py:461
  172.1 0.0 copy-start.8
  172.1 0.0 copy-done.7
  172.1 3.3 %fusion.5 = bf16[32,96,256]{2,1,0:T(8,128)(2,1)} fusion(bf16[32,96,256]{2,1,0:T(8,128)(2,1)S(1)} %copy-done.7, bf16[2,32,96,128]{3,2,1,0:T(8,128)(2,1)} %bitcast.40, bf16[2,128,256,1]{2,1,3,0:T(8,128)(2,1)S(1)} %bitcast.36), kind=kOutput, calls=%fused_computation.8 | convolution fusion | flops 405012480 | bytes 4849664 | tf_op jit(solution)/shard_map/hsqd,hdc->sqc/dot_general | solution.py:695
  175.3 0.0 copy-done.8
  175.3 1.4 copy.33
  (6 shorter events, 0.1 us)
Async XLA Ops:
  0.6 0.9 copy-start
  0.6 6.5 %copy-start.6 = (bf16[32,96,256]{2,1,0:T(8,128)(2,1)S(1)}, bf16[32,96,256]{2,1,0:T(8,128)(2,1)}, u32[]{:S(2)}) copy-start(bf16[32,96,256]{2,1,0:T(8,128)(2,1)} %emb_ref.3) | copy-start | bytes 4718596
  0.7 6.5 %copy-start.13 = (f32[256]{0:T(256)S(1)}, f32[256]{0:T(256)}, u32[]{:S(2)}) copy-start(f32[256]{0:T(256)} %param.17) | copy-start | bytes 3076
  0.7 6.5 %copy-start.11 = (bf16[256,32]{0,1:T(8,128)(2,1)S(1)}, bf16[256,32]{0,1:T(8,128)(2,1)}, u32[]{:S(2)}) copy-start(bf16[256,32]{0,1:T(8,128)(2,1)} %param.21) | copy-start | bytes 49156
  0.7 6.2 %copy-start.10 = (s32[32,96]{1,0:T(8,128)S(1)}, s32[32,96]{1,0:T(8,128)}, u32[]{:S(2)}) copy-start(s32[32,96]{1,0:T(8,128)} %param.14) | copy-start | bytes 36868
  4.4 5.1 %copy-start.12 = (bf16[256,32]{0,1:T(8,128)(2,1)S(1)}, bf16[256,32]{0,1:T(8,128)(2,1)}, u32[]{:S(2)}) copy-start(bf16[256,32]{0,1:T(8,128)(2,1)} %param.20) | copy-start | bytes 49156
  8.5 2.3 %copy-start.9 = (bf16[1024,128]{1,0:T(8,128)(2,1)S(1)}, bf16[1024,128]{1,0:T(8,128)(2,1)}, u32[]{:S(2)}) copy-start(bf16[1024,128]{1,0:T(8,128)(2,1)} %param.22) | copy-start | bytes 786436
  10.8 53.3 %copy-start.4 = (bf16[128,8]{0,1:T(8,128)(2,1)S(1)}, bf16[128,8]{0,1:T(8,128)(2,1)}, u32[]{:S(2)}) copy-start(bf16[128,8]{0,1:T(8,128)(2,1)} %param.23) | copy-start | bytes 6148
  10.8 53.3 %copy-start.5 = (f32[128]{0:T(128)S(1)}, f32[128]{0:T(128)}, u32[]{:S(2)}) copy-start(f32[128]{0:T(128)} %param.19) | copy-start | bytes 1540
  90.5 0.9 copy-start.1
  91.4 0.6 copy-start.2
  92.0 0.6 copy-start.3
  92.6 79.4 %copy-start.7 = (bf16[32,96,256]{2,1,0:T(8,128)(2,1)S(1)}, bf16[32,96,256]{2,1,0:T(8,128)(2,1)}, u32[]{:S(2)}) copy-start(bf16[32,96,256]{2,1,0:T(8,128)(2,1)} %emb_ref.3) | copy-start | bytes 4718596
  172.1 3.3 %copy-start.8 = (f32[48,96,128]{2,1,0:T(8,128)S(1)}, f32[48,96,128]{2,1,0:T(8,128)}, u32[]{:S(2)}) copy-start(f32[48,96,128]{2,1,0:T(8,128)} %get-tuple-element.21) | copy-start | bytes 7077892

commit v7 on v6

--- a/solution.py
+++ b/solution.py
@@ -103,6 +103,11 @@
                     pltpu.make_async_copy(left_ref.at[h], left_out.at[here], lrecv.at[r]).start()
 
     def along(n, d):
+        if d == 2:
+            turn = 1 if n == 0 else 3
+            block = right_out.at[rows(row_of((y + 4 - turn) % 4, (zh + n) % 2, core))]
+            at = n * 4 + d
+            return remote(block, block, ysend.at[at], yrecv.at[at], (row_of((y + turn) % 4, zh, core), c))
         block = rows(row_of(y, (zh + n) % 2, core))
         src = right_ref if n == 0 else right_out.at[block]
         return remote(src, right_out.at[block], ysend.at[n * 4 + d], yrecv.at[n * 4 + d], (row_of((y + d) % 4, zh, core), c))
@@ -112,7 +117,7 @@
         src = right_ref if n == 0 and d == 0 else right_out.at[block]
         return remote(src, right_out.at[block], fsend.at[n * 4 + d], frecv.at[n * 4 + d], partner)
 
-    for d in (1, 3, 2):
+    for d in (1, 3):
         along(0, d).start()
     own = pltpu.make_async_copy(right_ref, right_out.at[here], own_sem.at[0])
     own.start()
@@ -120,7 +125,7 @@
     for d in (1, 3, 2):
         move(d).start()
     over.wait_recv()
-    for d in (1, 3, 2):
+    for d in (3, 1):
         along(1, d).start()
     forward(1, 0).start()
 
@@ -129,17 +134,28 @@
         block = left_out.at[rows(source)]
         return block, source, remote(block, block, gsend.at[d * 2 + k], lrecv.at[source], aside)
 
-    for d in (0, 1, 3, 2):
+    def pass_left(d):
         for k in range(2):
             block, source, cp = relay(d, k)
             pltpu.make_async_copy(left_ref.at[0], block, lrecv.at[source]).wait()
             cp.start()
-        if d > 0:
-            along(0, d).wait_recv()
-            forward(0, d).start()
-    for d in (1, 3, 2):
-        along(1, d).wait_recv()
-        forward(1, d).start()
+
+    def pass_right(n, d):
+        along(n, d).wait_recv()
+        if (n, d) in ((0, 1), (1, 3)):
+            along(n, 2).start()
+        forward(n, d).start()
+
+    pass_left(0)
+    pass_right(0, 1)
+    pass_left(1)
+    pass_right(0, 3)
+    pass_right(1, 3)
+    pass_left(3)
+    pass_right(1, 1)
+    pass_left(2)
+    pass_right(0, 2)
+    pass_right(1, 2)
     for ys in range(4):
         for k in range(2):
             source = row_of(ys, 1 - zl, k)
@@ -461,7 +477,7 @@
     out = pl.pallas_call(
         attn_kernel,
         out_shape=jax.ShapeDtypeStruct((2, home, 3, 2, sub, lanes), jnp.bfloat16),
-        in_specs=[vmem, hbm, hbm, hbm, vmem, vmem, vmem],
+        in_specs=[hbm, hbm, hbm, hbm, hbm, vmem, vmem],
         out_specs=hbm,
         scratch_shapes=[
             pltpu.VMEM((channels, 4 * lanes), jnp.bfloat16),

time: 177 us -> 177 us (level)
  no operation moved by 1% of the time
where the time goes in v7:
time: 177 us
  Pallas kernels  158 us (89%)
  other arithmetic  6.58 us (4%)
  local copies, waits for them, and re-layouts  6.16 us (3%)
  matrix products  5.82 us (3%)
    pallas_call x1, Pallas kernels, attention(): pl.pallas_call(attn_kernel, out_shape=jax.ShapeDtypeStruct((2, home, 3, 2...  79.3 us
    pallas_call x1, Pallas kernels, spread(): pl.pallas_call(spread_kernel, out_shape=(jax.ShapeDtypeStruct((16 * seqs,...  51.5 us
    pallas_call x1, Pallas kernels, opm(): pl.pallas_call(opm_kernel, grid=(steps,), out_shape=(jax.ShapeDtypeStruct...  26.7 us
    unnamed x29, local copies, waits for them, and re-layouts  4.42 us

profile of v7, /device:TPU:1, one launch (start us, length us, event | category | flops | bytes accessed | tf_op | source)
XLA Modules:
  0.0 177.0 jit_solution(15255054963898233909)
XLA Ops:
  0.6 0.0 copy-start
  0.6 0.0 copy-start.6
  0.7 0.0 copy-start.13
  0.7 0.0 copy-start.11
  0.7 0.0 copy-start.10
  0.7 0.8 copy-done
  1.5 0.7 convert_element_type.39
  2.2 0.1 dynamic-slice_bitcast_fusion
  2.3 0.1 dynamic-slice_bitcast_fusion.1.rrow_ref
  2.4 2.0 %convert_reduce_fusion = f32[32,96]{1,0:T(8,128)S(1)} fusion(bf16[32,96,256]{2,1,0:T(8,128)(2,1)} %emb_ref.3), kind=kLoop, calls=%fused_computation.2 | loop fusion | flops 1569792 | bytes 1585152 | tf_op jit(solution)/shard_map/reduce_sum | solution.py:15
  4.4 0.0 copy-start.12
  4.4 2.5 %fusion.2 = f32[32,96]{1,0:T(8,128)S(1)} fusion(bf16[32,96,256]{2,1,0:T(8,128)(2,1)} %emb_ref.3, f32[32,96]{1,0:T(8,128)S(1)} %broadcast_multiply_fusion), kind=kLoop, calls=%fused_computation.5 | loop fusion | flops 3142656 | bytes 1597440 | tf_op jit(solution)/shard_map/reduce_sum | solution.py:17
  6.9 0.0 copy-done.10
  6.9 0.1 reshape.54
  7.0 0.1 copy.22.rcol_ref
  7.1 0.0 copy-done.6
  7.1 0.0 copy-done.13
  7.2 0.0 copy-done.11
  7.2 1.3 fusion.8
  8.5 0.0 copy-start.9
  8.5 0.3 reshape.55
  8.8 0.7 fusion.14.right_ref
  9.5 0.0 copy-done.12
  9.5 1.3 fusion.6
  10.8 0.0 copy-done.9
  10.8 0.0 copy-start.4
  10.8 0.0 copy-start.5
  10.8 0.1 copy.29
  10.9 0.4 copy.18
  11.3 0.6 reshape.53
  11.9 0.7 fusion.13.left_ref
  12.6 51.5 %spread.1 = (bf16[512,1664]{1,0:T(8,128)(2,1)}, bf16[512,3200]{1,0:T(8,128)(2,1)}, bf16[4,4,96,256]{3,2,1,0:T(8,128)(2,1)}) custom-call(bf16[2,32,1664]{2,1,0:T(8,128)(2,1)} %fusion.13.left_ref, bf16[32,3200]{1,0:T(8,128)(2,1)} %fusion.14.right_ref, bf16[32,96,256]{2,1,0:T(8,128)(2,1)} %emb_ref.3), custom_call_target="tpu_custom_call" | custom-call | tf_op jit(solution)/shard_map/spread/pallas_call | solution.py:184
  64.1 0.0 copy-done.4
  64.2 0.0 copy-done.5
  64.2 26.7 %opm.1 = (f32[48,96,128]{2,1,0:T(8,128)}, bf16[48,768]{1,0:T(8,128)(2,1)S(1)}, bf16[4,4,96,256]{3,2,1,0:T(8,128)(2,1)S(1)}, f32[8,8,128]{2,1,0:T(8,128)S(1)}) custom-call(bf16[512,1664]{1,0:T(8,128)(2,1)} %get-tuple-element.9.left_ref.lmask_ref, bf16[512,1664]{1,0:T(8,128)(2,1)} %get-tuple-element.9.left_ref.lmask_ref, ...), custom_call_target="tpu_custom_call" | custom-call | tf_op jit(solution)/shard_map/opm/pallas_call | solution.py:619
  90.8 0.0 copy-start.1
  90.8 0.9 copy-done.1
  91.7 0.0 copy-start.2
  91.7 0.6 copy-done.2
  92.3 0.0 copy-start.3
  92.3 0.6 copy-done.3
  92.9 0.0 copy-start.7
  92.9 79.3 %attn.1 = bf16[2,32,3,2,16,128]{5,4,3,2,1,0:T(8,128)(2,1)} custom-call(bf16[48,768]{1,0:T(8,128)(2,1)} %copy-done.2, bf16[32,96,256]{2,1,0:T(8,128)(2,1)} %emb_ref.3, bf16[4,4,96,256]{3,2,1,0:T(8,128)(2,1)} %get-tuple-element.12.near_ref, bf16[4,4,96,256]{3,2,1,0:T(8,128)(2,1)} %copy-done.1, f32[8,8,128]{2,1,0:T(8,128)} %copy-done.3, f32[1,256]{1,0:T(1,128)} %bitcast.45, ...), custom_call_target="tpu_custom_call" | custom-call | tf_op jit(solution)/shard_map/attn/pallas_call | solution.py:477
  172.3 0.0 copy-start.8
  172.3 0.0 copy-done.7
  172.3 3.3 %fusion.5 = bf16[32,96,256]{2,1,0:T(8,128)(2,1)} fusion(bf16[32,96,256]{2,1,0:T(8,128)(2,1)S(1)} %copy-done.7, bf16[2,32,96,128]{3,2,1,0:T(8,128)(2,1)} %bitcast.40, bf16[2,128,256,1]{2,1,3,0:T(8,128)(2,1)S(1)} %bitcast.36), kind=kOutput, calls=%fused_computation.8 | convolution fusion | flops 405012480 | bytes 4849664 | tf_op jit(solution)/shard_map/hsqd,hdc->sqc/dot_general | solution.py:711
  175.6 0.0 copy-done.8
  175.6 1.4 copy.33
  (6 shorter events, 0.1 us)
Async XLA Ops:
  0.6 0.9 copy-start
  0.6 6.5 %copy-start.6 = (bf16[32,96,256]{2,1,0:T(8,128)(2,1)S(1)}, bf16[32,96,256]{2,1,0:T(8,128)(2,1)}, u32[]{:S(2)}) copy-start(bf16[32,96,256]{2,1,0:T(8,128)(2,1)} %emb_ref.3) | copy-start | bytes 4718596
  0.7 6.5 %copy-start.13 = (f32[256]{0:T(256)S(1)}, f32[256]{0:T(256)}, u32[]{:S(2)}) copy-start(f32[256]{0:T(256)} %param.17) | copy-start | bytes 3076
  0.7 6.5 %copy-start.11 = (bf16[256,32]{0,1:T(8,128)(2,1)S(1)}, bf16[256,32]{0,1:T(8,128)(2,1)}, u32[]{:S(2)}) copy-start(bf16[256,32]{0,1:T(8,128)(2,1)} %param.21) | copy-start | bytes 49156
  0.7 6.2 %copy-start.10 = (s32[32,96]{1,0:T(8,128)S(1)}, s32[32,96]{1,0:T(8,128)}, u32[]{:S(2)}) copy-start(s32[32,96]{1,0:T(8,128)} %param.14) | copy-start | bytes 36868
  4.4 5.1 %copy-start.12 = (bf16[256,32]{0,1:T(8,128)(2,1)S(1)}, bf16[256,32]{0,1:T(8,128)(2,1)}, u32[]{:S(2)}) copy-start(bf16[256,32]{0,1:T(8,128)(2,1)} %param.20) | copy-start | bytes 49156
  8.5 2.3 %copy-start.9 = (bf16[1024,128]{1,0:T(8,128)(2,1)S(1)}, bf16[1024,128]{1,0:T(8,128)(2,1)}, u32[]{:S(2)}) copy-start(bf16[1024,128]{1,0:T(8,128)(2,1)} %param.22) | copy-start | bytes 786436
  10.8 53.4 %copy-start.4 = (bf16[128,8]{0,1:T(8,128)(2,1)S(1)}, bf16[128,8]{0,1:T(8,128)(2,1)}, u32[]{:S(2)}) copy-start(bf16[128,8]{0,1:T(8,128)(2,1)} %param.23) | copy-start | bytes 6148
  10.8 53.4 %copy-start.5 = (f32[128]{0:T(128)S(1)}, f32[128]{0:T(128)}, u32[]{:S(2)}) copy-start(f32[128]{0:T(128)} %param.19) | copy-start | bytes 1540
  90.8 0.9 copy-start.1
  91.7 0.6 copy-start.2
  92.3 0.6 copy-start.3
  92.9 79.3 %copy-start.7 = (bf16[32,96,256]{2,1,0:T(8,128)(2,1)S(1)}, bf16[32,96,256]{2,1,0:T(8,128)(2,1)}, u32[]{:S(2)}) copy-start(bf16[32,96,256]{2,1,0:T(8,128)(2,1)} %emb_ref.3) | copy-start | bytes 4718596
  172.3 3.3 %copy-start.8 = (f32[48,96,128]{2,1,0:T(8,128)S(1)}, f32[48,96,128]{2,1,0:T(8,128)}, u32[]{:S(2)}) copy-start(f32[48,96,128]{2,1,0:T(8,128)} %get-tuple-element.21) | copy-start | bytes 7077892
